TPU v7x, 256 devices: a whole 4x4x8 slice. The times are simulated.
256 devices in a mesh: wide: 128 (over z, y, x_hi, core), narrow: 2 (over x_lo).
Axes of the slice: x: 4 (x_hi: 2, x_lo: 2; x = x_hi * 2 + x_lo), y: 4, z: 8, core: 2. Of those that a mesh axis runs over, the one named last changes fastest.
Arguments:
- key_grads: bfloat16 [128, 2, 2, 2048, 512], P('wide', 'narrow'), may hold values from -1600 to 1600
- router_grads: bfloat16 [128, 2, 2, 64, 2048], P('wide', 'narrow'), may hold values from -1600 to 1600
- gain_grads: bfloat16 [128, 2, 2, 2048], P('wide', 'narrow'), may hold values from -1600 to 1600
- key_master: float32 [2048, 512], P('narrow'), may hold values from -3 to 3
- key_first: float32 [2048, 512], P('narrow'), may hold values from -3 to 3
- key_second: float32 [2048, 512], P('narrow'), may hold values from 0.01 to 1
- router_master: float32 [64, 2048], P(None, 'narrow'), may hold values from -3 to 3
- router_first: float32 [64, 2048], P(None, 'narrow'), may hold values from -3 to 3
- router_second: float32 [64, 2048], P(None, 'narrow'), may hold values from 0.01 to 1
- gain_master: float32 [2048], P('narrow'), may hold values from 0.5 to 1.5
- gain_first: float32 [2048], P('narrow'), may hold values from -3 to 3
- gain_second: float32 [2048], P('narrow'), may hold values from 0.01 to 1
Outputs:
- key_master_new: float32 [2048, 512], P('narrow')
- key_first_new: float32 [2048, 512], P('narrow')
- key_second_new: float32 [2048, 512], P('narrow')
- router_master_new: float32 [64, 2048], P(None, 'narrow')
- router_first_new: float32 [64, 2048], P(None, 'narrow')
- router_second_new: float32 [64, 2048], P(None, 'narrow')
- gain_master_new: float32 [2048], P('narrow')
- gain_first_new: float32 [2048], P('narrow')
- gain_second_new: float32 [2048], P('narrow')
- key_weight: bfloat16 [2048, 512], replicated
- router_weight: bfloat16 [64, 2048], replicated
- gain_weight: bfloat16 [2048], replicated
All inputs are finite; a program needn't handle non-finite values.
Results may differ from a plain program's by a relative error of at most 0.002.
Values may be sent and summed in bfloat16 or wider, within the bound.
No kernel may reach another device: no remote copies, remote signals or barrier semaphores. Data moves between devices by JAX's collectives and lax.ppermute only.
A program may use at most 64 MiB of HBM per device.

v0:
```python
import math

import jax
import jax.numpy as jnp
from jax import lax
from jax.sharding import PartitionSpec as P

D = 2048
KEY_WIDTH = 512
EXPERTS = 64


beta_one = 0.9
beta_two = 0.95
step_rate = 0.01
epsilon = 1e-08
bias_one = 1.0 - 0.9**10
bias_two = 1.0 - 0.95**10


def micro_total(grad_stack):
    summed = jnp.sum(grad_stack[0, 0].astype(jnp.float32), axis=0)
    rounded = lax.optimization_barrier(summed.astype(jnp.bfloat16))
    return rounded.astype(jnp.float32)


def adamw(master, first_moment, second, gradient, factor, decay_rate):
    scaled = factor * gradient
    first_new = beta_one * first_moment + (1.0 - beta_one) * scaled
    second_new = beta_two * second + (1.0 - beta_two) * scaled * scaled
    update = (
        first_new / bias_one / (jnp.sqrt(second_new / bias_two) + epsilon) + decay_rate * master
    )
    master_new = master - step_rate * update
    return (master_new, first_new, second_new)


def on_device(
    key_grads,
    router_grads,
    gain_grads,
    key_master,
    key_first,
    key_second,
    router_master,
    router_first,
    router_second,
    gain_master,
    gain_first,
    gain_second,
):
    key_local = micro_total(key_grads)
    router_local = micro_total(router_grads)
    gain_local = micro_total(gain_grads)
    key_part, router_part, gain_part = (
        lax.psum_scatter(
            key_local.astype(jnp.bfloat16), "narrow", scatter_dimension=0, tiled=True
        ).astype(jnp.float32),
        lax.psum_scatter(
            router_local.astype(jnp.bfloat16), "narrow", scatter_dimension=1, tiled=True
        ).astype(jnp.float32),
        lax.psum_scatter(
            gain_local.astype(jnp.bfloat16), "narrow", scatter_dimension=0, tiled=True
        ).astype(jnp.float32),
    )
    key_sum, router_sum, gain_sum = lax.psum((key_part, router_part, gain_part), "wide")
    squares = (
        jnp.sum(key_sum * key_sum) + jnp.sum(router_sum * router_sum) + jnp.sum(gain_sum * gain_sum)
    )
    squares = lax.psum(squares, "narrow")
    clip_limit = 0.5 * math.sqrt(D * KEY_WIDTH + EXPERTS * D + D)
    factor = clip_limit / jnp.maximum(jnp.sqrt(squares), clip_limit)
    key_new, key_first_new, key_second_new = adamw(
        key_master, key_first, key_second, key_sum, factor, 0.1
    )
    router_new, router_first_new, router_second_new = adamw(
        router_master, router_first, router_second, router_sum, factor, 0.1
    )
    gain_new, gain_first_new, gain_second_new = adamw(
        gain_master, gain_first, gain_second, gain_sum, factor, 0.0
    )
    key_weight, router_weight, gain_weight = (
        lax.all_gather(key_new.astype(jnp.bfloat16), "narrow", axis=0, tiled=True),
        lax.all_gather(router_new.astype(jnp.bfloat16), "narrow", axis=1, tiled=True),
        lax.all_gather(gain_new.astype(jnp.bfloat16), "narrow", axis=0, tiled=True),
    )
    return (
        key_new,
        key_first_new,
        key_second_new,
        router_new,
        router_first_new,
        router_second_new,
        gain_new,
        gain_first_new,
        gain_second_new,
        key_weight,
        router_weight,
        gain_weight,
    )


def solution(mesh):
    in_specs = (
        P("wide", "narrow", None, None, None),
        P("wide", "narrow", None, None, None),
        P("wide", "narrow", None, None),
        P("narrow", None),
        P("narrow", None),
        P("narrow", None),
        P(None, "narrow"),
        P(None, "narrow"),
        P(None, "narrow"),
        P("narrow"),
        P("narrow"),
        P("narrow"),
    )
    out_specs = (
        P("narrow", None),
        P("narrow", None),
        P("narrow", None),
        P(None, "narrow"),
        P(None, "narrow"),
        P(None, "narrow"),
        P("narrow"),
        P("narrow"),
        P("narrow"),
        P(),
        P(),
        P(),
    )
    return jax.shard_map(
        on_device, mesh=mesh, in_specs=in_specs, out_specs=out_specs, check_vma=False
    )
```

profile of v0, /device:TPU:1, one launch (start us, length us, event | category | flops | bytes accessed | tf_op | source)
XLA Modules:
  0.0 809.0 jit_solution(331207828802848789)
XLA Ops:
  7.2 0.0 reduce-scatter.5.cloned.1.call-start
  7.2 1.9 reduce_sum.65
  9.1 0.0 reduce-scatter.5.cloned.1.call-update
  9.2 0.0 reduce-scatter.3.cloned.1.call-start
  9.2 4.9 reduce_sum.63
  14.1 0.0 reduce-scatter.3.cloned.1.call-update
  14.1 0.0 all-gather.2.cloned.1.call-start
  14.2 0.6 copy-done.3
  14.8 0.0 copy-done.7
  14.8 0.6 dynamic-slice
  16.1 4.4 all-reduce
  20.4 11.2 %reduce-scatter.5.cloned.1.call-done = bf16[64,1024]{1,0:T(8,128)(2,1)} async-done(((bf16[64,2048]{1,0:T(8,128)(2,1)}), bf16[64,1024]{1,0:T(8,128)(2,1)}) %reduce-scatter.5.cloned.1.call-update) | async-done | bytes 131088 | tf_op jit(solution)/shard_map/reduce_scatter | solution.py:59
  31.6 41.1 %reduce-scatter.3.cloned.1.call-done = bf16[1024,512]{1,0:T(8,128)(2,1)} async-done(((bf16[2048,512]{1,0:T(8,128)(2,1)}), bf16[1024,512]{1,0:T(8,128)(2,1)}) %reduce-scatter.3.cloned.1.call-update) | async-done | bytes 1048592 | tf_op jit(solution)/shard_map/reduce_scatter | solution.py:56
  72.8 668.3 %all-reduce.3 = (f32[1024,512]{1,0:T(8,128)S(1)}, f32[64,1024]{1,0:T(8,128)S(1)}, f32[1024]{0:T(1024)S(1)}) all-reduce(bf16[1024,512]{1,0:T(8,128)(2,1)} %reduce-scatter.3.cloned.1.call-done, bf16[64,1024]{1,0:T(8,128)(2,1)} %reduce-scatter.5.cloned.1.call-done, ...), channel_id=1, replica_groups=mesh['wide'=128,'narrow'=2] {'wide'}, use_global_device_ids=true, to_apply=%region_2.0 | all-reduce | flops 590848 | bytes 3547136 | tf_op jit(solution)/shard_map/psum | solution.py:66
  741.1 1.1 multiply_reduce_fusion
  742.2 0.7 multiply_reduce_fusion.1
  742.9 0.6 multiply_reduce_fusion.2
  745.4 4.3 psum.31
  750.4 0.0 copy-start
  750.4 0.0 copy-start.1
  750.5 0.0 copy-start.2
  750.5 7.2 fusion.7
  757.6 0.0 all-gather.2.cloned.1.call-update
  757.7 1.0 fusion.5
  758.7 4.5 all_gather.10
  763.2 0.0 copy-done.5
  763.2 0.6 fusion.3
  763.8 3.2 all_gather.11
  767.0 31.2 %all-gather.2.cloned.1.call-done = bf16[2048,512]{1,0:T(8,128)(2,1)} async-done(((bf16[1024,512]{1,0:T(8,128)(2,1)}), bf16[2048,512]{1,0:T(8,128)(2,1)}) %all-gather.2.cloned.1.call-update) | async-done | bytes 2097168 | tf_op jit(solution)/shard_map/all_gather | solution.py:83
  798.2 3.0 copy.32
  801.2 0.7 copy.33
  801.9 0.6 copy.34
  (12 shorter events, 0.1 us)
Async XLA Ops:
  7.2 24.5 %reduce-scatter.5.cloned.1.call-start = ((), (), s32[]{:S(2)}) async-start(), calls=%async_computation.3 | async-start | bytes 393216 | tf_op jit(solution)/shard_map/reduce_scatter | solution.py:59
  9.2 63.6 %reduce-scatter.3.cloned.1.call-start = ((), (), s32[]{:S(2)}) async-start(), calls=%async_computation.2 | async-start | bytes 3145728 | tf_op jit(solution)/shard_map/reduce_scatter | solution.py:56
  14.1 0.7 copy-start.3
  14.1 0.7 copy-start.7
  14.1 784.0 %all-gather.2.cloned.1.call-start = ((), (), s32[]{:S(2)}) async-start(), calls=%async_computation.4 | async-start | bytes 3145728 | tf_op jit(solution)/shard_map/all_gather | solution.py:83
  750.4 7.2 copy-start
  750.4 7.2 copy-start.1
  750.5 7.2 copy-start.2
  757.6 5.6 copy-start.4
  757.6 5.6 copy-start.5
  757.6 5.6 copy-start.6
Sparse Core Ops, SparseCore 0:
  11.1 20.5 reduce-scatter.4
  34.9 37.8 reduce-scatter.2
  757.8 40.3 all-gather.1
where the time goes:
time: 810 us; the launch traced here: 809 us
  blocking collectives  685 us (85%)
  waiting for transfers between devices  83.6 us (10%)
  other arithmetic  18 us (2%)
  between operations  17.2 us (2%)
    psum x1, blocking collectives, on_device(): lax.psum((key_part, router_part, gain_part), 'wide')  668 us
    reduce_scatter x1, waiting for transfers between devices, on_device(): lax.psum_scatter(key_local.astype(jnp.bfloat16), 'narrow', scatter_dimens...  41.1 us
    all_gather x1, waiting for transfers between devices, on_device(): lax.all_gather(key_new.astype(jnp.bfloat16), 'narrow', axis=0, tiled=True)  31.2 us
  transfers between devices with their start and end apart: 3, of which 3 were waited for; matrix products, arithmetic and copies ran while one was open for 1% of the time, Pallas kernels for 0%

commit v1 on v0

v1 whole, which is shorter than its diff:
```python
import math

import jax
import jax.numpy as jnp
import numpy as np
from jax import lax
from jax.sharding import Mesh
from jax.sharding import PartitionSpec as P

D = 2048
KEY_WIDTH = 512
EXPERTS = 64
LANES = 128

beta_one = 0.9
beta_two = 0.95
step_rate = 0.01
epsilon = 1e-08
bias_one = 1.0 - 0.9**10
bias_two = 1.0 - 0.95**10

SWAP = [(0, 1), (1, 0)]
WIDE = ("z", "y", "xh", "c")


def micro_total(grad_stack):
    summed = jnp.sum(grad_stack.astype(jnp.float32), axis=0)
    return summed.astype(jnp.bfloat16)


def adamw(master, first_moment, second, gradient, factor, decay_rate):
    scaled = factor * gradient
    first_new = beta_one * first_moment + (1.0 - beta_one) * scaled
    second_new = beta_two * second + (1.0 - beta_two) * scaled * scaled
    update = (
        first_new / bias_one / (jnp.sqrt(second_new / bias_two) + epsilon) + decay_rate * master
    )
    master_new = master - step_rate * update
    return (master_new, first_new, second_new)


def pack(key, router, gain):
    key = key.reshape(2, 128, 8, KEY_WIDTH)
    router = router.reshape(16, 4, 2, 8, LANES).transpose(2, 0, 3, 1, 4).reshape(2, 128, 4, LANES)
    gain = jnp.pad(gain.reshape(2, 8, 1, LANES), ((0, 0), (0, 120), (0, 3), (0, 0)))
    return jnp.concatenate([key, jnp.concatenate([router, gain], axis=2)], axis=3)


def unpack(blocks):
    key = blocks[:, :, :KEY_WIDTH].reshape(1024, KEY_WIDTH)
    router = blocks[:, :4, KEY_WIDTH:].reshape(16, 8, 4, LANES)
    router = router.transpose(0, 2, 1, 3).reshape(EXPERTS, 1024)
    gain = blocks[:8, 4, KEY_WIDTH:].reshape(1024)
    return key, router, gain


def on_device(
    key_grads,
    router_grads,
    gain_grads,
    key_master,
    key_first,
    key_second,
    router_master,
    router_first,
    router_second,
    gain_master,
    gain_first,
    gain_second,
):
    core = lax.axis_index("c")
    half = lax.axis_index("xl")
    local = pack(
        micro_total(key_grads[0, 0]), micro_total(router_grads[0, 0]), micro_total(gain_grads[0, 0])
    )
    local = local.reshape(2, 2, 64, 8, 640)
    sent = lax.dynamic_index_in_dim(local, 1 - core, 1, keepdims=False)
    kept = lax.dynamic_index_in_dim(local, core, 1, keepdims=False)
    got = lax.ppermute(sent, "c", SWAP)
    pair = (kept.astype(jnp.float32) + got.astype(jnp.float32)).astype(jnp.bfloat16)
    spread = lax.all_to_all(
        pair.reshape(128, 8, 640), ("xl", "z", "y", "xh"), 0, 0, tiled=True
    )
    own = jnp.sum(spread.astype(jnp.float32), axis=0)
    largest = jnp.maximum(jnp.max(jnp.abs(own)), 1e-30)
    exponent = jnp.floor(jnp.log2(largest)) - 13.0
    scaled_own = own * jnp.exp2(-exponent)
    at = (lax.broadcasted_iota(jnp.int32, own.shape, 0) == 5) & (
        lax.broadcasted_iota(jnp.int32, own.shape, 1) == KEY_WIDTH
    )
    code = jnp.where(at, exponent, scaled_own).astype(jnp.float16)
    parts = lax.all_to_all(
        jnp.broadcast_to(code[None], (64, 8, 640)), ("z", "y", "xh"), 0, 0, tiled=True
    )
    other = lax.ppermute(parts, "c", SWAP)
    blocks = jnp.where(
        core == 0, jnp.concatenate([parts, other]), jnp.concatenate([other, parts])
    )
    blocks = blocks.astype(jnp.float32)
    blocks = blocks * jnp.exp2(blocks[:, 5:6, KEY_WIDTH : KEY_WIDTH + 1])
    key_sum, router_sum, gain_sum = unpack(blocks)
    squares = (
        jnp.sum(key_sum * key_sum) + jnp.sum(router_sum * router_sum) + jnp.sum(gain_sum * gain_sum)
    )
    squares = squares + lax.ppermute(squares, "xl", SWAP)
    clip_limit = 0.5 * math.sqrt(D * KEY_WIDTH + EXPERTS * D + D)
    factor = clip_limit / jnp.maximum(jnp.sqrt(squares), clip_limit)
    key_new, key_first_new, key_second_new = adamw(
        key_master, key_first, key_second, key_sum, factor, 0.1
    )
    router_new, router_first_new, router_second_new = adamw(
        router_master, router_first, router_second, router_sum, factor, 0.1
    )
    gain_new, gain_first_new, gain_second_new = adamw(
        gain_master, gain_first, gain_second, gain_sum, factor, 0.0
    )
    key_low = key_new.astype(jnp.bfloat16)
    router_low = router_new.astype(jnp.bfloat16)
    gain_low = gain_new.astype(jnp.bfloat16)

    def exchange(low):
        mine = lax.dynamic_index_in_dim(low, core, 0, keepdims=False)
        far = lax.ppermute(mine, "xl", SWAP)
        near = lax.ppermute(far, "c", SWAP)
        far = jnp.where(core == 0, jnp.stack([far, near]), jnp.stack([near, far]))
        return jnp.where(half == 0, jnp.stack([low, far]), jnp.stack([far, low]))

    key_weight = exchange(key_low.reshape(2, 512, 512)).reshape(D, KEY_WIDTH)
    router_weight = exchange(router_low.reshape(2, 32, 1024)).reshape(2, EXPERTS, 1024)
    router_weight = jnp.concatenate([router_weight[0], router_weight[1]], axis=1)
    gain_far = lax.ppermute(gain_low, "xl", SWAP)
    gain_weight = jnp.where(
        half == 0, jnp.concatenate([gain_low, gain_far]), jnp.concatenate([gain_far, gain_low])
    )
    return (
        key_new,
        key_first_new,
        key_second_new,
        router_new,
        router_first_new,
        router_second_new,
        gain_new,
        gain_first_new,
        gain_second_new,
        key_weight,
        router_weight,
        gain_weight,
    )


def solution(mesh):
    fine = Mesh(np.asarray(mesh.devices).reshape(8, 4, 2, 2, 2), ("z", "y", "xh", "c", "xl"))
    in_specs = (
        P(WIDE, "xl", None, None, None),
        P(WIDE, "xl", None, None, None),
        P(WIDE, "xl", None, None),
        P("xl", None),
        P("xl", None),
        P("xl", None),
        P(None, "xl"),
        P(None, "xl"),
        P(None, "xl"),
        P("xl"),
        P("xl"),
        P("xl"),
    )
    out_specs = (
        P("xl", None),
        P("xl", None),
        P("xl", None),
        P(None, "xl"),
        P(None, "xl"),
        P(None, "xl"),
        P("xl"),
        P("xl"),
        P("xl"),
        P(),
        P(),
        P(),
    )
    return jax.shard_map(
        on_device, mesh=fine, in_specs=in_specs, out_specs=out_specs, check_vma=False
    )
```

time: 810 us -> 144 us (0.18)
  blocking collectives: 685 us -> 25.4 us
  waiting for transfers between devices: 83.6 us -> 51.2 us
  starting transfers between devices: 0.12 us -> 28 us
  between operations: 17.2 us -> 4.3 us
  other arithmetic: 18 us -> 29.2 us
    psum x2 -> x0, blocking collectives: 673 us -> none  [the longest x1 668 us: on_device(): lax.psum((key_part, router_part, gain_part), 'wide')]
    reduce_scatter x2 -> x0, waiting for transfers between devices: 52.3 us -> none  [the longest x1 41.1 us: on_device(): lax.psum_scatter(key_local.astype(jnp.bfloat16), 'narrow', scatter_dimens...]
    all_to_all x0 -> x1, waiting for transfers between devices: none -> 34.4 us  [on_device(): lax.all_to_all(pair.reshape(128, 8, 640), ('xl', 'z', 'y', 'xh'), 0, 0, t...]
    all_gather x1 -> x0, waiting for transfers between devices: 31.2 us -> none  [on_device(): lax.all_gather(key_new.astype(jnp.bfloat16), 'narrow', axis=0, tiled=True)]
    all_to_all x0 -> x1, blocking collectives: none -> 25.4 us  [on_device(): lax.all_to_all(jnp.broadcast_to(code[None], (64, 8, 640)), ('z', 'y', 'xh...]
    ppermute x0 -> x8, waiting for transfers between devices: none -> 16.8 us  [the longest x2 9.84 us: exchange(): far = lax.ppermute(mine, 'xl', SWAP)]
    ppermute x0 -> x8, starting transfers between devices: none -> 14.2 us  [the longest x1 4.42 us: on_device(): other = lax.ppermute(parts, 'c', SWAP)]
    all_to_all x0 -> x1, starting transfers between devices: none -> 13.8 us  [on_device(): lax.all_to_all(pair.reshape(128, 8, 640), ('xl', 'z', 'y', 'xh'), 0, 0, t...]
  transfers between devices with their start and end apart: 3 -> 9, of which waited for: 3 -> 7; matrix products, arithmetic and copies ran while one was open for 1% -> 2% of each run, Pallas kernels for 0% -> 0%
where the time goes in v1:
time: 144 us; the launch traced here: 143 us
  waiting for transfers between devices  51.2 us (36%)
  other arithmetic  29.2 us (20%)
  starting transfers between devices  28 us (19%)
  blocking collectives  25.4 us (18%)
  local copies, waits for them, and re-layouts  5 us (3%)
  between operations  4.3 us (3%)
    all_to_all x1, waiting for transfers between devices, on_device(): lax.all_to_all(pair.reshape(128, 8, 640), ('xl', 'z', 'y', 'xh'), 0, 0, t...  34.4 us
    all_to_all x1, blocking collectives, on_device(): lax.all_to_all(jnp.broadcast_to(code[None], (64, 8, 640)), ('z', 'y', 'xh...  25.4 us
    all_to_all x1, starting transfers between devices, on_device(): lax.all_to_all(pair.reshape(128, 8, 640), ('xl', 'z', 'y', 'xh'), 0, 0, t...  13.8 us
    ppermute x2, waiting for transfers between devices, exchange(): far = lax.ppermute(mine, 'xl', SWAP)  9.84 us
    reduce_sum x3, other arithmetic, micro_total(): summed = jnp.sum(grad_stack.astype(jnp.float32), axis=0)  6.78 us
    convert_element_type x1, other arithmetic, on_device(): key_low = key_new.astype(jnp.bfloat16)  6.7 us
    ppermute x1, starting transfers between devices, on_device(): other = lax.ppermute(parts, 'c', SWAP)  4.42 us
    ppermute x1, starting transfers between devices, on_device(): got = lax.ppermute(sent, 'c', SWAP)  3.24 us
  transfers between devices with their start and end apart: 9, of which 7 were waited for; matrix products, arithmetic and copies ran while one was open for 2% of the time, Pallas kernels for 0%

profile of v1, /device:TPU:1, one launch (start us, length us, event | category | flops | bytes accessed | tf_op | source)
XLA Modules:
  0.0 143.0 jit_solution(6735030354644546178)
XLA Ops:
  0.6 0.7 reduce_sum.74
  1.5 1.1 reduce_sum.73
  2.9 4.9 %reduce_sum.72 = bf16[2048,512]{1,0:T(8,128)(2,1)} reduce(bf16[1,1,2,2048,512]{4,3,2,1,0:T(8,128)(2,1)} %param.12, bf16[]{:T(256)} %constant.29.clone.1), dimensions={0,1,2}, to_apply=%region_0.0 | reduce | flops 1048576 | bytes 6291458 | tf_op jit(solution)/shard_map/reduce_sum | solution.py:27
  7.8 2.2 %maximum_maximum_fusion = bf16[2,2,64,8,640]{4,3,2,1,0:T(8,128)(2,1)S(1)} fusion(bf16[2,2,64,4,128]{4,3,2,1,0:T(4,128)(2,1)S(1)} %bitcast.63, bf16[2,2,64,4,128]{4,3,2,1,0:T(4,128)(2,1)S(1)} %copy.49, bf16[2,2,64,8,512]{4,3,2,1,0:T(8,128)(2,1)} %bitcast.57), kind=kLoop, calls=%fused_computation.1 | loop fusion | flops 7864320 | bytes 5242880 | tf_op jit(solution)/shard_map/concatenate | solution.py:46
  10.1 1.2 dynamic-slice_bitcast_fusion
  11.2 3.2 %collective-permute-start = (bf16[2,64,8,640]{3,2,1,0:T(8,128)(2,1)}, bf16[2,64,8,640]{3,2,1,0:T(8,128)(2,1)}, u32[]{:S(2)}, u32[]{:S(2)}) collective-permute-start(bf16[2,64,8,640]{3,2,1,0:T(8,128)(2,1)} %dynamic-slice_bitcast_fusion), channel_id=1, source_target_pairs={{0,2},{2,0},{1,3},{3,1},{4,6},{6,4},{5,7},{7,5},{8,10},{10,8},{9,1... | collective-permute-start | bytes 3932168 | tf_op jit(solution)/shard_map/ppermute | solution.py:79
  14.5 3.0 %collective-permute-done = bf16[2,64,8,640]{3,2,1,0:T(8,128)(2,1)} collective-permute-done((bf16[2,64,8,640]{3,2,1,0:T(8,128)(2,1)}, bf16[2,64,8,640]{3,2,1,0:T(8,128)(2,1)}, u32[]{:S(2)}, u32[]{:S(2)}) %collective-permute-start) | collective-permute-done | bytes 1310752 | tf_op jit(solution)/shard_map/ppermute | solution.py:79
  17.5 2.7 %fusion = bf16[2,64,8,640]{3,2,1,0:T(8,128)(2,1)} fusion(bf16[2,64,8,640]{3,2,1,0:T(8,128)(2,1)} %collective-permute-done, bf16[2,2,64,8,640]{4,3,2,1,0:T(8,128)(2,1)S(1)} %maximum_maximum_fusion, s32[]{:T(128)S(6)} %select_n.86), kind=kLoop, calls=%fused_computation.3 | loop fusion | flops 2621440 | bytes 3932164 | tf_op jit(solution)/shard_map/convert_element_type | solution.py:80
  20.2 13.8 %all-to-all-start = ((bf16[128,8,640]{2,1,0:T(8,128)(2,1)}), bf16[128,8,640]{2,1,0:T(8,128)(2,1)S(1)}, u32[]{:S(2)}, u32[]{:S(2)}) async-start(bf16[128,8,640]{2,1,0:T(8,128)(2,1)} %bitcast.60), calls=%async_computation | async-start | bytes 2621440 | tf_op jit(solution)/shard_map/all_to_all | solution.py:81
  34.0 34.4 %all-to-all-done = bf16[128,8,640]{2,1,0:T(8,128)(2,1)S(1)} async-done(((bf16[128,8,640]{2,1,0:T(8,128)(2,1)}), bf16[128,8,640]{2,1,0:T(8,128)(2,1)S(1)}, u32[]{:S(2)}, u32[]{:S(2)}) %all-to-all-start) | async-done | bytes 1310752 | tf_op jit(solution)/shard_map/all_to_all | solution.py:81
  70.1 25.4 %all_to_all.10 = f16[64,8,640]{2,1,0:T(8,128)(2,1)S(1)} all-to-all(f16[64,8,640]{2,1,0:T(8,128)(2,1)S(1)} %broadcast_in_dim.11), channel_id=1, replica_groups=mesh['z'=8,'y'=4,'xh'=2,'c'=2,'xl'=2] {'z','y','xh'}, dimensions={0} | all-to-all | bytes 1310720 | tf_op jit(solution)/shard_map/all_to_all | solution.py:92
  95.7 4.4 %collective-permute-start.1 = (f16[64,8,640]{2,0,1:T(8,128)(2,1)S(1)}, f16[64,8,640]{2,0,1:T(8,128)(2,1)S(1)}, u32[]{:S(2)}, u32[]{:S(2)}) collective-permute-start(f16[64,8,640]{2,0,1:T(8,128)(2,1)S(1)} %copy.51), channel_id=1, source_target_pairs={{0,2},{2,0},{1,3},{3,1},{4,6},{6,4},{5,7},{7,5},{8,10},{10,8},{9,1... | collective-permute-start | bytes 1966088 | tf_op jit(solution)/shard_map/ppermute | solution.py:95
  100.1 1.7 %collective-permute-done.1 = f16[64,8,640]{2,0,1:T(8,128)(2,1)S(1)} collective-permute-done((f16[64,8,640]{2,0,1:T(8,128)(2,1)S(1)}, f16[64,8,640]{2,0,1:T(8,128)(2,1)S(1)}, u32[]{:S(2)}, u32[]{:S(2)}) %collective-permute-start.1) | collective-permute-done | bytes 655392 | tf_op jit(solution)/shard_map/ppermute | solution.py:95
  102.8 1.8 %broadcast_multiply_fusion = f32[128,8,640]{2,0,1:T(8,128)S(1)} fusion(f32[128]{0:T(128)S(1)} %fusion.7, f16[64,8,640]{2,0,1:T(8,128)(2,1)S(1)} %copy.51, f16[64,8,640]{2,0,1:T(8,128)(2,1)} %copy-done.2, pred[]{:T(512)S(6)} %eq.24), kind=kLoop, calls=%fused_computation.14 | loop fusion | flops 3276800 | bytes 3932673 | tf_op jit(solution)/shard_map/mul | solution.py:100
  105.2 0.7 multiply_reduce_fusion.1
  105.9 1.1 multiply_reduce_fusion
  109.0 1.7 %collective-permute-start.2 = (f32[]{:T(128)}, f32[]{:T(128)}, u32[]{:S(2)}, u32[]{:S(2)}) collective-permute-start(f32[]{:T(128)} %add.76), channel_id=1, source_target_pairs={{0,1},{1,0},{2,3},{3,2},{4,5},{5,4},{6,7},{7,6},{8,9},{9,8},{10,11... | collective-permute-start | bytes 20 | tf_op jit(solution)/shard_map/ppermute | solution.py:105
  110.6 1.1 collective-permute-done.2
  112.9 1.3 copy-done.3
  114.1 0.6 copy-done.4
  114.8 6.7 %fusion.16 = (bf16[1024,512]{1,0:T(8,128)(2,1)S(1)}, f32[1024,512]{1,0:T(8,128)}, f32[1024,512]{1,0:T(8,128)}, f32[1024,512]{1,0:T(8,128)}) fusion(f32[1024,512]{1,0:T(8,128)S(1)} %copy-done.3, f32[128,8,512]{2,0,1:T(8,128)S(1)} %slice_multiply_fusion, f32[1024,512]{1,0:T(8,128)S(1)} %copy-done.4, f32[1024,512]{1,0:T(8,128)} %param.17), kind=kLoop, calls=%fused_computation.46 | loop fusion | flops 8388608 | bytes 15728640 | tf_op jit(solution)/shard_map/convert_element_type | solution.py:117
  121.5 0.8 dynamic-slice_bitcast_fusion.1
  122.3 0.7 collective-permute-start.3
  123.0 1.0 fusion.13
  124.0 0.8 collective-permute-start.5
  124.8 0.6 fusion.10
  125.5 0.7 collective-permute-start.7
  126.1 9.8 %collective-permute-done.5 = bf16[32,1024]{1,0:T(8,128)(2,1)S(1)} collective-permute-done((bf16[32,1024]{1,0:T(8,128)(2,1)S(1)}, bf16[32,1024]{1,0:T(8,128)(2,1)S(1)}, u32[]{:S(2)}, u32[]{:S(2)}) %collective-permute-start.5) | collective-permute-done | bytes 65568 | tf_op jit(solution)/shard_map/ppermute | solution.py:123
  136.0 2.3 %collective-permute-start.6 = (bf16[32,1024]{1,0:T(8,128)(2,1)S(1)}, bf16[32,1024]{1,0:T(8,128)(2,1)S(1)}, u32[]{:S(2)}, u32[]{:S(2)}) collective-permute-start(bf16[32,1024]{1,0:T(8,128)(2,1)S(1)} %collective-permute-done.5), channel_id=1, source_target_pairs={{0,2},{2,0},{1,3},{3,1},{4,6},{6,4},{5,7},{7,5},{8,10},{10,8},{9,1... | collective-permute-start | bytes 196616 | tf_op jit(solution)/shard_map/ppermute | solution.py:124
  139.7 0.7 pad_maximum_fusion
  140.4 0.8 collective-permute-done.4
  141.4 1.6 %maximum_select_fusion = bf16[2,2,512,512]{3,2,1,0:T(8,128)(2,1)} fusion(bf16[1,2,512,512]{3,2,1,0:T(8,128)(2,1)S(1)} %maximum_select_fusion.2, bf16[1,2,512,512]{3,2,1,0:T(8,128)(2,1)S(1)} %bitcast.59, pred[]{:T(512)S(6)} %eq.29), kind=kLoop, calls=%fused_computation.6 | loop fusion | flops 3145728 | bytes 4194305 | tf_op jit(solution)/shard_map/jit(_where)/select_n | solution.py:126
  (48 shorter events, 5.0 us)
Async XLA Ops:
  11.2 6.2 %collective-permute-start = (bf16[2,64,8,640]{3,2,1,0:T(8,128)(2,1)}, bf16[2,64,8,640]{3,2,1,0:T(8,128)(2,1)}, u32[]{:S(2)}, u32[]{:S(2)}) collective-permute-start(bf16[2,64,8,640]{3,2,1,0:T(8,128)(2,1)} %dynamic-slice_bitcast_fusion), channel_id=1, source_target_pairs={{0,2},{2,0},{1,3},{3,1},{4,6},{6,4},{5,7},{7,5},{8,10},{10,8},{9,1... | collective-permute-start | bytes 3932168 | tf_op jit(solution)/shard_map/ppermute | solution.py:79
  20.2 48.2 %all-to-all-start = ((bf16[128,8,640]{2,1,0:T(8,128)(2,1)}), bf16[128,8,640]{2,1,0:T(8,128)(2,1)S(1)}, u32[]{:S(2)}, u32[]{:S(2)}) async-start(bf16[128,8,640]{2,1,0:T(8,128)(2,1)} %bitcast.60), calls=%async_computation | async-start | bytes 2621440 | tf_op jit(solution)/shard_map/all_to_all | solution.py:81
  95.7 6.1 %collective-permute-start.1 = (f16[64,8,640]{2,0,1:T(8,128)(2,1)S(1)}, f16[64,8,640]{2,0,1:T(8,128)(2,1)S(1)}, u32[]{:S(2)}, u32[]{:S(2)}) collective-permute-start(f16[64,8,640]{2,0,1:T(8,128)(2,1)S(1)} %copy.51), channel_id=1, source_target_pairs={{0,2},{2,0},{1,3},{3,1},{4,6},{6,4},{5,7},{7,5},{8,10},{10,8},{9,1... | collective-permute-start | bytes 1966088 | tf_op jit(solution)/shard_map/ppermute | solution.py:95
  101.8 0.8 copy-start.2
  109.0 2.8 %collective-permute-start.2 = (f32[]{:T(128)}, f32[]{:T(128)}, u32[]{:S(2)}, u32[]{:S(2)}) collective-permute-start(f32[]{:T(128)} %add.76), channel_id=1, source_target_pairs={{0,1},{1,0},{2,3},{3,2},{4,5},{5,4},{6,7},{7,6},{8,9},{9,8},{10,11... | collective-permute-start | bytes 20 | tf_op jit(solution)/shard_map/ppermute | solution.py:105
  112.5 1.6 %copy-start.3 = (f32[1024,512]{1,0:T(8,128)S(1)}, f32[1024,512]{1,0:T(8,128)}, u32[]{:S(2)}) copy-start(f32[1024,512]{1,0:T(8,128)} %param.15) | copy-start | bytes 6291460
  112.5 2.2 %copy-start.4 = (f32[1024,512]{1,0:T(8,128)S(1)}, f32[1024,512]{1,0:T(8,128)}, u32[]{:S(2)}) copy-start(f32[1024,512]{1,0:T(8,128)} %param.16) | copy-start | bytes 6291460
  114.8 8.2 %copy-start.5 = (f32[64,1024]{1,0:T(8,128)S(1)}, f32[64,1024]{1,0:T(8,128)}, u32[]{:S(2)}) copy-start(f32[64,1024]{1,0:T(8,128)} %param.18) | copy-start | bytes 786436
  114.8 8.2 %copy-start.6 = (f32[64,1024]{1,0:T(8,128)S(1)}, f32[64,1024]{1,0:T(8,128)}, u32[]{:S(2)}) copy-start(f32[64,1024]{1,0:T(8,128)} %param.19) | copy-start | bytes 786436
  114.8 8.2 %copy-start.7 = (f32[64,1024]{1,0:T(8,128)S(1)}, f32[64,1024]{1,0:T(8,128)}, u32[]{:S(2)}) copy-start(f32[64,1024]{1,0:T(8,128)} %param.20) | copy-start | bytes 786436
  121.5 4.0 %copy-start = (bf16[1024,512]{1,0:T(8,128)(2,1)}, bf16[1024,512]{1,0:T(8,128)(2,1)S(1)}, u32[]{:S(2)}) copy-start(bf16[1024,512]{1,0:T(8,128)(2,1)S(1)} %get-tuple-element.20) | copy-start | bytes 3145732
  121.5 3.4 %copy-start.8 = (f32[1024]{0:T(1024)S(1)}, f32[1024]{0:T(1024)}, u32[]{:S(2)}) copy-start(f32[1024]{0:T(1024)} %param.21) | copy-start | bytes 12292
  121.5 3.4 %copy-start.9 = (f32[1024]{0:T(1024)S(1)}, f32[1024]{0:T(1024)}, u32[]{:S(2)}) copy-start(f32[1024]{0:T(1024)} %param.22) | copy-start | bytes 12292
  121.5 3.4 %copy-start.10 = (f32[1024]{0:T(1024)S(1)}, f32[1024]{0:T(1024)}, u32[]{:S(2)}) copy-start(f32[1024]{0:T(1024)} %param.23) | copy-start | bytes 12292
  122.3 16.9 %collective-permute-start.3 = (bf16[512,512]{1,0:T(8,128)(2,1)}, bf16[512,512]{1,0:T(8,128)(2,1)S(1)}, u32[]{:S(2)}, u32[]{:S(2)}) collective-permute-start(bf16[512,512]{1,0:T(8,128)(2,1)} %dynamic-slice_bitcast_fusion.1), channel_id=1, source_target_pairs={{0,1},{1,0},{2,3},{3,2},{4,5},{5,4},{6,7},{7,6},{8,9},{9,8},{10,11... | collective-permute-start | bytes 1572872 | tf_op jit(solution)/shard_map/ppermute | solution.py:123
  124.0 11.9 %collective-permute-start.5 = (bf16[32,1024]{1,0:T(8,128)(2,1)S(1)}, bf16[32,1024]{1,0:T(8,128)(2,1)S(1)}, u32[]{:S(2)}, u32[]{:S(2)}) collective-permute-start(bf16[32,1024]{1,0:T(8,128)(2,1)S(1)} %dynamic-slice_bitcast_fusion.2), channel_id=1, source_target_pairs={{0,1},{1,0},{2,3},{3,2},{4,5},{5,4},{6,7},{7,6},{8,9},{9,8},{10,11... | collective-permute-start | bytes 196616 | tf_op jit(solution)/shard_map/ppermute | solution.py:123
  125.5 15.9 %copy-start.1 = (bf16[1024,512]{1,0:T(8,128)(2,1)S(1)}, bf16[1024,512]{1,0:T(8,128)(2,1)}, u32[]{:S(2)}) copy-start(bf16[1024,512]{1,0:T(8,128)(2,1)} %copy-done) | copy-start | bytes 3145732
  125.5 12.8 %collective-permute-start.7 = (bf16[1024]{0:T(1024)(128)(2,1)S(1)}, bf16[1024]{0:T(1024)(128)(2,1)S(1)}, u32[]{:S(2)}, u32[]{:S(2)}) collective-permute-start(bf16[1024]{0:T(1024)(128)(2,1)S(1)} %get-tuple-element.12), channel_id=1, source_target_pairs={{0,1},{1,0},{2,3},{3,2},{4,5},{5,4},{6,7},{7,6},{8,9},{9,8},{10,11... | collective-permute-start | bytes 6152 | tf_op jit(solution)/shard_map/ppermute | solution.py:131
  136.0 3.2 %collective-permute-start.6 = (bf16[32,1024]{1,0:T(8,128)(2,1)S(1)}, bf16[32,1024]{1,0:T(8,128)(2,1)S(1)}, u32[]{:S(2)}, u32[]{:S(2)}) collective-permute-start(bf16[32,1024]{1,0:T(8,128)(2,1)S(1)} %collective-permute-done.5), channel_id=1, source_target_pairs={{0,2},{2,0},{1,3},{3,1},{4,6},{6,4},{5,7},{7,5},{8,10},{10,8},{9,1... | collective-permute-start | bytes 196616 | tf_op jit(solution)/shard_map/ppermute | solution.py:124
  139.2 2.0 %collective-permute-start.4 = (bf16[512,512]{1,0:T(8,128)(2,1)S(1)}, bf16[512,512]{1,0:T(8,128)(2,1)S(1)}, u32[]{:S(2)}, u32[]{:S(2)}) collective-permute-start(bf16[512,512]{1,0:T(8,128)(2,1)S(1)} %collective-permute-done.3), channel_id=1, source_target_pairs={{0,2},{2,0},{1,3},{3,1},{4,6},{6,4},{5,7},{7,5},{8,10},{10,8},{9,1... | collective-permute-start | bytes 1572872 | tf_op jit(solution)/shard_map/ppermute | solution.py:124

commit v2 on v1

v2 whole, which is shorter than its diff:
```python
import math

import jax
import jax.numpy as jnp
import numpy as np
from jax import lax
from jax.experimental import pallas as pl
from jax.experimental.pallas import tpu as pltpu
from jax.sharding import Mesh
from jax.sharding import PartitionSpec as P

D = 2048
KEY_WIDTH = 512
EXPERTS = 64
LANES = 128
ROW = KEY_WIDTH + LANES

beta_one = 0.9
beta_two = 0.95
step_rate = 0.01
epsilon = 1e-08
bias_one = 1.0 - 0.9**10
bias_two = 1.0 - 0.95**10

WIDE = ("z", "y", "xh", "c")
ALL = ("z", "y", "xh", "c", "xl")


def place(z, y, x, c):
    return (((z * 4 + y) * 2 + x // 2) * 2 + c) * 2 + x % 2


def permutation(target):
    return [
        (place(z, y, x, c), place(*target(z, y, x, c)))
        for z in range(8)
        for y in range(4)
        for x in range(4)
        for c in range(2)
    ]


def along(stage, shift):
    def target(z, y, x, c):
        if c == stage:
            return z, y, (x + shift) % 4, c
        return z, (y + shift) % 4, x, c

    return permutation(target)


SIBLING = permutation(lambda z, y, x, c: (z, y, x, 1 - c))
PARTNER = permutation(lambda z, y, x, c: (z, y, x ^ 1, c))


def send(x, pairs):
    return lax.ppermute(x, ALL, pairs)


def adamw(master, first_moment, second, gradient, factor, decay_rate):
    scaled = factor * gradient
    first_new = beta_one * first_moment + (1.0 - beta_one) * scaled
    second_new = beta_two * second + (1.0 - beta_two) * scaled * scaled
    update = (
        first_new / bias_one / (jnp.sqrt(second_new / bias_two) + epsilon) + decay_rate * master
    )
    master_new = master - step_rate * update
    return (master_new, first_new, second_new)


def group_of(t, p, q):
    x = jnp.where(t == 0, p, q)
    y = jnp.where(t == 0, q, p)
    return x % 2, t * 8 + (x // 2) * 4 + y


def micro_total(stack):
    return (stack[0].astype(jnp.float32) + stack[1].astype(jnp.float32)).astype(jnp.bfloat16)


def pack_group(key_ref, router_ref, gain_ref, half, group, store):
    key = micro_total(key_ref[...]).astype(jnp.float32)
    router = micro_total(router_ref[...]).astype(jnp.float32)
    gain = micro_total(gain_ref[:, half]).astype(jnp.float32)
    gain = jnp.where(group == 0, gain, 0.0)
    lane = lax.broadcasted_iota(jnp.int32, (8, LANES), 1)
    row = lax.broadcasted_iota(jnp.int32, (8, LANES), 0)
    for z in range(8):
        tile = router[:, (z // 2) * LANES : (z // 2 + 1) * LANES]
        low = lane < 64
        mine = low if z % 2 == 0 else jnp.logical_not(low)
        spare = jnp.where(row // 2 == z // 2, gain, 0.0)
        store(z, key[z * 8 : (z + 1) * 8], jnp.where(mine, tile, spare))


def pack_sent(where_ref, *refs):
    keys, routers, gain_ref, out_ref = refs[:4], refs[4:8], refs[8], refs[9]
    t, p, q = where_ref[0], where_ref[1], pl.program_id(0)
    for k in range(4):
        half, group = group_of(t, (p + k) % 4, q)

        def store(z, key, tile, k=k):
            out_ref[k, 0, z, :, :KEY_WIDTH] = key.astype(jnp.bfloat16)
            out_ref[k, 0, z, :, KEY_WIDTH:] = tile.astype(jnp.bfloat16)

        pack_group(keys[k], routers[k], gain_ref, half, group, store)


def pack_kept(where_ref, *refs):
    keys, routers, gain_ref, got_ref, outs = refs[:4], refs[4:8], refs[8], refs[9], refs[10:]
    t, p, q = where_ref[0], where_ref[1], pl.program_id(0)
    for k in range(4):
        half, group = group_of(t, (p + k) % 4, q)

        def store(z, key, tile, k=k):
            got = got_ref[k, 0, z].astype(jnp.float32)
            outs[k][0, z, :, :KEY_WIDTH] = (key + got[:, :KEY_WIDTH]).astype(jnp.bfloat16)
            outs[k][0, z, :, KEY_WIDTH:] = (tile + got[:, KEY_WIDTH:]).astype(jnp.bfloat16)

        pack_group(keys[k], routers[k], gain_ref, half, group, store)


def pack(t, p, key_grads, router_grads, gain_grads, got=None):
    def key_map(k):
        def index(q, where_ref):
            half, group = group_of(where_ref[0], (where_ref[1] + k) % 4, q)
            return 0, half * 16 + group, 0

        return index

    def router_map(k):
        def index(q, where_ref):
            half, group = group_of(where_ref[0], (where_ref[1] + k) % 4, q)
            return 0, group // 2, half * 2 + group % 2

        return index

    in_specs = [pl.BlockSpec((2, 64, KEY_WIDTH), key_map(k)) for k in range(4)]
    in_specs += [pl.BlockSpec((2, 8, 512), router_map(k)) for k in range(4)]
    in_specs += [pl.BlockSpec((2, 2, 8, LANES), lambda q, where_ref: (0, 0, 0, 0))]
    operands = [key_grads] * 4 + [router_grads] * 4 + [gain_grads]
    whole = pl.BlockSpec((4, 1, 8, 8, ROW), lambda q, where_ref: (0, q, 0, 0, 0))
    if got is None:
        body, out_specs = pack_sent, whole
        out_shape = jax.ShapeDtypeStruct((4, 4, 8, 8, ROW), jnp.bfloat16)
    else:
        body = pack_kept
        in_specs += [whole]
        operands += [got]
        out_specs = [pl.BlockSpec((1, 8, 8, ROW), lambda q, where_ref: (q, 0, 0, 0))] * 4
        out_shape = [jax.ShapeDtypeStruct((4, 8, 8, ROW), jnp.bfloat16)] * 4
    return pl.pallas_call(
        body,
        grid_spec=pltpu.PrefetchScalarGridSpec(
            num_scalar_prefetch=1, grid=(4,), in_specs=in_specs, out_specs=out_specs
        ),
        out_shape=out_shape,
        compiler_params=pltpu.CompilerParams(vmem_limit_bytes=32 * 1024 * 1024),
    )(jnp.stack([t, p]), *operands)


def add_rows(where_ref, *refs):
    terms, outs = refs[:4], refs[4:]
    for k in range(4):
        at = (where_ref[0] + k) % 4
        total = terms[0][at].astype(jnp.float32)
        for term in terms[1:]:
            total = total + term[at].astype(jnp.float32)
        outs[k][...] = total


def sum_rotated(q, terms):
    return pl.pallas_call(
        add_rows,
        in_specs=[pl.BlockSpec(memory_space=pltpu.SMEM)]
        + [pl.BlockSpec(memory_space=pltpu.VMEM)] * 4,
        out_specs=[pl.BlockSpec(memory_space=pltpu.VMEM)] * 4,
        out_shape=[jax.ShapeDtypeStruct((8, 8, ROW), jnp.float32)] * 4,
        compiler_params=pltpu.CompilerParams(vmem_limit_bytes=32 * 1024 * 1024),
    )(q.reshape(1), *terms)


def spare_place(z, shape, block_axis=None):
    row = lax.broadcasted_iota(jnp.int32, shape, len(shape) - 2)
    lane = lax.broadcasted_iota(jnp.int32, shape, len(shape) - 1)
    if block_axis is not None:
        z = lax.broadcasted_iota(jnp.int32, shape, block_axis) % 8
    return (row == (2 * (z // 2) + 2) % 8) & (lane == jnp.where(z % 2 == 0, 64, 0))


def unpack(blocks):
    key = blocks[:, :, :KEY_WIDTH].reshape(1024, KEY_WIDTH)
    tiles = blocks[:, :, KEY_WIDTH:].reshape(8, 2, 4, 2, 8, LANES)
    low = lax.broadcasted_iota(jnp.int32, (8, LANES), 1) < 64
    router = jnp.where(low, tiles[:, :, :, 0], tiles[:, :, :, 1])
    router = router.transpose(0, 3, 1, 2, 4).reshape(EXPERTS, 1024)
    pairs = jnp.where(low, tiles[0, 0, :, 1], tiles[0, 0, :, 0])
    gain = jnp.concatenate([pairs[m, 2 * m : 2 * m + 2] for m in range(4)]).reshape(1024)
    return key, router, gain


def on_device(
    key_grads,
    router_grads,
    gain_grads,
    key_master,
    key_first,
    key_second,
    router_master,
    router_first,
    router_second,
    gain_master,
    gain_first,
    gain_second,
):
    core = lax.axis_index("c")
    half = lax.axis_index("xl")
    x = lax.axis_index("xh") * 2 + half
    y = lax.axis_index("y")
    z = lax.axis_index("z")
    grads = (key_grads[0, 0], router_grads[0, 0], gain_grads.reshape(2, 2, 8, LANES))
    first_place = jnp.where(core == 0, x, y)
    second_place = jnp.where(core == 0, y, x)
    got = send(pack(1 - core, second_place, *grads), SIBLING)
    parts = pack(core, first_place, *grads, got)
    parts = [parts[0]] + [send(parts[k], along(0, k)) for k in (1, 2, 3)]
    parts = sum_rotated(second_place, parts)
    parts = [parts[0]] + [send(parts[k], along(1, k)) for k in (1, 2, 3)]
    partial = (parts[0] + parts[1]) + (parts[2] + parts[3])
    own = jnp.sum(lax.all_to_all(partial, "z", 0, 0, tiled=True), axis=0)
    largest = jnp.maximum(jnp.max(jnp.abs(own)), 1e-30)
    exponent = jnp.floor(jnp.log2(largest)) - 13.0
    tile = jnp.where(spare_place(z, (8, LANES)), exponent, own[:, KEY_WIDTH:] * jnp.exp2(-exponent))
    code = jnp.concatenate([own[:, :KEY_WIDTH] * jnp.exp2(-exponent), tile], axis=1)
    code = code.astype(jnp.float16)
    parts = lax.all_to_all(
        jnp.broadcast_to(code[None], (64, 8, ROW)), ("xh", "y", "z"), 0, 0, tiled=True
    )
    other = send(parts, SIBLING)
    blocks = jnp.where(
        core == 0, jnp.concatenate([parts, other]), jnp.concatenate([other, parts])
    )
    blocks = blocks.astype(jnp.float32)
    held = spare_place(None, (128, 8, LANES), 0)
    exponents = jnp.sum(jnp.where(held, blocks[:, :, KEY_WIDTH:], 0.0), axis=(1, 2), keepdims=True)
    blocks = blocks * jnp.exp2(exponents)
    key_sum, router_sum, gain_sum = unpack(blocks)
    squares = (
        jnp.sum(key_sum * key_sum) + jnp.sum(router_sum * router_sum) + jnp.sum(gain_sum * gain_sum)
    )
    squares = squares + send(squares, PARTNER)
    clip_limit = 0.5 * math.sqrt(D * KEY_WIDTH + EXPERTS * D + D)
    factor = clip_limit / jnp.maximum(jnp.sqrt(squares), clip_limit)
    key_new, key_first_new, key_second_new = adamw(
        key_master, key_first, key_second, key_sum, factor, 0.1
    )
    router_new, router_first_new, router_second_new = adamw(
        router_master, router_first, router_second, router_sum, factor, 0.1
    )
    gain_new, gain_first_new, gain_second_new = adamw(
        gain_master, gain_first, gain_second, gain_sum, factor, 0.0
    )
    key_low = key_new.astype(jnp.bfloat16)
    router_low = router_new.astype(jnp.bfloat16)
    gain_low = gain_new.astype(jnp.bfloat16)

    def exchange(low):
        mine = lax.dynamic_index_in_dim(low, core, 0, keepdims=False)
        far = send(mine, PARTNER)
        near = send(far, SIBLING)
        far = jnp.where(core == 0, jnp.stack([far, near]), jnp.stack([near, far]))
        return jnp.where(half == 0, jnp.stack([low, far]), jnp.stack([far, low]))

    key_weight = exchange(key_low.reshape(2, 512, 512)).reshape(D, KEY_WIDTH)
    router_weight = exchange(router_low.reshape(2, 32, 1024)).reshape(2, EXPERTS, 1024)
    router_weight = jnp.concatenate([router_weight[0], router_weight[1]], axis=1)
    gain_far = send(gain_low, PARTNER)
    gain_weight = jnp.where(
        half == 0, jnp.concatenate([gain_low, gain_far]), jnp.concatenate([gain_far, gain_low])
    )
    return (
        key_new,
        key_first_new,
        key_second_new,
        router_new,
        router_first_new,
        router_second_new,
        gain_new,
        gain_first_new,
        gain_second_new,
        key_weight,
        router_weight,
        gain_weight,
    )


def solution(mesh):
    fine = Mesh(np.asarray(mesh.devices).reshape(8, 4, 2, 2, 2), ("z", "y", "xh", "c", "xl"))
    in_specs = (
        P(WIDE, "xl", None, None, None),
        P(WIDE, "xl", None, None, None),
        P(WIDE, "xl", None, None),
        P("xl", None),
        P("xl", None),
        P("xl", None),
        P(None, "xl"),
        P(None, "xl"),
        P(None, "xl"),
        P("xl"),
        P("xl"),
        P("xl"),
    )
    out_specs = (
        P("xl", None),
        P("xl", None),
        P("xl", None),
        P(None, "xl"),
        P(None, "xl"),
        P(None, "xl"),
        P("xl"),
        P("xl"),
        P("xl"),
        P(),
        P(),
        P(),
    )
    return jax.shard_map(
        on_device, mesh=fine, in_specs=in_specs, out_specs=out_specs, check_vma=False
    )
```

time: 144 us -> 130 us (0.903)
  waiting for transfers between devices: 51.2 us -> 38.8 us
  other arithmetic: 29.2 us -> 20.2 us
  Pallas kernels: 0 us -> 6.9 us
  blocking collectives: 25.4 us -> 22.4 us
  local copies, waits for them, and re-layouts: 5 us -> 7.28 us
  starting transfers between devices: 28 us -> 30.2 us
    all_to_all x1, waiting for transfers between devices: 34.4 us -> 8.36 us  [on_device(): own = jnp.sum(lax.all_to_all(partial, 'z', 0, 0, tiled=True), axis=0)]
    ppermute x8 -> x14, waiting for transfers between devices: 16.8 us -> 30.4 us  [send(): return lax.ppermute(x, ALL, pairs)]
    ppermute x8 -> x14, starting transfers between devices: 14.2 us -> 22.3 us  [send(): return lax.ppermute(x, ALL, pairs)]
    pallas_call x0 -> x3, Pallas kernels: none -> 6.9 us  [the longest x2 6.75 us: pack(): pl.pallas_call(body, grid_spec=pltpu.PrefetchScalarGridSpec(num_scalar_pr...]
    all_to_all x1, starting transfers between devices: 13.8 us -> 7.89 us  [on_device(): own = jnp.sum(lax.all_to_all(partial, 'z', 0, 0, tiled=True), axis=0)]
    unnamed x24 -> x27, local copies, waits for them, and re-layouts: 2.38 us -> 7.12 us
    reduce_sum x4 -> x2, other arithmetic: 7.01 us -> 2.33 us  [the longest x1 2.32 us: on_device(): jnp.sum(jnp.where(held, blocks[:, :, KEY_WIDTH:], 0.0), axis=(1, 2), keep...]
    all_to_all x1, blocking collectives: 25.4 us -> 22.4 us  [on_device(): lax.all_to_all(jnp.broadcast_to(code[None], (64, 8, ROW)), ('xh', 'y', 'z...]
  transfers between devices with their start and end apart: 9 -> 15, of which waited for: 7 -> 12; matrix products, arithmetic and copies ran while one was open for 2% -> 2% of each run, Pallas kernels for 0% -> 0%
where the time goes in v2:
time: 130 us
  waiting for transfers between devices  38.8 us (30%)
  starting transfers between devices  30.2 us (23%)
  blocking collectives  22.4 us (17%)
  other arithmetic  20.2 us (16%)
  local copies, waits for them, and re-layouts  7.28 us (6%)
  Pallas kernels  6.9 us (5%)
  between operations  4.3 us (3%)
    ppermute x14, waiting for transfers between devices, send(): return lax.ppermute(x, ALL, pairs)  30.4 us
    all_to_all x1, blocking collectives, on_device(): lax.all_to_all(jnp.broadcast_to(code[None], (64, 8, ROW)), ('xh', 'y', 'z...  22.4 us
    ppermute x14, starting transfers between devices, send(): return lax.ppermute(x, ALL, pairs)  22.3 us
    all_to_all x1, waiting for transfers between devices, on_device(): own = jnp.sum(lax.all_to_all(partial, 'z', 0, 0, tiled=True), axis=0)  8.36 us
    all_to_all x1, starting transfers between devices, on_device(): own = jnp.sum(lax.all_to_all(partial, 'z', 0, 0, tiled=True), axis=0)  7.89 us
    unnamed x27, local copies, waits for them, and re-layouts  7.12 us
    convert_element_type x1, other arithmetic, on_device(): key_low = key_new.astype(jnp.bfloat16)  6.76 us
    pallas_call x2, Pallas kernels, pack(): pl.pallas_call(body, grid_spec=pltpu.PrefetchScalarGridSpec(num_scalar_pr...  6.75 us
  transfers between devices with their start and end apart: 15, of which 12 were waited for; matrix products, arithmetic and copies ran while one was open for 2% of the time, Pallas kernels for 0%

profile of v2, /device:TPU:1, one launch (start us, length us, event | category | flops | bytes accessed | tf_op | source)
XLA Modules:
  0.0 130.1 jit_solution(2596083442715545059)
XLA Ops:
  1.4 2.2 %copy-done = bf16[1,1,2,2048,512]{4,3,2,1,0:T(8,128)(2,1)S(1)} copy-done((bf16[1,1,2,2048,512]{4,3,2,1,0:T(8,128)(2,1)S(1)}, bf16[1,1,2,2048,512]{4,3,2,1,0:T(8,128)(2,1)}, u32[]{:S(2)}) %copy-start) | copy-done | bytes 4194328
  3.6 1.0 copy-done.2
  4.7 3.2 %shard_map.211 = bf16[4,4,8,8,640]{4,3,2,1,0:T(8,128)(2,1)S(1)} custom-call(s32[2]{0:T(128)S(1)} %pad_add_fusion.1.where_ref, bf16[2,2048,512]{2,1,0:T(8,128)(2,1)S(1)} %bitcast.81, bf16[2,2048,512]{2,1,0:T(8,128)(2,1)S(1)} %bitcast.82, bf16[2,2048,512]{2,1,0:T(8,128)(2,1)S(1)} %bitcast.83, bf16[2,2048,512]{2,1,0:T(8,128)(2,1)S(1)} %bitcast.84, ...), custom_call_target="tpu_custom_call" | custom-call | tf_op jit(solution)/shard_map/pallas_call | solution.py:152
  7.9 3.3 %collective-permute-start = (bf16[4,4,8,8,640]{4,3,2,1,0:T(8,128)(2,1)S(1)}, bf16[4,4,8,8,640]{4,3,2,1,0:T(8,128)(2,1)S(1)}, u32[]{:S(2)}, u32[]{:S(2)}) collective-permute-start(bf16[4,4,8,8,640]{4,3,2,1,0:T(8,128)(2,1)S(1)} %shard_map.211), channel_id=1, source_target_pairs={{0,2},{2,0},{1,3},{3,1},{4,6},{6,4},{5,7},{7,5},{8,10},{10,8},{9,1... | collective-permute-start | bytes 3932168 | tf_op jit(solution)/shard_map/ppermute | solution.py:57
  11.3 2.6 %collective-permute-done.refs_9_ = bf16[4,4,8,8,640]{4,3,2,1,0:T(8,128)(2,1)S(1)} collective-permute-done((bf16[4,4,8,8,640]{4,3,2,1,0:T(8,128)(2,1)S(1)}, bf16[4,4,8,8,640]{4,3,2,1,0:T(8,128)(2,1)S(1)}, u32[]{:S(2)}, u32[]{:S(2)}) %collective-permute-start) | collective-permute-done | bytes 1310752 | tf_op jit(solution)/shard_map/ppermute | solution.py:57
  13.9 2.2 %copy-done.1 = bf16[1,1,2,2048,512]{4,3,2,1,0:T(8,128)(2,1)S(1)} copy-done((bf16[1,1,2,2048,512]{4,3,2,1,0:T(8,128)(2,1)S(1)}, bf16[1,1,2,2048,512]{4,3,2,1,0:T(8,128)(2,1)}, u32[]{:S(2)}) %copy-start.1) | copy-done | bytes 4194328
  16.0 3.6 %shard_map.212 = (bf16[4,8,8,640]{3,2,1,0:T(8,128)(2,1)S(1)}, bf16[4,8,8,640]{3,2,1,0:T(8,128)(2,1)S(1)}, bf16[4,8,8,640]{3,2,1,0:T(8,128)(2,1)S(1)}, bf16[4,8,8,640]{3,2,1,0:T(8,128)(2,1)S(1)}) custom-call(s32[2]{0:T(128)S(1)} %pad_add_fusion.where_ref, bf16[2,2048,512]{2,1,0:T(8,128)(2,1)S(1)} %bitcast.85, bf16[2,2048,512]{2,1,0:T(8,128)(2,1)S(1)} %bitcast.86, ...), custom_call_target="tpu_custom_call" | custom-call | tf_op jit(solution)/shard_map/pallas_call | solution.py:152
  19.7 2.2 %collective-permute-start.2 = (bf16[4,8,8,640]{3,2,1,0:T(8,128)(2,1)S(1)}, bf16[4,8,8,640]{3,2,1,0:T(8,128)(2,1)S(1)}, u32[]{:S(2)}, u32[]{:S(2)}) collective-permute-start(bf16[4,8,8,640]{3,2,1,0:T(8,128)(2,1)S(1)} %get-tuple-element.22), channel_id=1, source_target_pairs={{0,4},{2,18},{1,5},{3,19},{4,0},{6,22},{5,1},{7,23},{8,12},{10,26}... | collective-permute-start | bytes 983048 | tf_op jit(solution)/shard_map/ppermute | solution.py:57
  21.9 1.1 collective-permute-start.3
  22.9 7.7 %collective-permute-done.1.refs_1_ = bf16[4,8,8,640]{3,2,1,0:T(8,128)(2,1)S(1)} collective-permute-done((bf16[4,8,8,640]{3,2,1,0:T(8,128)(2,1)S(1)}, bf16[4,8,8,640]{3,2,1,0:T(8,128)(2,1)S(1)}, u32[]{:S(2)}, u32[]{:S(2)}) %collective-permute-start.1) | collective-permute-done | bytes 327712 | tf_op jit(solution)/shard_map/ppermute | solution.py:57
  31.4 1.4 %collective-permute-start.5 = (f32[8,8,640]{2,1,0:T(8,128)S(1)}, f32[8,8,640]{2,1,0:T(8,128)S(1)}, u32[]{:S(2)}, u32[]{:S(2)}) collective-permute-start(f32[8,8,640]{2,1,0:T(8,128)S(1)} %get-tuple-element.26), channel_id=1, source_target_pairs={{0,16},{2,6},{1,17},{3,7},{4,20},{6,2},{5,21},{7,3},{8,24},{10,14}... | collective-permute-start | bytes 491528 | tf_op jit(solution)/shard_map/ppermute | solution.py:57
  32.8 0.9 collective-permute-start.6
  34.3 2.9 %collective-permute-done.5 = f32[8,8,640]{2,1,0:T(8,128)S(1)} collective-permute-done((f32[8,8,640]{2,1,0:T(8,128)S(1)}, f32[8,8,640]{2,1,0:T(8,128)S(1)}, u32[]{:S(2)}, u32[]{:S(2)}) %collective-permute-start.5) | collective-permute-done | bytes 163872 | tf_op jit(solution)/shard_map/ppermute | solution.py:57
  37.9 1.5 %collective-permute-done.4 = f32[8,8,640]{2,1,0:T(8,128)S(1)} collective-permute-done((f32[8,8,640]{2,1,0:T(8,128)S(1)}, f32[8,8,640]{2,1,0:T(8,128)S(1)}, u32[]{:S(2)}, u32[]{:S(2)}) %collective-permute-start.4) | collective-permute-done | bytes 163872 | tf_op jit(solution)/shard_map/ppermute | solution.py:57
  40.1 7.9 %all-to-all-start = ((f32[8,8,640]{2,1,0:T(8,128)}), f32[8,8,640]{2,1,0:T(8,128)S(1)}, u32[]{:S(2)}, u32[]{:S(2)}) async-start(f32[8,8,640]{2,1,0:T(8,128)} %add_add_fusion), calls=%async_computation | async-start | bytes 327680 | tf_op jit(solution)/shard_map/all_to_all | solution.py:230
  48.0 8.4 %all-to-all-done = f32[8,8,640]{2,1,0:T(8,128)S(1)} async-done(((f32[8,8,640]{2,1,0:T(8,128)}), f32[8,8,640]{2,1,0:T(8,128)S(1)}, u32[]{:S(2)}, u32[]{:S(2)}) %all-to-all-start) | async-done | bytes 163872 | tf_op jit(solution)/shard_map/all_to_all | solution.py:230
  57.9 22.4 %all_to_all.10 = f16[64,8,640]{2,1,0:T(8,128)(2,1)S(1)} all-to-all(f16[64,8,640]{2,1,0:T(8,128)(2,1)S(1)} %broadcast_in_dim.30), channel_id=1, replica_groups=mesh['z'=8,'y'=4,'xh'=2,'c'=2,'xl'=2] {'xh','y','z'}, dimensions={0} | all-to-all | bytes 1310720 | tf_op jit(solution)/shard_map/all_to_all | solution.py:236
  80.3 7.1 %collective-permute-start.7 = (f16[64,8,640]{2,1,0:T(8,128)(2,1)S(1)}, f16[64,8,640]{2,1,0:T(8,128)(2,1)S(1)}, u32[]{:S(2)}, u32[]{:S(2)}) collective-permute-start(f16[64,8,640]{2,1,0:T(8,128)(2,1)S(1)} %all_to_all.10), channel_id=1, source_target_pairs={{0,2},{2,0},{1,3},{3,1},{4,6},{6,4},{5,7},{7,5},{8,10},{10,8},{9,1... | collective-permute-start | bytes 1966088 | tf_op jit(solution)/shard_map/ppermute | solution.py:57
  87.4 1.7 %collective-permute-done.7 = f16[64,8,640]{2,1,0:T(8,128)(2,1)S(1)} collective-permute-done((f16[64,8,640]{2,1,0:T(8,128)(2,1)S(1)}, f16[64,8,640]{2,1,0:T(8,128)(2,1)S(1)}, u32[]{:S(2)}, u32[]{:S(2)}) %collective-permute-start.7) | collective-permute-done | bytes 655392 | tf_op jit(solution)/shard_map/ppermute | solution.py:57
  89.5 2.3 %fusion.11 = f32[128]{0:T(128)S(1)} fusion(f32[128,8,640]{2,1,0:T(8,128)S(1)} %fusion.2, s32[128]{0:T(128)S(1)} %get-tuple-element.46, s32[128]{0:T(128)S(1)} %get-tuple-element.47, pred[128]{0:T(512)(128)(4,1)S(1)} %compare_and_fusion), kind=kLoop, calls=%fused_computation.32 | loop fusion | flops 5242752 | bytes 525952 | tf_op jit(solution)/shard_map/reduce_sum | solution.py:245
  91.8 1.8 %broadcast_multiply_fusion = f32[128,8,640]{2,1,0:T(8,128)S(1)} fusion(f32[128]{0:T(128)S(1)} %multiply_exponential_fusion, f16[64,8,640]{2,1,0:T(8,128)(2,1)S(1)} %all_to_all.10, f16[64,8,640]{2,1,0:T(8,128)(2,1)} %copy-done.6, pred[]{:T(512)S(6)} %eq.46), kind=kLoop, calls=%fused_computation.10 | loop fusion | flops 3276800 | bytes 3932673 | tf_op jit(solution)/shard_map/mul | solution.py:246
  93.6 1.1 multiply_reduce_fusion
  98.1 1.1 collective-permute-start.8
  99.2 1.6 %collective-permute-done.8 = f32[]{:T(128)} collective-permute-done((f32[]{:T(128)}, f32[]{:T(128)}, u32[]{:S(2)}, u32[]{:S(2)}) %collective-permute-start.8) | collective-permute-done | bytes 36 | tf_op jit(solution)/shard_map/ppermute | solution.py:57
  101.7 6.8 %fusion.27 = (bf16[1024,512]{1,0:T(8,128)(2,1)S(1)}, f32[1024,512]{1,0:T(8,128)}, f32[1024,512]{1,0:T(8,128)}, f32[1024,512]{1,0:T(8,128)}) fusion(f32[1024,512]{1,0:T(8,128)} %param.15, f32[128,8,640]{2,1,0:T(8,128)S(1)} %broadcast_multiply_fusion, f32[]{:T(128)S(6)} %div.72, f32[1024,512]{1,0:T(8,128)} %param.16, f32[1024,512]{1,0:T(8,128)} %param.17), kind=kLoop, calls=%fused_computation.85 | loop fusion | flops 8912896 | bytes 15728644 | tf_op jit(solution)/shard_map/convert_element_type | solution.py:263
  108.4 1.0 copy-done.4
  109.7 1.0 fusion.25
  110.7 1.4 %collective-permute-start.11 = (bf16[32,1024]{1,0:T(8,128)(2,1)S(1)}, bf16[32,1024]{1,0:T(8,128)(2,1)S(1)}, u32[]{:S(2)}, u32[]{:S(2)}) collective-permute-start(bf16[32,1024]{1,0:T(8,128)(2,1)S(1)} %dynamic-slice_bitcast_fusion.1), channel_id=1, source_target_pairs={{0,1},{2,3},{1,0},{3,2},{4,5},{6,7},{5,4},{7,6},{8,9},{10,11},{9,8... | collective-permute-start | bytes 196616 | tf_op jit(solution)/shard_map/ppermute | solution.py:57
  112.9 10.1 %collective-permute-done.11 = bf16[32,1024]{1,0:T(8,128)(2,1)S(1)} collective-permute-done((bf16[32,1024]{1,0:T(8,128)(2,1)S(1)}, bf16[32,1024]{1,0:T(8,128)(2,1)S(1)}, u32[]{:S(2)}, u32[]{:S(2)}) %collective-permute-start.11) | collective-permute-done | bytes 65568 | tf_op jit(solution)/shard_map/ppermute | solution.py:57
  123.0 2.3 %collective-permute-start.12 = (bf16[32,1024]{1,0:T(8,128)(2,1)S(1)}, bf16[32,1024]{1,0:T(8,128)(2,1)S(1)}, u32[]{:S(2)}, u32[]{:S(2)}) collective-permute-start(bf16[32,1024]{1,0:T(8,128)(2,1)S(1)} %collective-permute-done.11), channel_id=1, source_target_pairs={{0,2},{2,0},{1,3},{3,1},{4,6},{6,4},{5,7},{7,5},{8,10},{10,8},{9,1... | collective-permute-start | bytes 196616 | tf_op jit(solution)/shard_map/ppermute | solution.py:57
  127.4 0.8 collective-permute-done.10
  128.4 1.6 %maximum_select_fusion = bf16[2,2,512,512]{3,2,1,0:T(8,128)(2,1)} fusion(bf16[1,2,512,512]{3,2,1,0:T(8,128)(2,1)S(1)} %maximum_select_fusion.2, bf16[1,2,512,512]{3,2,1,0:T(8,128)(2,1)S(1)} %bitcast.100, pred[]{:T(512)S(6)} %eq.55), kind=kLoop, calls=%fused_computation.2 | loop fusion | flops 3145728 | bytes 4194305 | tf_op jit(solution)/shard_map/jit(_where)/select_n | solution.py:272
  (66 shorter events, 9.8 us)
Async XLA Ops:
  1.4 2.2 %copy-start = (bf16[1,1,2,2048,512]{4,3,2,1,0:T(8,128)(2,1)S(1)}, bf16[1,1,2,2048,512]{4,3,2,1,0:T(8,128)(2,1)}, u32[]{:S(2)}) copy-start(bf16[1,1,2,2048,512]{4,3,2,1,0:T(8,128)(2,1)} %param.12) | copy-start | bytes 12582916
  3.6 1.0 copy-start.2
  4.7 9.2 %copy-start.3 = (bf16[1,1,2,64,2048]{4,3,2,1,0:T(8,128)(2,1)S(1)}, bf16[1,1,2,64,2048]{4,3,2,1,0:T(8,128)(2,1)}, u32[]{:S(2)}) copy-start(bf16[1,1,2,64,2048]{4,3,2,1,0:T(8,128)(2,1)} %param.13) | copy-start | bytes 1572868
  7.9 6.0 %collective-permute-start = (bf16[4,4,8,8,640]{4,3,2,1,0:T(8,128)(2,1)S(1)}, bf16[4,4,8,8,640]{4,3,2,1,0:T(8,128)(2,1)S(1)}, u32[]{:S(2)}, u32[]{:S(2)}) collective-permute-start(bf16[4,4,8,8,640]{4,3,2,1,0:T(8,128)(2,1)S(1)} %shard_map.211), channel_id=1, source_target_pairs={{0,2},{2,0},{1,3},{3,1},{4,6},{6,4},{5,7},{7,5},{8,10},{10,8},{9,1... | collective-permute-start | bytes 3932168 | tf_op jit(solution)/shard_map/ppermute | solution.py:57
  13.9 2.2 %copy-start.1 = (bf16[1,1,2,2048,512]{4,3,2,1,0:T(8,128)(2,1)S(1)}, bf16[1,1,2,2048,512]{4,3,2,1,0:T(8,128)(2,1)}, u32[]{:S(2)}) copy-start(bf16[1,1,2,2048,512]{4,3,2,1,0:T(8,128)(2,1)} %param.12) | copy-start | bytes 12582916
  19.6 11.0 %collective-permute-start.1 = (bf16[4,8,8,640]{3,2,1,0:T(8,128)(2,1)S(1)}, bf16[4,8,8,640]{3,2,1,0:T(8,128)(2,1)S(1)}, u32[]{:S(2)}, u32[]{:S(2)}) collective-permute-start(bf16[4,8,8,640]{3,2,1,0:T(8,128)(2,1)S(1)} %get-tuple-element.21), channel_id=1, source_target_pairs={{0,1},{2,10},{1,4},{3,11},{4,5},{6,14},{5,0},{7,15},{8,9},{10,18},... | collective-permute-start | bytes 983048 | tf_op jit(solution)/shard_map/ppermute | solution.py:57
  19.7 10.9 %collective-permute-start.2 = (bf16[4,8,8,640]{3,2,1,0:T(8,128)(2,1)S(1)}, bf16[4,8,8,640]{3,2,1,0:T(8,128)(2,1)S(1)}, u32[]{:S(2)}, u32[]{:S(2)}) collective-permute-start(bf16[4,8,8,640]{3,2,1,0:T(8,128)(2,1)S(1)} %get-tuple-element.22), channel_id=1, source_target_pairs={{0,4},{2,18},{1,5},{3,19},{4,0},{6,22},{5,1},{7,23},{8,12},{10,26}... | collective-permute-start | bytes 983048 | tf_op jit(solution)/shard_map/ppermute | solution.py:57
  21.9 9.4 %collective-permute-start.3 = (bf16[4,8,8,640]{3,2,1,0:T(8,128)(2,1)S(1)}, bf16[4,8,8,640]{3,2,1,0:T(8,128)(2,1)S(1)}, u32[]{:S(2)}, u32[]{:S(2)}) collective-permute-start(bf16[4,8,8,640]{3,2,1,0:T(8,128)(2,1)S(1)} %get-tuple-element.23), channel_id=1, source_target_pairs={{0,5},{2,26},{1,0},{3,27},{4,1},{6,30},{5,4},{7,31},{8,13},{10,2},... | collective-permute-start | bytes 983048 | tf_op jit(solution)/shard_map/ppermute | solution.py:57
  31.4 5.8 %collective-permute-start.5 = (f32[8,8,640]{2,1,0:T(8,128)S(1)}, f32[8,8,640]{2,1,0:T(8,128)S(1)}, u32[]{:S(2)}, u32[]{:S(2)}) collective-permute-start(f32[8,8,640]{2,1,0:T(8,128)S(1)} %get-tuple-element.26), channel_id=1, source_target_pairs={{0,16},{2,6},{1,17},{3,7},{4,20},{6,2},{5,21},{7,3},{8,24},{10,14}... | collective-permute-start | bytes 491528 | tf_op jit(solution)/shard_map/ppermute | solution.py:57
  32.8 5.1 %collective-permute-start.6 = (f32[8,8,640]{2,1,0:T(8,128)S(1)}, f32[8,8,640]{2,1,0:T(8,128)S(1)}, u32[]{:S(2)}, u32[]{:S(2)}) collective-permute-start(f32[8,8,640]{2,1,0:T(8,128)S(1)} %get-tuple-element.27), channel_id=1, source_target_pairs={{0,24},{2,7},{1,25},{3,2},{4,28},{6,3},{5,29},{7,6},{8,0},{10,15},... | collective-permute-start | bytes 491528 | tf_op jit(solution)/shard_map/ppermute | solution.py:57
  33.7 5.7 %collective-permute-start.4 = (f32[8,8,640]{2,1,0:T(8,128)S(1)}, f32[8,8,640]{2,1,0:T(8,128)S(1)}, u32[]{:S(2)}, u32[]{:S(2)}) collective-permute-start(f32[8,8,640]{2,1,0:T(8,128)S(1)} %get-tuple-element.25), channel_id=1, source_target_pairs={{0,8},{2,3},{1,9},{3,6},{4,12},{6,7},{5,13},{7,2},{8,16},{10,11},{... | collective-permute-start | bytes 491528 | tf_op jit(solution)/shard_map/ppermute | solution.py:57
  40.1 16.3 %all-to-all-start = ((f32[8,8,640]{2,1,0:T(8,128)}), f32[8,8,640]{2,1,0:T(8,128)S(1)}, u32[]{:S(2)}, u32[]{:S(2)}) async-start(f32[8,8,640]{2,1,0:T(8,128)} %add_add_fusion), calls=%async_computation | async-start | bytes 327680 | tf_op jit(solution)/shard_map/all_to_all | solution.py:230
  80.3 8.8 %collective-permute-start.7 = (f16[64,8,640]{2,1,0:T(8,128)(2,1)S(1)}, f16[64,8,640]{2,1,0:T(8,128)(2,1)S(1)}, u32[]{:S(2)}, u32[]{:S(2)}) collective-permute-start(f16[64,8,640]{2,1,0:T(8,128)(2,1)S(1)} %all_to_all.10), channel_id=1, source_target_pairs={{0,2},{2,0},{1,3},{3,1},{4,6},{6,4},{5,7},{7,5},{8,10},{10,8},{9,1... | collective-permute-start | bytes 1966088 | tf_op jit(solution)/shard_map/ppermute | solution.py:57
  89.1 2.7 %copy-start.6 = (f16[64,8,640]{2,1,0:T(8,128)(2,1)}, f16[64,8,640]{2,1,0:T(8,128)(2,1)S(1)}, u32[]{:S(2)}) copy-start(f16[64,8,640]{2,1,0:T(8,128)(2,1)S(1)} %collective-permute-done.7) | copy-start | bytes 1966084
  98.1 2.8 %collective-permute-start.8 = (f32[]{:T(128)}, f32[]{:T(128)}, u32[]{:S(2)}, u32[]{:S(2)}) collective-permute-start(f32[]{:T(128)} %add.115), channel_id=1, source_target_pairs={{0,1},{2,3},{1,0},{3,2},{4,5},{6,7},{5,4},{7,6},{8,9},{10,11},{9,8... | collective-permute-start | bytes 20 | tf_op jit(solution)/shard_map/ppermute | solution.py:57
  101.6 8.1 %copy-start.7 = (f32[64,1024]{1,0:T(8,128)S(1)}, f32[64,1024]{1,0:T(8,128)}, u32[]{:S(2)}) copy-start(f32[64,1024]{1,0:T(8,128)} %param.18) | copy-start | bytes 786436
  101.6 8.0 %copy-start.8 = (f32[64,1024]{1,0:T(8,128)S(1)}, f32[64,1024]{1,0:T(8,128)}, u32[]{:S(2)}) copy-start(f32[64,1024]{1,0:T(8,128)} %param.19) | copy-start | bytes 786436
  101.7 8.0 %copy-start.9 = (f32[64,1024]{1,0:T(8,128)S(1)}, f32[64,1024]{1,0:T(8,128)}, u32[]{:S(2)}) copy-start(f32[64,1024]{1,0:T(8,128)} %param.20) | copy-start | bytes 786436
  108.4 1.0 copy-start.4
  108.4 3.7 %copy-start.10 = (f32[1024]{0:T(1024)S(1)}, f32[1024]{0:T(1024)}, u32[]{:S(2)}) copy-start(f32[1024]{0:T(1024)} %param.21) | copy-start | bytes 12292
  108.4 3.7 %copy-start.11 = (f32[1024]{0:T(1024)S(1)}, f32[1024]{0:T(1024)}, u32[]{:S(2)}) copy-start(f32[1024]{0:T(1024)} %param.22) | copy-start | bytes 12292
  108.4 3.7 %copy-start.12 = (f32[1024]{0:T(1024)S(1)}, f32[1024]{0:T(1024)}, u32[]{:S(2)}) copy-start(f32[1024]{0:T(1024)} %param.23) | copy-start | bytes 12292
  109.4 16.8 %collective-permute-start.9 = (bf16[512,512]{1,0:T(8,128)(2,1)S(1)}, bf16[512,512]{1,0:T(8,128)(2,1)S(1)}, u32[]{:S(2)}, u32[]{:S(2)}) collective-permute-start(bf16[512,512]{1,0:T(8,128)(2,1)S(1)} %dynamic-slice_bitcast_fusion), channel_id=1, source_target_pairs={{0,1},{2,3},{1,0},{3,2},{4,5},{6,7},{5,4},{7,6},{8,9},{10,11},{9,8... | collective-permute-start | bytes 1572872 | tf_op jit(solution)/shard_map/ppermute | solution.py:57
  110.7 17.7 %copy-start.5 = (bf16[1024,512]{1,0:T(8,128)(2,1)S(1)}, bf16[1024,512]{1,0:T(8,128)(2,1)}, u32[]{:S(2)}) copy-start(bf16[1024,512]{1,0:T(8,128)(2,1)} %copy-done.4) | copy-start | bytes 3145732
  110.7 12.3 %collective-permute-start.11 = (bf16[32,1024]{1,0:T(8,128)(2,1)S(1)}, bf16[32,1024]{1,0:T(8,128)(2,1)S(1)}, u32[]{:S(2)}, u32[]{:S(2)}) collective-permute-start(bf16[32,1024]{1,0:T(8,128)(2,1)S(1)} %dynamic-slice_bitcast_fusion.1), channel_id=1, source_target_pairs={{0,1},{2,3},{1,0},{3,2},{4,5},{6,7},{5,4},{7,6},{8,9},{10,11},{9,8... | collective-permute-start | bytes 196616 | tf_op jit(solution)/shard_map/ppermute | solution.py:57
  112.7 12.6 %collective-permute-start.13 = (bf16[1024]{0:T(1024)(128)(2,1)S(1)}, bf16[1024]{0:T(1024)(128)(2,1)S(1)}, u32[]{:S(2)}, u32[]{:S(2)}) collective-permute-start(bf16[1024]{0:T(1024)(128)(2,1)S(1)} %get-tuple-element.28), channel_id=1, source_target_pairs={{0,1},{2,3},{1,0},{3,2},{4,5},{6,7},{5,4},{7,6},{8,9},{10,11},{9,8... | collective-permute-start | bytes 6152 | tf_op jit(solution)/shard_map/ppermute | solution.py:57
  123.0 3.2 %collective-permute-start.12 = (bf16[32,1024]{1,0:T(8,128)(2,1)S(1)}, bf16[32,1024]{1,0:T(8,128)(2,1)S(1)}, u32[]{:S(2)}, u32[]{:S(2)}) collective-permute-start(bf16[32,1024]{1,0:T(8,128)(2,1)S(1)} %collective-permute-done.11), channel_id=1, source_target_pairs={{0,2},{2,0},{1,3},{3,1},{4,6},{6,4},{5,7},{7,5},{8,10},{10,8},{9,1... | collective-permute-start | bytes 196616 | tf_op jit(solution)/shard_map/ppermute | solution.py:57
  126.2 2.0 %collective-permute-start.10 = (bf16[512,512]{1,0:T(8,128)(2,1)S(1)}, bf16[512,512]{1,0:T(8,128)(2,1)S(1)}, u32[]{:S(2)}, u32[]{:S(2)}) collective-permute-start(bf16[512,512]{1,0:T(8,128)(2,1)S(1)} %collective-permute-done.9), channel_id=1, source_target_pairs={{0,2},{2,0},{1,3},{3,1},{4,6},{6,4},{5,7},{7,5},{8,10},{10,8},{9,1... | collective-permute-start | bytes 1572872 | tf_op jit(solution)/shard_map/ppermute | solution.py:57

commit v3 on v2

--- a/solution.py
+++ b/solution.py
@@ -78,85 +78,90 @@
     return (stack[0].astype(jnp.float32) + stack[1].astype(jnp.float32)).astype(jnp.bfloat16)
 
 
-def pack_group(key_ref, router_ref, gain_ref, half, group, store):
-    key = micro_total(key_ref[...]).astype(jnp.float32)
-    router = micro_total(router_ref[...]).astype(jnp.float32)
-    gain = micro_total(gain_ref[:, half]).astype(jnp.float32)
-    gain = jnp.where(group == 0, gain, 0.0)
+def pack_local(where_ref, key_ref, router_ref, gain_ref, out_ref, keys, routers, gains, tiles, sems):
+    t, p = where_ref[0], where_ref[1]
+    copies = []
+    for i in range(16):
+        half, group = group_of(t, (p + i // 4) % 4, i % 4)
+        rows = pl.ds(pl.multiple_of((half * 16 + group) * 64, 64), 64)
+        copies.append(pltpu.make_async_copy(key_ref.at[:, rows], keys.at[i], sems.at[i]))
+        rows = pl.ds(pl.multiple_of(group // 2 * 8, 8), 8)
+        columns = pl.ds(pl.multiple_of((half * 2 + group % 2) * 512, 512), 512)
+        copies.append(
+            pltpu.make_async_copy(
+                router_ref.at[:, rows, columns], routers.at[i], sems.at[16 + i]
+            )
+        )
+    gain_copy = pltpu.make_async_copy(gain_ref, gains, sems.at[32])
+    gain_copy.start()
+    for copy in copies:
+        copy.start()
     lane = lax.broadcasted_iota(jnp.int32, (8, LANES), 1)
     row = lax.broadcasted_iota(jnp.int32, (8, LANES), 0)
-    for z in range(8):
-        tile = router[:, (z // 2) * LANES : (z // 2 + 1) * LANES]
-        low = lane < 64
-        mine = low if z % 2 == 0 else jnp.logical_not(low)
-        spare = jnp.where(row // 2 == z // 2, gain, 0.0)
-        store(z, key[z * 8 : (z + 1) * 8], jnp.where(mine, tile, spare))
-
-
-def pack_sent(where_ref, *refs):
-    keys, routers, gain_ref, out_ref = refs[:4], refs[4:8], refs[8], refs[9]
-    t, p, q = where_ref[0], where_ref[1], pl.program_id(0)
-    for k in range(4):
-        half, group = group_of(t, (p + k) % 4, q)
-
-        def store(z, key, tile, k=k):
-            out_ref[k, 0, z, :, :KEY_WIDTH] = key.astype(jnp.bfloat16)
-            out_ref[k, 0, z, :, KEY_WIDTH:] = tile.astype(jnp.bfloat16)
-
-        pack_group(keys[k], routers[k], gain_ref, half, group, store)
-
-
-def pack_kept(where_ref, *refs):
-    keys, routers, gain_ref, got_ref, outs = refs[:4], refs[4:8], refs[8], refs[9], refs[10:]
-    t, p, q = where_ref[0], where_ref[1], pl.program_id(0)
-    for k in range(4):
-        half, group = group_of(t, (p + k) % 4, q)
-
-        def store(z, key, tile, k=k):
-            got = got_ref[k, 0, z].astype(jnp.float32)
-            outs[k][0, z, :, :KEY_WIDTH] = (key + got[:, :KEY_WIDTH]).astype(jnp.bfloat16)
-            outs[k][0, z, :, KEY_WIDTH:] = (tile + got[:, KEY_WIDTH:]).astype(jnp.bfloat16)
-
-        pack_group(keys[k], routers[k], gain_ref, half, group, store)
-
-
-def pack(t, p, key_grads, router_grads, gain_grads, got=None):
-    def key_map(k):
-        def index(q, where_ref):
-            half, group = group_of(where_ref[0], (where_ref[1] + k) % 4, q)
-            return 0, half * 16 + group, 0
-
-        return index
-
-    def router_map(k):
-        def index(q, where_ref):
-            half, group = group_of(where_ref[0], (where_ref[1] + k) % 4, q)
-            return 0, group // 2, half * 2 + group % 2
-
-        return index
-
-    in_specs = [pl.BlockSpec((2, 64, KEY_WIDTH), key_map(k)) for k in range(4)]
-    in_specs += [pl.BlockSpec((2, 8, 512), router_map(k)) for k in range(4)]
-    in_specs += [pl.BlockSpec((2, 2, 8, LANES), lambda q, where_ref: (0, 0, 0, 0))]
-    operands = [key_grads] * 4 + [router_grads] * 4 + [gain_grads]
-    whole = pl.BlockSpec((4, 1, 8, 8, ROW), lambda q, where_ref: (0, q, 0, 0, 0))
-    if got is None:
-        body, out_specs = pack_sent, whole
-        out_shape = jax.ShapeDtypeStruct((4, 4, 8, 8, ROW), jnp.bfloat16)
-    else:
-        body = pack_kept
-        in_specs += [whole]
-        operands += [got]
-        out_specs = [pl.BlockSpec((1, 8, 8, ROW), lambda q, where_ref: (q, 0, 0, 0))] * 4
-        out_shape = [jax.ShapeDtypeStruct((4, 8, 8, ROW), jnp.bfloat16)] * 4
+    low = lane < 64
+    gain_copy.wait()
+    gain = gains[...].astype(jnp.float32)
+    gain = (gain[0:1] + gain[1:2]).astype(jnp.bfloat16).astype(jnp.float32)
+    for half in range(2):
+        tile = jnp.zeros((8, LANES), jnp.float32)
+        for r in range(8):
+            at = half * 1024 + r * LANES
+            tile = jnp.where(row == r, gain[:, at : at + LANES], tile)
+        tiles[half] = tile
+    for i in range(16):
+        half, group = group_of(t, (p + i // 4) % 4, i % 4)
+        copies[2 * i].wait()
+        copies[2 * i + 1].wait()
+        key = keys[i, 0].astype(jnp.float32) + keys[i, 1].astype(jnp.float32)
+        out_ref[i // 4, i % 4, :, :, :KEY_WIDTH] = key.astype(jnp.bfloat16).reshape(
+            8, 8, KEY_WIDTH
+        )
+        router = routers[i, 0].astype(jnp.float32) + routers[i, 1].astype(jnp.float32)
+        spare = jnp.where(group == 0, tiles[half], 0.0)
+        for z in range(8):
+            tile = router[:, (z // 2) * LANES : (z // 2 + 1) * LANES]
+            mine = low if z % 2 == 0 else jnp.logical_not(low)
+            kept = jnp.where(row // 2 == z // 2, spare, 0.0)
+            out_ref[i // 4, i % 4, z, :, KEY_WIDTH:] = jnp.where(mine, tile, kept).astype(
+                jnp.bfloat16
+            )
+
+
+def pack(t, p, grads):
+    return pl.pallas_call(
+        pack_local,
+        in_specs=[pl.BlockSpec(memory_space=pltpu.SMEM)]
+        + [pl.BlockSpec(memory_space=pltpu.HBM)] * 3,
+        out_specs=pl.BlockSpec(memory_space=pltpu.VMEM),
+        out_shape=jax.ShapeDtypeStruct((4, 4, 8, 8, ROW), jnp.bfloat16),
+        scratch_shapes=[
+            pltpu.VMEM((16, 2, 64, KEY_WIDTH), jnp.bfloat16),
+            pltpu.VMEM((16, 2, 8, 512), jnp.bfloat16),
+            pltpu.VMEM((2, D), jnp.bfloat16),
+            pltpu.VMEM((2, 8, LANES), jnp.float32),
+            pltpu.SemaphoreType.DMA((33,)),
+        ],
+        compiler_params=pltpu.CompilerParams(vmem_limit_bytes=16 * 1024 * 1024),
+    )(jnp.stack([t, p]), *[pltpu.with_memory_space_constraint(g, pltpu.HBM) for g in grads])
+
+
+def in_vmem(body, operands, shapes, scalars=()):
+    scalars = [jnp.stack(scalars)] if scalars else []
     return pl.pallas_call(
         body,
-        grid_spec=pltpu.PrefetchScalarGridSpec(
-            num_scalar_prefetch=1, grid=(4,), in_specs=in_specs, out_specs=out_specs
-        ),
-        out_shape=out_shape,
-        compiler_params=pltpu.CompilerParams(vmem_limit_bytes=32 * 1024 * 1024),
-    )(jnp.stack([t, p]), *operands)
+        in_specs=[pl.BlockSpec(memory_space=pltpu.SMEM)] * len(scalars)
+        + [pl.BlockSpec(memory_space=pltpu.VMEM)] * len(operands),
+        out_specs=[pl.BlockSpec(memory_space=pltpu.VMEM)] * len(shapes),
+        out_shape=[jax.ShapeDtypeStruct(*shape) for shape in shapes],
+        compiler_params=pltpu.CompilerParams(vmem_limit_bytes=8 * 1024 * 1024),
+    )(*scalars, *operands)
+
+
+def add_pair(kept_ref, got_ref, *outs):
+    for k in range(4):
+        for q in range(4):
+            total = kept_ref[k, q].astype(jnp.float32) + got_ref[k, q].astype(jnp.float32)
+            outs[k][q] = total.astype(jnp.bfloat16)
 
 
 def add_rows(where_ref, *refs):
@@ -169,15 +174,25 @@
         outs[k][...] = total
 
 
-def sum_rotated(q, terms):
-    return pl.pallas_call(
-        add_rows,
-        in_specs=[pl.BlockSpec(memory_space=pltpu.SMEM)]
-        + [pl.BlockSpec(memory_space=pltpu.VMEM)] * 4,
-        out_specs=[pl.BlockSpec(memory_space=pltpu.VMEM)] * 4,
-        out_shape=[jax.ShapeDtypeStruct((8, 8, ROW), jnp.float32)] * 4,
-        compiler_params=pltpu.CompilerParams(vmem_limit_bytes=32 * 1024 * 1024),
-    )(q.reshape(1), *terms)
+def add_split(where_ref, *refs):
+    terms, (kept_ref, sent_ref) = refs[:-2], refs[-2:]
+    bit = where_ref[0]
+    for i in range(kept_ref.shape[0]):
+        for out_ref, b in ((kept_ref, bit), (sent_ref, 1 - bit)):
+            at = 2 * i + b
+            total = terms[0][at]
+            for term in terms[1:]:
+                total = total + term[at]
+            out_ref[i] = total
+
+
+def reduce_along_z(z, terms):
+    for step in range(3):
+        shape = ((4 >> step, 8, ROW), jnp.float32)
+        kept, sent = in_vmem(add_split, terms, [shape] * 2, [(z >> step) & 1])
+        pairs = permutation(lambda z, y, x, c, step=step: (z ^ (1 << step), y, x, c))
+        terms = [kept, send(sent, pairs)]
+    return (terms[0] + terms[1])[0]
 
 
 def spare_place(z, shape, block_axis=None):
@@ -218,16 +233,16 @@
     x = lax.axis_index("xh") * 2 + half
     y = lax.axis_index("y")
     z = lax.axis_index("z")
-    grads = (key_grads[0, 0], router_grads[0, 0], gain_grads.reshape(2, 2, 8, LANES))
+    grads = (key_grads[0, 0], router_grads[0, 0], gain_grads[0, 0])
     first_place = jnp.where(core == 0, x, y)
     second_place = jnp.where(core == 0, y, x)
-    got = send(pack(1 - core, second_place, *grads), SIBLING)
-    parts = pack(core, first_place, *grads, got)
+    got = send(pack(1 - core, second_place, grads), SIBLING)
+    kept = pack(core, first_place, grads)
+    parts = in_vmem(add_pair, [kept, got], [((4, 8, 8, ROW), jnp.bfloat16)] * 4)
     parts = [parts[0]] + [send(parts[k], along(0, k)) for k in (1, 2, 3)]
-    parts = sum_rotated(second_place, parts)
+    parts = in_vmem(add_rows, parts, [((8, 8, ROW), jnp.float32)] * 4, [second_place])
     parts = [parts[0]] + [send(parts[k], along(1, k)) for k in (1, 2, 3)]
-    partial = (parts[0] + parts[1]) + (parts[2] + parts[3])
-    own = jnp.sum(lax.all_to_all(partial, "z", 0, 0, tiled=True), axis=0)
+    own = reduce_along_z(z, parts)
     largest = jnp.maximum(jnp.max(jnp.abs(own)), 1e-30)
     exponent = jnp.floor(jnp.log2(largest)) - 13.0
     tile = jnp.where(spare_place(z, (8, LANES)), exponent, own[:, KEY_WIDTH:] * jnp.exp2(-exponent))

time: 130 us -> 124 us (0.954)
  local copies, waits for them, and re-layouts: 7.28 us -> 1.15 us
  blocking collectives: 22.4 us -> 28 us
  waiting for transfers between devices: 38.8 us -> 33.4 us
  starting transfers between devices: 30.2 us -> 32 us
    ppermute x14 -> x17, starting transfers between devices: 22.3 us -> 32 us  [send(): return lax.ppermute(x, ALL, pairs)]
    all_to_all x1 -> x0, waiting for transfers between devices: 8.36 us -> none  [on_device(): own = jnp.sum(lax.all_to_all(partial, 'z', 0, 0, tiled=True), axis=0)]
    all_to_all x1 -> x0, starting transfers between devices: 7.89 us -> none  [on_device(): own = jnp.sum(lax.all_to_all(partial, 'z', 0, 0, tiled=True), axis=0)]
    unnamed x27 -> x18, local copies, waits for them, and re-layouts: 7.12 us -> 0.99 us
    all_to_all x1, blocking collectives: 22.4 us -> 28 us  [on_device(): lax.all_to_all(jnp.broadcast_to(code[None], (64, 8, ROW)), ('xh', 'y', 'z...]
    ppermute x14 -> x17, waiting for transfers between devices: 30.4 us -> 33.4 us  [send(): return lax.ppermute(x, ALL, pairs)]
    pallas_call x3 -> x7, Pallas kernels: 6.9 us -> 5.89 us  [the longest x2 5.33 us: pack(): pl.pallas_call(pack_local, in_specs=[pl.BlockSpec(memory_space=pltpu.SMEM...]
  transfers between devices with their start and end apart: 15 -> 17, of which waited for: 12 -> 12; matrix products, arithmetic and copies ran while one was open for 2% -> 3% of each run, Pallas kernels for 0% -> 2%
where the time goes in v3:
time: 124 us
  waiting for transfers between devices  33.4 us (27%)
  starting transfers between devices  32 us (26%)
  blocking collectives  28 us (23%)
  other arithmetic  19.4 us (16%)
  Pallas kernels  5.89 us (5%)
  between operations  4.25 us (3%)
    ppermute x17, waiting for transfers between devices, send(): return lax.ppermute(x, ALL, pairs)  33.4 us
    ppermute x17, starting transfers between devices, send(): return lax.ppermute(x, ALL, pairs)  32 us
    all_to_all x1, blocking collectives, on_device(): lax.all_to_all(jnp.broadcast_to(code[None], (64, 8, ROW)), ('xh', 'y', 'z...  28 us
    convert_element_type x1, other arithmetic, on_device(): key_low = key_new.astype(jnp.bfloat16)  6.76 us
    pallas_call x2, Pallas kernels, pack(): pl.pallas_call(pack_local, in_specs=[pl.BlockSpec(memory_space=pltpu.SMEM...  5.33 us
  transfers between devices with their start and end apart: 17, of which 12 were waited for; matrix products, arithmetic and copies ran while one was open for 3% of the time, Pallas kernels for 2%

profile of v3, /device:TPU:1, one launch (start us, length us, event | category | flops | bytes accessed | tf_op | source)
XLA Modules:
  0.0 124.1 jit_solution(2932497640588578839)
XLA Ops:
  0.7 2.7 %shard_map.212 = bf16[4,4,8,8,640]{4,3,2,1,0:T(8,128)(2,1)S(1)} custom-call(s32[2]{0:T(128)S(1)} %pad_add_fusion.1.where_ref, bf16[2,2048,512]{2,1,0:T(8,128)(2,1)} %bitcast.82, bf16[2,64,2048]{2,1,0:T(8,128)(2,1)} %bitcast.89, bf16[2,2048]{1,0:T(2,128)(2,1)} %bitcast.101), custom_call_target="tpu_custom_call" | custom-call | tf_op jit(solution)/shard_map/pallas_call | solution.py:131
  3.4 3.3 %collective-permute-start = (bf16[4,4,8,8,640]{4,3,2,1,0:T(8,128)(2,1)S(1)}, bf16[4,4,8,8,640]{4,3,2,1,0:T(8,128)(2,1)S(1)}, u32[]{:S(2)}, u32[]{:S(2)}) collective-permute-start(bf16[4,4,8,8,640]{4,3,2,1,0:T(8,128)(2,1)S(1)} %shard_map.212), channel_id=1, source_target_pairs={{0,2},{2,0},{1,3},{3,1},{4,6},{6,4},{5,7},{7,5},{8,10},{10,8},{9,1... | collective-permute-start | bytes 3932168 | tf_op jit(solution)/shard_map/ppermute | solution.py:57
  6.8 2.7 %shard_map.211.kept_ref = bf16[4,4,8,8,640]{4,3,2,1,0:T(8,128)(2,1)S(1)} custom-call(s32[2]{0:T(128)S(1)} %pad_add_fusion.where_ref, bf16[2,2048,512]{2,1,0:T(8,128)(2,1)} %bitcast.83, bf16[2,64,2048]{2,1,0:T(8,128)(2,1)} %bitcast.90, bf16[2,2048]{1,0:T(2,128)(2,1)} %bitcast.102), custom_call_target="tpu_custom_call" | custom-call | tf_op jit(solution)/shard_map/pallas_call | solution.py:131
  9.9 2.2 %collective-permute-start.2 = (bf16[4,8,8,640]{3,2,1,0:T(8,128)(2,1)S(1)}, bf16[4,8,8,640]{3,2,1,0:T(8,128)(2,1)S(1)}, u32[]{:S(2)}, u32[]{:S(2)}) collective-permute-start(bf16[4,8,8,640]{3,2,1,0:T(8,128)(2,1)S(1)} %get-tuple-element.28), channel_id=1, source_target_pairs={{0,4},{2,18},{1,5},{3,19},{4,0},{6,22},{5,1},{7,23},{8,12},{10,26}... | collective-permute-start | bytes 983048 | tf_op jit(solution)/shard_map/ppermute | solution.py:57
  12.1 1.1 collective-permute-start.3
  13.2 7.7 %collective-permute-done.1.refs_1_ = bf16[4,8,8,640]{3,2,1,0:T(8,128)(2,1)S(1)} collective-permute-done((bf16[4,8,8,640]{3,2,1,0:T(8,128)(2,1)S(1)}, bf16[4,8,8,640]{3,2,1,0:T(8,128)(2,1)S(1)}, u32[]{:S(2)}, u32[]{:S(2)}) %collective-permute-start.1) | collective-permute-done | bytes 327712 | tf_op jit(solution)/shard_map/ppermute | solution.py:57
  21.7 2.2 %collective-permute-start.5 = (f32[8,8,640]{2,1,0:T(8,128)S(1)}, f32[8,8,640]{2,1,0:T(8,128)S(1)}, u32[]{:S(2)}, u32[]{:S(2)}) collective-permute-start(f32[8,8,640]{2,1,0:T(8,128)S(1)} %get-tuple-element.32), channel_id=1, source_target_pairs={{0,16},{2,6},{1,17},{3,7},{4,20},{6,2},{5,21},{7,3},{8,24},{10,14}... | collective-permute-start | bytes 491528 | tf_op jit(solution)/shard_map/ppermute | solution.py:57
  24.0 1.2 collective-permute-start.6
  25.1 4.0 %collective-permute-done.4.refs_1_ = f32[8,8,640]{2,1,0:T(8,128)S(1)} collective-permute-done((f32[8,8,640]{2,1,0:T(8,128)S(1)}, f32[8,8,640]{2,1,0:T(8,128)S(1)}, u32[]{:S(2)}, u32[]{:S(2)}) %collective-permute-start.4) | collective-permute-done | bytes 163872 | tf_op jit(solution)/shard_map/ppermute | solution.py:57
  30.2 2.9 %collective-permute-done.7.refs_1_ = f32[4,8,640]{2,1,0:T(8,128)S(1)} collective-permute-done((f32[4,8,640]{2,1,0:T(8,128)S(1)}, f32[4,8,640]{2,1,0:T(8,128)S(1)}, u32[]{:S(2)}, u32[]{:S(2)}) %collective-permute-start.7) | collective-permute-done | bytes 81952 | tf_op jit(solution)/shard_map/ppermute | solution.py:57
  33.2 2.0 %collective-permute-start.8 = (f32[2,8,640]{2,1,0:T(8,128)S(1)}, f32[2,8,640]{2,1,0:T(8,128)S(1)}, u32[]{:S(2)}, u32[]{:S(2)}) collective-permute-start(f32[2,8,640]{2,1,0:T(8,128)S(1)} %get-tuple-element.37), channel_id=1, source_target_pairs={{0,64},{2,66},{1,65},{3,67},{4,68},{6,70},{5,69},{7,71},{8,72},{10... | collective-permute-start | bytes 122888 | tf_op jit(solution)/shard_map/ppermute | solution.py:57
  35.1 1.9 %collective-permute-done.8.refs_1_ = f32[2,8,640]{2,1,0:T(8,128)S(1)} collective-permute-done((f32[2,8,640]{2,1,0:T(8,128)S(1)}, f32[2,8,640]{2,1,0:T(8,128)S(1)}, u32[]{:S(2)}, u32[]{:S(2)}) %collective-permute-start.8) | collective-permute-done | bytes 40992 | tf_op jit(solution)/shard_map/ppermute | solution.py:57
  37.0 5.6 %collective-permute-start.9 = (f32[1,8,640]{2,1,0:T(8,128)S(1)}, f32[1,8,640]{2,1,0:T(8,128)S(1)}, u32[]{:S(2)}, u32[]{:S(2)}) collective-permute-start(f32[1,8,640]{2,1,0:T(8,128)S(1)} %get-tuple-element.39), channel_id=1, source_target_pairs={{0,128},{2,130},{1,129},{3,131},{4,132},{6,134},{5,133},{7,135},{8... | collective-permute-start | bytes 61448 | tf_op jit(solution)/shard_map/ppermute | solution.py:57
  42.6 1.2 collective-permute-done.9
  45.3 28.0 %all_to_all.5 = f16[64,8,640]{2,1,0:T(8,128)(2,1)S(1)} all-to-all(f16[64,8,640]{2,1,0:T(8,128)(2,1)S(1)} %broadcast_in_dim.30), channel_id=1, replica_groups=mesh['z'=8,'y'=4,'xh'=2,'c'=2,'xl'=2] {'xh','y','z'}, dimensions={0} | all-to-all | bytes 1310720 | tf_op jit(solution)/shard_map/all_to_all | solution.py:251
  73.3 8.3 %collective-permute-start.10 = (f16[64,8,640]{2,1,0:T(8,128)(2,1)S(1)}, f16[64,8,640]{2,1,0:T(8,128)(2,1)S(1)}, u32[]{:S(2)}, u32[]{:S(2)}) collective-permute-start(f16[64,8,640]{2,1,0:T(8,128)(2,1)S(1)} %all_to_all.5), channel_id=1, source_target_pairs={{0,2},{2,0},{1,3},{3,1},{4,6},{6,4},{5,7},{7,5},{8,10},{10,8},{9,1... | collective-permute-start | bytes 1966088 | tf_op jit(solution)/shard_map/ppermute | solution.py:57
  81.7 1.7 %collective-permute-done.10 = f16[64,8,640]{2,1,0:T(8,128)(2,1)S(1)} collective-permute-done((f16[64,8,640]{2,1,0:T(8,128)(2,1)S(1)}, f16[64,8,640]{2,1,0:T(8,128)(2,1)S(1)}, u32[]{:S(2)}, u32[]{:S(2)}) %collective-permute-start.10) | collective-permute-done | bytes 655392 | tf_op jit(solution)/shard_map/ppermute | solution.py:57
  83.8 2.3 %fusion.11 = f32[128]{0:T(128)S(1)} fusion(f32[128,8,640]{2,1,0:T(8,128)S(1)} %fusion.2, s32[128]{0:T(128)S(1)} %get-tuple-element.60, s32[128]{0:T(128)S(1)} %get-tuple-element.61, pred[128]{0:T(512)(128)(4,1)S(1)} %compare_and_fusion), kind=kLoop, calls=%fused_computation.32 | loop fusion | flops 5242752 | bytes 525952 | tf_op jit(solution)/shard_map/reduce_sum | solution.py:260
  86.1 1.8 %broadcast_multiply_fusion = f32[128,8,640]{2,1,0:T(8,128)S(1)} fusion(f32[128]{0:T(128)S(1)} %multiply_exponential_fusion, f16[64,8,640]{2,1,0:T(8,128)(2,1)S(1)} %all_to_all.5, f16[64,8,640]{2,1,0:T(8,128)(2,1)} %copy-done.2, pred[]{:T(512)S(6)} %eq.46), kind=kLoop, calls=%fused_computation.10 | loop fusion | flops 3276800 | bytes 3932673 | tf_op jit(solution)/shard_map/mul | solution.py:261
  87.9 1.1 multiply_reduce_fusion
  89.1 0.7 multiply_reduce_fusion.1
  92.3 1.0 collective-permute-start.11
  93.3 1.6 %collective-permute-done.11 = f32[]{:T(128)} collective-permute-done((f32[]{:T(128)}, f32[]{:T(128)}, u32[]{:S(2)}, u32[]{:S(2)}) %collective-permute-start.11) | collective-permute-done | bytes 36 | tf_op jit(solution)/shard_map/ppermute | solution.py:57
  95.7 6.8 %fusion.27 = (bf16[1024,512]{1,0:T(8,128)(2,1)S(1)}, f32[1024,512]{1,0:T(8,128)}, f32[1024,512]{1,0:T(8,128)}, f32[1024,512]{1,0:T(8,128)}) fusion(f32[1024,512]{1,0:T(8,128)} %param.15, f32[128,8,640]{2,1,0:T(8,128)S(1)} %broadcast_multiply_fusion, f32[]{:T(128)S(6)} %div.72, f32[1024,512]{1,0:T(8,128)} %param.16, f32[1024,512]{1,0:T(8,128)} %param.17), kind=kLoop, calls=%fused_computation.84 | loop fusion | flops 8912896 | bytes 15728644 | tf_op jit(solution)/shard_map/convert_element_type | solution.py:278
  102.5 1.0 copy-done
  103.7 1.0 fusion.25
  104.7 1.4 %collective-permute-start.14 = (bf16[32,1024]{1,0:T(8,128)(2,1)S(1)}, bf16[32,1024]{1,0:T(8,128)(2,1)S(1)}, u32[]{:S(2)}, u32[]{:S(2)}) collective-permute-start(bf16[32,1024]{1,0:T(8,128)(2,1)S(1)} %dynamic-slice_bitcast_fusion.1), channel_id=1, source_target_pairs={{0,1},{2,3},{1,0},{3,2},{4,5},{6,7},{5,4},{7,6},{8,9},{10,11},{9,8... | collective-permute-start | bytes 196616 | tf_op jit(solution)/shard_map/ppermute | solution.py:57
  106.9 10.1 %collective-permute-done.14 = bf16[32,1024]{1,0:T(8,128)(2,1)S(1)} collective-permute-done((bf16[32,1024]{1,0:T(8,128)(2,1)S(1)}, bf16[32,1024]{1,0:T(8,128)(2,1)S(1)}, u32[]{:S(2)}, u32[]{:S(2)}) %collective-permute-start.14) | collective-permute-done | bytes 65568 | tf_op jit(solution)/shard_map/ppermute | solution.py:57
  117.0 2.3 %collective-permute-start.15 = (bf16[32,1024]{1,0:T(8,128)(2,1)S(1)}, bf16[32,1024]{1,0:T(8,128)(2,1)S(1)}, u32[]{:S(2)}, u32[]{:S(2)}) collective-permute-start(bf16[32,1024]{1,0:T(8,128)(2,1)S(1)} %collective-permute-done.14), channel_id=1, source_target_pairs={{0,2},{2,0},{1,3},{3,1},{4,6},{6,4},{5,7},{7,5},{8,10},{10,8},{9,1... | collective-permute-start | bytes 196616 | tf_op jit(solution)/shard_map/ppermute | solution.py:57
  120.8 0.7 pad_maximum_fusion
  121.5 0.8 collective-permute-done.13
  122.5 1.6 %maximum_select_fusion = bf16[2,2,512,512]{3,2,1,0:T(8,128)(2,1)} fusion(bf16[1,2,512,512]{3,2,1,0:T(8,128)(2,1)S(1)} %maximum_select_fusion.2, bf16[1,2,512,512]{3,2,1,0:T(8,128)(2,1)S(1)} %bitcast.85, pred[]{:T(512)S(6)} %eq.55), kind=kLoop, calls=%fused_computation.2 | loop fusion | flops 3145728 | bytes 4194305 | tf_op jit(solution)/shard_map/jit(_where)/select_n | solution.py:287
  (63 shorter events, 7.1 us)
Async XLA Ops:
  3.4 6.1 %collective-permute-start = (bf16[4,4,8,8,640]{4,3,2,1,0:T(8,128)(2,1)S(1)}, bf16[4,4,8,8,640]{4,3,2,1,0:T(8,128)(2,1)S(1)}, u32[]{:S(2)}, u32[]{:S(2)}) collective-permute-start(bf16[4,4,8,8,640]{4,3,2,1,0:T(8,128)(2,1)S(1)} %shard_map.212), channel_id=1, source_target_pairs={{0,2},{2,0},{1,3},{3,1},{4,6},{6,4},{5,7},{7,5},{8,10},{10,8},{9,1... | collective-permute-start | bytes 3932168 | tf_op jit(solution)/shard_map/ppermute | solution.py:57
  9.8 11.0 %collective-permute-start.1 = (bf16[4,8,8,640]{3,2,1,0:T(8,128)(2,1)S(1)}, bf16[4,8,8,640]{3,2,1,0:T(8,128)(2,1)S(1)}, u32[]{:S(2)}, u32[]{:S(2)}) collective-permute-start(bf16[4,8,8,640]{3,2,1,0:T(8,128)(2,1)S(1)} %get-tuple-element.27), channel_id=1, source_target_pairs={{0,1},{2,10},{1,4},{3,11},{4,5},{6,14},{5,0},{7,15},{8,9},{10,18},... | collective-permute-start | bytes 983048 | tf_op jit(solution)/shard_map/ppermute | solution.py:57
  9.9 10.9 %collective-permute-start.2 = (bf16[4,8,8,640]{3,2,1,0:T(8,128)(2,1)S(1)}, bf16[4,8,8,640]{3,2,1,0:T(8,128)(2,1)S(1)}, u32[]{:S(2)}, u32[]{:S(2)}) collective-permute-start(bf16[4,8,8,640]{3,2,1,0:T(8,128)(2,1)S(1)} %get-tuple-element.28), channel_id=1, source_target_pairs={{0,4},{2,18},{1,5},{3,19},{4,0},{6,22},{5,1},{7,23},{8,12},{10,26}... | collective-permute-start | bytes 983048 | tf_op jit(solution)/shard_map/ppermute | solution.py:57
  12.1 9.4 %collective-permute-start.3 = (bf16[4,8,8,640]{3,2,1,0:T(8,128)(2,1)S(1)}, bf16[4,8,8,640]{3,2,1,0:T(8,128)(2,1)S(1)}, u32[]{:S(2)}, u32[]{:S(2)}) collective-permute-start(bf16[4,8,8,640]{3,2,1,0:T(8,128)(2,1)S(1)} %get-tuple-element.29), channel_id=1, source_target_pairs={{0,5},{2,26},{1,0},{3,27},{4,1},{6,30},{5,4},{7,31},{8,13},{10,2},... | collective-permute-start | bytes 983048 | tf_op jit(solution)/shard_map/ppermute | solution.py:57
  21.6 7.5 %collective-permute-start.4 = (f32[8,8,640]{2,1,0:T(8,128)S(1)}, f32[8,8,640]{2,1,0:T(8,128)S(1)}, u32[]{:S(2)}, u32[]{:S(2)}) collective-permute-start(f32[8,8,640]{2,1,0:T(8,128)S(1)} %get-tuple-element.31), channel_id=1, source_target_pairs={{0,8},{2,3},{1,9},{3,6},{4,12},{6,7},{5,13},{7,2},{8,16},{10,11},{... | collective-permute-start | bytes 491528 | tf_op jit(solution)/shard_map/ppermute | solution.py:57
  21.7 7.4 %collective-permute-start.5 = (f32[8,8,640]{2,1,0:T(8,128)S(1)}, f32[8,8,640]{2,1,0:T(8,128)S(1)}, u32[]{:S(2)}, u32[]{:S(2)}) collective-permute-start(f32[8,8,640]{2,1,0:T(8,128)S(1)} %get-tuple-element.32), channel_id=1, source_target_pairs={{0,16},{2,6},{1,17},{3,7},{4,20},{6,2},{5,21},{7,3},{8,24},{10,14}... | collective-permute-start | bytes 491528 | tf_op jit(solution)/shard_map/ppermute | solution.py:57
  24.0 5.8 %collective-permute-start.6 = (f32[8,8,640]{2,1,0:T(8,128)S(1)}, f32[8,8,640]{2,1,0:T(8,128)S(1)}, u32[]{:S(2)}, u32[]{:S(2)}) collective-permute-start(f32[8,8,640]{2,1,0:T(8,128)S(1)} %get-tuple-element.33), channel_id=1, source_target_pairs={{0,24},{2,7},{1,25},{3,2},{4,28},{6,3},{5,29},{7,6},{8,0},{10,15},... | collective-permute-start | bytes 491528 | tf_op jit(solution)/shard_map/ppermute | solution.py:57
  29.8 3.4 %collective-permute-start.7 = (f32[4,8,640]{2,1,0:T(8,128)S(1)}, f32[4,8,640]{2,1,0:T(8,128)S(1)}, u32[]{:S(2)}, u32[]{:S(2)}) collective-permute-start(f32[4,8,640]{2,1,0:T(8,128)S(1)} %get-tuple-element.35), channel_id=1, source_target_pairs={{0,32},{2,34},{1,33},{3,35},{4,36},{6,38},{5,37},{7,39},{8,40},{10... | collective-permute-start | bytes 245768 | tf_op jit(solution)/shard_map/ppermute | solution.py:57
  33.2 3.8 %collective-permute-start.8 = (f32[2,8,640]{2,1,0:T(8,128)S(1)}, f32[2,8,640]{2,1,0:T(8,128)S(1)}, u32[]{:S(2)}, u32[]{:S(2)}) collective-permute-start(f32[2,8,640]{2,1,0:T(8,128)S(1)} %get-tuple-element.37), channel_id=1, source_target_pairs={{0,64},{2,66},{1,65},{3,67},{4,68},{6,70},{5,69},{7,71},{8,72},{10... | collective-permute-start | bytes 122888 | tf_op jit(solution)/shard_map/ppermute | solution.py:57
  37.0 6.8 %collective-permute-start.9 = (f32[1,8,640]{2,1,0:T(8,128)S(1)}, f32[1,8,640]{2,1,0:T(8,128)S(1)}, u32[]{:S(2)}, u32[]{:S(2)}) collective-permute-start(f32[1,8,640]{2,1,0:T(8,128)S(1)} %get-tuple-element.39), channel_id=1, source_target_pairs={{0,128},{2,130},{1,129},{3,131},{4,132},{6,134},{5,133},{7,135},{8... | collective-permute-start | bytes 61448 | tf_op jit(solution)/shard_map/ppermute | solution.py:57
  73.3 10.0 %collective-permute-start.10 = (f16[64,8,640]{2,1,0:T(8,128)(2,1)S(1)}, f16[64,8,640]{2,1,0:T(8,128)(2,1)S(1)}, u32[]{:S(2)}, u32[]{:S(2)}) collective-permute-start(f16[64,8,640]{2,1,0:T(8,128)(2,1)S(1)} %all_to_all.5), channel_id=1, source_target_pairs={{0,2},{2,0},{1,3},{3,1},{4,6},{6,4},{5,7},{7,5},{8,10},{10,8},{9,1... | collective-permute-start | bytes 1966088 | tf_op jit(solution)/shard_map/ppermute | solution.py:57
  83.4 2.7 %copy-start.2 = (f16[64,8,640]{2,1,0:T(8,128)(2,1)}, f16[64,8,640]{2,1,0:T(8,128)(2,1)S(1)}, u32[]{:S(2)}) copy-start(f16[64,8,640]{2,1,0:T(8,128)(2,1)S(1)} %collective-permute-done.10) | copy-start | bytes 1966084
  92.3 2.6 %collective-permute-start.11 = (f32[]{:T(128)}, f32[]{:T(128)}, u32[]{:S(2)}, u32[]{:S(2)}) collective-permute-start(f32[]{:T(128)} %add.107), channel_id=1, source_target_pairs={{0,1},{2,3},{1,0},{3,2},{4,5},{6,7},{5,4},{7,6},{8,9},{10,11},{9,8... | collective-permute-start | bytes 20 | tf_op jit(solution)/shard_map/ppermute | solution.py:57
  95.7 8.0 %copy-start.3 = (f32[64,1024]{1,0:T(8,128)S(1)}, f32[64,1024]{1,0:T(8,128)}, u32[]{:S(2)}) copy-start(f32[64,1024]{1,0:T(8,128)} %param.18) | copy-start | bytes 786436
  95.7 8.0 %copy-start.4 = (f32[64,1024]{1,0:T(8,128)S(1)}, f32[64,1024]{1,0:T(8,128)}, u32[]{:S(2)}) copy-start(f32[64,1024]{1,0:T(8,128)} %param.19) | copy-start | bytes 786436
  95.7 8.0 %copy-start.5 = (f32[64,1024]{1,0:T(8,128)S(1)}, f32[64,1024]{1,0:T(8,128)}, u32[]{:S(2)}) copy-start(f32[64,1024]{1,0:T(8,128)} %param.20) | copy-start | bytes 786436
  102.5 1.0 copy-start
  102.5 3.7 %copy-start.6 = (f32[1024]{0:T(1024)S(1)}, f32[1024]{0:T(1024)}, u32[]{:S(2)}) copy-start(f32[1024]{0:T(1024)} %param.21) | copy-start | bytes 12292
  102.5 3.7 %copy-start.7 = (f32[1024]{0:T(1024)S(1)}, f32[1024]{0:T(1024)}, u32[]{:S(2)}) copy-start(f32[1024]{0:T(1024)} %param.22) | copy-start | bytes 12292
  102.5 3.7 %copy-start.8 = (f32[1024]{0:T(1024)S(1)}, f32[1024]{0:T(1024)}, u32[]{:S(2)}) copy-start(f32[1024]{0:T(1024)} %param.23) | copy-start | bytes 12292
  103.5 16.8 %collective-permute-start.12 = (bf16[512,512]{1,0:T(8,128)(2,1)S(1)}, bf16[512,512]{1,0:T(8,128)(2,1)S(1)}, u32[]{:S(2)}, u32[]{:S(2)}) collective-permute-start(bf16[512,512]{1,0:T(8,128)(2,1)S(1)} %dynamic-slice_bitcast_fusion), channel_id=1, source_target_pairs={{0,1},{2,3},{1,0},{3,2},{4,5},{6,7},{5,4},{7,6},{8,9},{10,11},{9,8... | collective-permute-start | bytes 1572872 | tf_op jit(solution)/shard_map/ppermute | solution.py:57
  104.7 17.7 %copy-start.1 = (bf16[1024,512]{1,0:T(8,128)(2,1)S(1)}, bf16[1024,512]{1,0:T(8,128)(2,1)}, u32[]{:S(2)}) copy-start(bf16[1024,512]{1,0:T(8,128)(2,1)} %copy-done) | copy-start | bytes 3145732
  104.7 12.3 %collective-permute-start.14 = (bf16[32,1024]{1,0:T(8,128)(2,1)S(1)}, bf16[32,1024]{1,0:T(8,128)(2,1)S(1)}, u32[]{:S(2)}, u32[]{:S(2)}) collective-permute-start(bf16[32,1024]{1,0:T(8,128)(2,1)S(1)} %dynamic-slice_bitcast_fusion.1), channel_id=1, source_target_pairs={{0,1},{2,3},{1,0},{3,2},{4,5},{6,7},{5,4},{7,6},{8,9},{10,11},{9,8... | collective-permute-start | bytes 196616 | tf_op jit(solution)/shard_map/ppermute | solution.py:57
  106.8 12.6 %collective-permute-start.16 = (bf16[1024]{0:T(1024)(128)(2,1)S(1)}, bf16[1024]{0:T(1024)(128)(2,1)S(1)}, u32[]{:S(2)}, u32[]{:S(2)}) collective-permute-start(bf16[1024]{0:T(1024)(128)(2,1)S(1)} %get-tuple-element.40), channel_id=1, source_target_pairs={{0,1},{2,3},{1,0},{3,2},{4,5},{6,7},{5,4},{7,6},{8,9},{10,11},{9,8... | collective-permute-start | bytes 6152 | tf_op jit(solution)/shard_map/ppermute | solution.py:57
  117.0 3.2 %collective-permute-start.15 = (bf16[32,1024]{1,0:T(8,128)(2,1)S(1)}, bf16[32,1024]{1,0:T(8,128)(2,1)S(1)}, u32[]{:S(2)}, u32[]{:S(2)}) collective-permute-start(bf16[32,1024]{1,0:T(8,128)(2,1)S(1)} %collective-permute-done.14), channel_id=1, source_target_pairs={{0,2},{2,0},{1,3},{3,1},{4,6},{6,4},{5,7},{7,5},{8,10},{10,8},{9,1... | collective-permute-start | bytes 196616 | tf_op jit(solution)/shard_map/ppermute | solution.py:57
  120.3 2.0 %collective-permute-start.13 = (bf16[512,512]{1,0:T(8,128)(2,1)S(1)}, bf16[512,512]{1,0:T(8,128)(2,1)S(1)}, u32[]{:S(2)}, u32[]{:S(2)}) collective-permute-start(bf16[512,512]{1,0:T(8,128)(2,1)S(1)} %collective-permute-done.12), channel_id=1, source_target_pairs={{0,2},{2,0},{1,3},{3,1},{4,6},{6,4},{5,7},{7,5},{8,10},{10,8},{9,1... | collective-permute-start | bytes 1572872 | tf_op jit(solution)/shard_map/ppermute | solution.py:57

commit v4 on v3

--- a/solution.py
+++ b/solution.py
@@ -51,14 +51,15 @@
 
 SIBLING = permutation(lambda z, y, x, c: (z, y, x, 1 - c))
 PARTNER = permutation(lambda z, y, x, c: (z, y, x ^ 1, c))
+OTHER_PARTNER = permutation(lambda z, y, x, c: (z, y, x ^ 3, c))
+PARTNER_SIBLING = permutation(lambda z, y, x, c: (z, y, x ^ 1, 1 - c))
 
 
 def send(x, pairs):
     return lax.ppermute(x, ALL, pairs)
 
 
-def adamw(master, first_moment, second, gradient, factor, decay_rate):
-    scaled = factor * gradient
+def adamw(master, first_moment, second, scaled, decay_rate):
     first_new = beta_one * first_moment + (1.0 - beta_one) * scaled
     second_new = beta_two * second + (1.0 - beta_two) * scaled * scaled
     update = (
@@ -103,11 +104,11 @@
     gain = gains[...].astype(jnp.float32)
     gain = (gain[0:1] + gain[1:2]).astype(jnp.bfloat16).astype(jnp.float32)
     for half in range(2):
-        tile = jnp.zeros((8, LANES), jnp.float32)
-        for r in range(8):
-            at = half * 1024 + r * LANES
-            tile = jnp.where(row == r, gain[:, at : at + LANES], tile)
-        tiles[half] = tile
+        for z in range(8):
+            at = half * 1024 + z * LANES
+            line = gain[:, at : at + LANES]
+            turned = jnp.concatenate([line[:, 64:], line[:, :64]], axis=1)
+            tiles[half, z] = jnp.where(row == 0, line, jnp.where(row == 1, turned, 0.0))
     for i in range(16):
         half, group = group_of(t, (p + i // 4) % 4, i % 4)
         copies[2 * i].wait()
@@ -117,11 +118,10 @@
             8, 8, KEY_WIDTH
         )
         router = routers[i, 0].astype(jnp.float32) + routers[i, 1].astype(jnp.float32)
-        spare = jnp.where(group == 0, tiles[half], 0.0)
         for z in range(8):
             tile = router[:, (z // 2) * LANES : (z // 2 + 1) * LANES]
             mine = low if z % 2 == 0 else jnp.logical_not(low)
-            kept = jnp.where(row // 2 == z // 2, spare, 0.0)
+            kept = jnp.where(group == 0, tiles[half, z], 0.0)
             out_ref[i // 4, i % 4, z, :, KEY_WIDTH:] = jnp.where(mine, tile, kept).astype(
                 jnp.bfloat16
             )
@@ -138,7 +138,7 @@
             pltpu.VMEM((16, 2, 64, KEY_WIDTH), jnp.bfloat16),
             pltpu.VMEM((16, 2, 8, 512), jnp.bfloat16),
             pltpu.VMEM((2, D), jnp.bfloat16),
-            pltpu.VMEM((2, 8, LANES), jnp.float32),
+            pltpu.VMEM((2, 8, 8, LANES), jnp.float32),
             pltpu.SemaphoreType.DMA((33,)),
         ],
         compiler_params=pltpu.CompilerParams(vmem_limit_bytes=16 * 1024 * 1024),
@@ -192,26 +192,250 @@
         kept, sent = in_vmem(add_split, terms, [shape] * 2, [(z >> step) & 1])
         pairs = permutation(lambda z, y, x, c, step=step: (z ^ (1 << step), y, x, c))
         terms = [kept, send(sent, pairs)]
-    return (terms[0] + terms[1])[0]
-
-
-def spare_place(z, shape, block_axis=None):
-    row = lax.broadcasted_iota(jnp.int32, shape, len(shape) - 2)
-    lane = lax.broadcasted_iota(jnp.int32, shape, len(shape) - 1)
-    if block_axis is not None:
-        z = lax.broadcasted_iota(jnp.int32, shape, block_axis) % 8
-    return (row == (2 * (z // 2) + 2) % 8) & (lane == jnp.where(z % 2 == 0, 64, 0))
-
-
-def unpack(blocks):
-    key = blocks[:, :, :KEY_WIDTH].reshape(1024, KEY_WIDTH)
-    tiles = blocks[:, :, KEY_WIDTH:].reshape(8, 2, 4, 2, 8, LANES)
+    return terms
+
+
+def spare_lanes(parity):
+    lane = lax.broadcasted_iota(jnp.int32, (8, LANES), 1)
+    return lane // 64 + parity == 1
+
+
+def encode(where_ref, kept_ref, got_ref, out_ref):
+    own = kept_ref[0] + got_ref[0]
+    largest = jnp.max(jnp.max(jnp.abs(own), axis=1, keepdims=True), axis=0, keepdims=True)
+    largest = jnp.maximum(jnp.broadcast_to(largest, (8, LANES)), 1e-30)
+    exponent = jnp.floor(jnp.log(largest) * (1.0 / math.log(2.0))) - 13.0
+    own = own * jnp.concatenate([jnp.exp2(-exponent)] * 5, axis=1)
+    squares = jnp.sum(jnp.sum(own * own, axis=1, keepdims=True), axis=0, keepdims=True)
+    squares = jnp.broadcast_to(squares, (8, LANES)) * 2.0**-30
+    digit = squares.astype(jnp.bfloat16).astype(jnp.float32)
+    row = lax.broadcasted_iota(jnp.int32, (8, LANES), 0)
+    notes = jnp.where(row == 7, exponent, jnp.where(row == 6, digit, (squares - digit) * 256.0))
+    spare = spare_lanes(where_ref[0]) & (row >= 5)
+    out_ref[:, :KEY_WIDTH] = own[:, :KEY_WIDTH]
+    out_ref[:, KEY_WIDTH:] = jnp.where(spare, notes, own[:, KEY_WIDTH:])
+
+
+def add_squares(blocks_ref, out_ref):
+    totals = [jnp.zeros((1, LANES), jnp.float32)] * 2
+    for b in range(64):
+        tile = blocks_ref[b, :, KEY_WIDTH:]
+        digits = tile[6:7] + tile[5:6] * (1.0 / 256.0)
+        totals[b % 2] = totals[b % 2] + digits * jnp.exp2(2.0 * tile[7:8] + 30.0)
+    lane = lax.broadcasted_iota(jnp.int32, (1, LANES), 1)
+    total = jnp.where(lane == 64, totals[0], 0.0) + jnp.where(lane == 0, totals[1], 0.0)
+    out_ref[...] = jnp.broadcast_to(jnp.sum(total, axis=1, keepdims=True), (8, LANES))
+
+
+def scale_of(tile, z):
+    line = tile[7:8]
+    turned = jnp.concatenate([line[:, 64:], line[:, :64]], axis=1)
+    lane = lax.broadcasted_iota(jnp.int32, (1, LANES), 1)
+    line = jnp.where(lane < 64, turned, line) if z % 2 == 0 else jnp.where(lane < 64, line, turned)
+    return jnp.exp2(jnp.broadcast_to(line, (8, LANES)))
+
+
+def gain_line(tile, z):
+    first, second = tile[0:1], tile[1:2]
+    turned = jnp.concatenate([second[:, 64:], second[:, :64]], axis=1)
+    lane = lax.broadcasted_iota(jnp.int32, (1, LANES), 1)
+    if z % 2 == 0:
+        return jnp.where(lane < 64, turned, first)
+    return jnp.where(lane < 64, first, turned)
+
+
+def clip_factor(squares):
+    total = (squares[0][...] + squares[1][...]) + (squares[2][...] + squares[3][...])
+    clip_limit = 0.5 * math.sqrt(D * KEY_WIDTH + EXPERTS * D + D)
+    return clip_limit / jnp.maximum(jnp.sqrt(total), clip_limit)
+
+
+def update_rows(t, half, factor, blocks_ref, ins, outs, messages, keys, routers, sems):
+    key_ins, router_ins = ins[:3], ins[3:]
+    key_outs, router_outs, key_weight, router_weight = outs[:3], outs[3:6], outs[6], outs[7]
     low = lax.broadcasted_iota(jnp.int32, (8, LANES), 1) < 64
-    router = jnp.where(low, tiles[:, :, :, 0], tiles[:, :, :, 1])
-    router = router.transpose(0, 3, 1, 2, 4).reshape(EXPERTS, 1024)
-    pairs = jnp.where(low, tiles[0, 0, :, 1], tiles[0, 0, :, 0])
-    gain = jnp.concatenate([pairs[m, 2 * m : 2 * m + 2] for m in range(4)]).reshape(1024)
-    return key, router, gain
+
+    def key_rows(g, base=0):
+        return pl.ds(pl.multiple_of(base + t * 512 + g * 64, 64), 64)
+
+    router_rows = pl.ds(pl.multiple_of(t * 32, 32), 32)
+    loads = [
+        [
+            pltpu.make_async_copy(
+                key_ins[a].at[key_rows(g)], keys.at[a, pl.ds(g * 64, 64)], sems.at[g * 3 + a]
+            )
+            for a in range(3)
+        ]
+        for g in range(8)
+    ]
+    router_loads = [
+        pltpu.make_async_copy(router_ins[a].at[router_rows], routers.at[a], sems.at[24 + a])
+        for a in range(3)
+    ]
+    for copy in loads[0] + router_loads + [c for load in loads[1:] for c in load]:
+        copy.start()
+    stores = []
+
+    def store(source, target):
+        copy = pltpu.make_async_copy(source, target, sems.at[27 + len(stores)])
+        copy.start()
+        stores.append(copy)
+
+    for copy in router_loads:
+        copy.wait()
+    for g in range(8):
+        for copy in loads[g]:
+            copy.wait()
+        message, at = messages[g // 4], g % 4
+        tiles = []
+        for z in range(8):
+            tile = blocks_ref[g * 8 + z, :, KEY_WIDTH:]
+            scale = scale_of(tile, z) * factor
+            tiles.append(tile * scale)
+            scaled = blocks_ref[g * 8 + z, :, :KEY_WIDTH] * jnp.concatenate([scale] * 4, axis=1)
+            rows = pl.ds(g * 64 + z * 8, 8)
+            new = adamw(keys[0, rows], keys[1, rows], keys[2, rows], scaled, 0.1)
+            for a in range(3):
+                keys[a, rows] = new[a]
+            message[pl.ds(at * 64 + z * 8, 8)] = new[0].astype(jnp.bfloat16)
+        scaled = jnp.concatenate(
+            [jnp.where(low, tiles[2 * i], tiles[2 * i + 1]) for i in range(4)], axis=1
+        )
+        rows, columns = pl.ds(g // 2 * 8, 8), pl.ds(g % 2 * 512, 512)
+        new = adamw(
+            routers[0, rows, columns], routers[1, rows, columns], routers[2, rows, columns], scaled, 0.1
+        )
+        for a in range(3):
+            routers[a, rows, columns] = new[a]
+        message[pl.ds(256 + at * 8, 8)] = new[0].astype(jnp.bfloat16)
+        for a in range(3):
+            store(keys.at[a, pl.ds(g * 64, 64)], key_outs[a].at[key_rows(g)])
+        if at == 3:
+            write_message(t, half, g // 4, message, key_weight, router_weight, store)
+    for a in range(3):
+        store(routers.at[a], router_outs[a].at[router_rows])
+    for copy in stores:
+        copy.wait()
+
+
+def write_message(t, half, which, message, key_weight, router_weight, store):
+    rows = pl.ds(pl.multiple_of(half * 1024 + t * 512 + which * 256, 256), 256)
+    store(message.at[pl.ds(0, 256)], key_weight.at[rows])
+    for i in range(4):
+        rows = pl.ds(pl.multiple_of(t * 32 + (which * 2 + i // 2) * 8, 8), 8)
+        columns = pl.ds(pl.multiple_of(half * 1024 + i % 2 * 512, 512), 512)
+        store(message.at[pl.ds(256 + i * 8, 8)], router_weight.at[rows, columns])
+
+
+def update_first(where_ref, *refs):
+    squares, blocks_ref, ins = refs[:4], refs[4], refs[5:11]
+    outs, messages, scratch = refs[11:19], refs[19:21], refs[21:]
+    factor = clip_factor(squares)
+    update_rows(where_ref[0], where_ref[1], factor, blocks_ref, ins, outs, messages, *scratch)
+
+
+def update_second(where_ref, *refs):
+    squares, blocks_ref, first_ref, ins, gains = refs[:4], refs[4], refs[5], refs[6:12], refs[12:15]
+    outs, gain_outs, scratch = refs[23:31], refs[31:35], refs[35:]
+    messages, scratch = scratch[:2], scratch[2:]
+    factor = clip_factor(squares)
+    row = lax.broadcasted_iota(jnp.int32, (8, LANES), 0)
+    scaled = jnp.zeros((8, LANES), jnp.float32)
+    for z in range(8):
+        tile = jnp.where(
+            where_ref[0] == 0, blocks_ref[z, :, KEY_WIDTH:], first_ref[z, :, KEY_WIDTH:]
+        )
+        line = gain_line(tile * (scale_of(tile, z) * factor), z)
+        scaled = jnp.where(row == z, line, scaled)
+    new = adamw(*[gain[...] for gain in gains], scaled, 0.0)
+    for a in range(3):
+        gain_outs[a][...] = new[a]
+    gain_outs[3][...] = new[0].astype(jnp.bfloat16)
+    update_rows(where_ref[0], where_ref[1], factor, blocks_ref, ins, outs, messages, *scratch)
+
+
+def write_received(where_ref, far0, far1, near0, near1, gain_ref, gain_far_ref, *refs):
+    key_weight, router_weight, gain_out, sems = refs[2:]
+    t, half = where_ref[0], where_ref[1]
+    stores = []
+
+    def store(source, target):
+        copy = pltpu.make_async_copy(source, target, sems.at[len(stores)])
+        copy.start()
+        stores.append(copy)
+
+    write_message(t, 1 - half, 0, far0, key_weight, router_weight, store)
+    write_message(t, 1 - half, 1, far1, key_weight, router_weight, store)
+    write_message(1 - t, 1 - half, 0, near0, key_weight, router_weight, store)
+    write_message(1 - t, 1 - half, 1, near1, key_weight, router_weight, store)
+    mine, far = gain_ref[...].astype(jnp.float32), gain_far_ref[...].astype(jnp.float32)
+    gain_out[:8] = jnp.where(half == 0, mine, far).astype(jnp.bfloat16)
+    gain_out[8:] = jnp.where(half == 0, far, mine).astype(jnp.bfloat16)
+    for copy in stores:
+        copy.wait()
+
+
+IN_VMEM = pl.BlockSpec(memory_space=pltpu.VMEM)
+IN_HBM = pl.BlockSpec(memory_space=pltpu.HBM)
+IN_SMEM = pl.BlockSpec(memory_space=pltpu.SMEM)
+MESSAGE = ((288, KEY_WIDTH), jnp.bfloat16)
+
+
+def in_hbm(arrays):
+    return [pltpu.with_memory_space_constraint(a, pltpu.HBM) for a in arrays]
+
+
+def updated(core, half, squares, parts, other, states, gains):
+    shapes = [jax.ShapeDtypeStruct(a.shape, jnp.float32) for a in states]
+    shapes += [
+        jax.ShapeDtypeStruct((D, KEY_WIDTH), jnp.bfloat16),
+        jax.ShapeDtypeStruct((EXPERTS, D), jnp.bfloat16),
+    ]
+    scratch = [
+        pltpu.VMEM((3, 512, KEY_WIDTH), jnp.float32),
+        pltpu.VMEM((3, 32, 1024), jnp.float32),
+        pltpu.SemaphoreType.DMA((64,)),
+    ]
+    params = pltpu.CompilerParams(vmem_limit_bytes=24 * 1024 * 1024)
+    cost = pl.CostEstimate(flops=7_000_000, bytes_accessed=8_000_000, transcendentals=600_000)
+    states = in_hbm(states)
+    *outs, sent0, sent1 = pl.pallas_call(
+        update_first,
+        in_specs=[IN_SMEM] + [IN_VMEM] * 5 + [IN_HBM] * 6,
+        out_specs=[IN_HBM] * 8 + [IN_VMEM] * 2,
+        out_shape=shapes + [jax.ShapeDtypeStruct(*MESSAGE)] * 2,
+        scratch_shapes=scratch,
+        compiler_params=params,
+        cost_estimate=cost,
+    )(jnp.stack([core, half]), *squares, parts, *states)
+    far = [send(sent0, PARTNER), send(sent1, OTHER_PARTNER)]
+    outs = pl.pallas_call(
+        update_second,
+        in_specs=[IN_SMEM] + [IN_VMEM] * 6 + [IN_HBM] * 6 + [IN_VMEM] * 3 + [IN_HBM] * 8,
+        out_specs=[IN_HBM] * 8 + [IN_VMEM] * 4,
+        out_shape=shapes
+        + [jax.ShapeDtypeStruct((8, LANES), jnp.float32)] * 3
+        + [jax.ShapeDtypeStruct((8, LANES), jnp.bfloat16)],
+        input_output_aliases={16 + i: i for i in range(8)},
+        scratch_shapes=[pltpu.VMEM(*MESSAGE)] * 2 + scratch,
+        compiler_params=params,
+        cost_estimate=cost,
+    )(jnp.stack([1 - core, half]), *squares, other, parts, *states, *gains, *outs)
+    outs, gain_new, gain_low = outs[:8], outs[8:11], outs[11]
+    far0, far1, gain_low = lax.optimization_barrier((*far, gain_low))
+    far = [far0, far1]
+    gain_far = send(gain_low, PARTNER)
+    near = [send(a, SIBLING) for a in far]
+    key_weight, router_weight, gain_weight = pl.pallas_call(
+        write_received,
+        in_specs=[IN_SMEM] + [IN_VMEM] * 6 + [IN_HBM] * 2,
+        out_specs=[IN_HBM] * 2 + [IN_VMEM],
+        out_shape=shapes[6:] + [jax.ShapeDtypeStruct((16, LANES), jnp.bfloat16)],
+        input_output_aliases={7: 0, 8: 1},
+        scratch_shapes=[pltpu.SemaphoreType.DMA((20,))],
+        compiler_params=pltpu.CompilerParams(vmem_limit_bytes=8 * 1024 * 1024),
+    )(jnp.stack([core, half]), *far, *near, gain_low, gain_far, *outs[6:])
+    return outs[:6], gain_new, key_weight, router_weight, gain_weight
 
 
 def on_device(
@@ -242,71 +466,30 @@
     parts = [parts[0]] + [send(parts[k], along(0, k)) for k in (1, 2, 3)]
     parts = in_vmem(add_rows, parts, [((8, 8, ROW), jnp.float32)] * 4, [second_place])
     parts = [parts[0]] + [send(parts[k], along(1, k)) for k in (1, 2, 3)]
-    own = reduce_along_z(z, parts)
-    largest = jnp.maximum(jnp.max(jnp.abs(own)), 1e-30)
-    exponent = jnp.floor(jnp.log2(largest)) - 13.0
-    tile = jnp.where(spare_place(z, (8, LANES)), exponent, own[:, KEY_WIDTH:] * jnp.exp2(-exponent))
-    code = jnp.concatenate([own[:, :KEY_WIDTH] * jnp.exp2(-exponent), tile], axis=1)
-    code = code.astype(jnp.float16)
+    terms = reduce_along_z(z, parts)
+    [code] = in_vmem(encode, terms, [((8, ROW), jnp.float32)], [z & 1])
     parts = lax.all_to_all(
-        jnp.broadcast_to(code[None], (64, 8, ROW)), ("xh", "y", "z"), 0, 0, tiled=True
+        jnp.broadcast_to(code.astype(jnp.float16)[None], (64, 8, ROW)),
+        ("xh", "y", "z"),
+        0,
+        0,
+        tiled=True,
     )
-    other = send(parts, SIBLING)
-    blocks = jnp.where(
-        core == 0, jnp.concatenate([parts, other]), jnp.concatenate([other, parts])
+    other = send(parts, SIBLING).astype(jnp.float32)
+    parts = parts.astype(jnp.float32)
+    [squares] = in_vmem(add_squares, [parts], [((8, LANES), jnp.float32)])
+    squares = [squares] + [send(squares, to) for to in (SIBLING, PARTNER, PARTNER_SIBLING)]
+    states, gains, key_weight, router_weight, gain_weight = updated(
+        core,
+        half,
+        squares,
+        parts,
+        other,
+        [key_master, key_first, key_second, router_master, router_first, router_second],
+        [gain.reshape(8, LANES) for gain in (gain_master, gain_first, gain_second)],
     )
-    blocks = blocks.astype(jnp.float32)
-    held = spare_place(None, (128, 8, LANES), 0)
-    exponents = jnp.sum(jnp.where(held, blocks[:, :, KEY_WIDTH:], 0.0), axis=(1, 2), keepdims=True)
-    blocks = blocks * jnp.exp2(exponents)
-    key_sum, router_sum, gain_sum = unpack(blocks)
-    squares = (
-        jnp.sum(key_sum * key_sum) + jnp.sum(router_sum * router_sum) + jnp.sum(gain_sum * gain_sum)
-    )
-    squares = squares + send(squares, PARTNER)
-    clip_limit = 0.5 * math.sqrt(D * KEY_WIDTH + EXPERTS * D + D)
-    factor = clip_limit / jnp.maximum(jnp.sqrt(squares), clip_limit)
-    key_new, key_first_new, key_second_new = adamw(
-        key_master, key_first, key_second, key_sum, factor, 0.1
-    )
-    router_new, router_first_new, router_second_new = adamw(
-        router_master, router_first, router_second, router_sum, factor, 0.1
-    )
-    gain_new, gain_first_new, gain_second_new = adamw(
-        gain_master, gain_first, gain_second, gain_sum, factor, 0.0
-    )
-    key_low = key_new.astype(jnp.bfloat16)
-    router_low = router_new.astype(jnp.bfloat16)
-    gain_low = gain_new.astype(jnp.bfloat16)
-
-    def exchange(low):
-        mine = lax.dynamic_index_in_dim(low, core, 0, keepdims=False)
-        far = send(mine, PARTNER)
-        near = send(far, SIBLING)
-        far = jnp.where(core == 0, jnp.stack([far, near]), jnp.stack([near, far]))
-        return jnp.where(half == 0, jnp.stack([low, far]), jnp.stack([far, low]))
-
-    key_weight = exchange(key_low.reshape(2, 512, 512)).reshape(D, KEY_WIDTH)
-    router_weight = exchange(router_low.reshape(2, 32, 1024)).reshape(2, EXPERTS, 1024)
-    router_weight = jnp.concatenate([router_weight[0], router_weight[1]], axis=1)
-    gain_far = send(gain_low, PARTNER)
-    gain_weight = jnp.where(
-        half == 0, jnp.concatenate([gain_low, gain_far]), jnp.concatenate([gain_far, gain_low])
-    )
-    return (
-        key_new,
-        key_first_new,
-        key_second_new,
-        router_new,
-        router_first_new,
-        router_second_new,
-        gain_new,
-        gain_first_new,
-        gain_second_new,
-        key_weight,
-        router_weight,
-        gain_weight,
-    )
+    gains = [gain.reshape(1024) for gain in gains]
+    return (*states, *gains, key_weight, router_weight, gain_weight.reshape(D))
 
 
 def solution(mesh):

time: 124 us -> 105 us (0.85)
  other arithmetic: 19.4 us -> 0.48 us
  Pallas kernels: 5.89 us -> 19.2 us
  waiting for transfers between devices: 33.4 us -> 22.9 us
  between operations: 4.25 us -> 0.97 us
  starting transfers between devices: 32 us -> 33.4 us
    pallas_call x0 -> x3, Pallas kernels: none -> 13 us  [the longest x1 5.67 us: updated(): pl.pallas_call(update_second, in_specs=[IN_SMEM] + [IN_VMEM] * 6 + [IN_HB...]
    ppermute x17 -> x19, waiting for transfers between devices: 33.4 us -> 22.9 us  [send(): return lax.ppermute(x, ALL, pairs)]
    convert_element_type x4 -> x3, other arithmetic: 8.81 us -> 0.18 us  [the longest x1 0.09 us: on_device(): parts = parts.astype(jnp.float32)]
    reduce_sum x4 -> x0, other arithmetic: 4.73 us -> none  [the longest x1 2.32 us: on_device(): jnp.sum(jnp.where(held, blocks[:, :, KEY_WIDTH:], 0.0), axis=(1, 2), keep...]
    select_n x6 -> x0, other arithmetic: 2.46 us -> none  [the longest x2 1.67 us: exchange(): return jnp.where(half == 0, jnp.stack([low, far]), jnp.stack([far, low]))]
    mul x2 -> x0, other arithmetic: 1.84 us -> none  [the longest x1 1.81 us: on_device(): blocks = blocks * jnp.exp2(exponents)]
    ppermute x17 -> x19, starting transfers between devices: 32 us -> 33.4 us  [send(): return lax.ppermute(x, ALL, pairs)]
  transfers between devices with their start and end apart: 17 -> 19, of which waited for: 12 -> 10; matrix products, arithmetic and copies ran while one was open for 3% -> 0% of each run, Pallas kernels for 2% -> 13%
where the time goes in v4:
time: 105 us
  starting transfers between devices  33.4 us (32%)
  blocking collectives  28 us (27%)
  waiting for transfers between devices  22.9 us (22%)
  Pallas kernels  19.2 us (18%)
    ppermute x19, starting transfers between devices, send(): return lax.ppermute(x, ALL, pairs)  33.4 us
    all_to_all x1, blocking collectives, on_device(): lax.all_to_all(jnp.broadcast_to(code.astype(jnp.float16)[None], (64, 8, R...  28 us
    ppermute x19, waiting for transfers between devices, send(): return lax.ppermute(x, ALL, pairs)  22.9 us
    pallas_call x1, Pallas kernels, updated(): pl.pallas_call(update_second, in_specs=[IN_SMEM] + [IN_VMEM] * 6 + [IN_HB...  5.67 us
    pallas_call x2, Pallas kernels, pack(): pl.pallas_call(pack_local, in_specs=[pl.BlockSpec(memory_space=pltpu.SMEM...  5.32 us
    pallas_call x1, Pallas kernels, updated(): pl.pallas_call(update_first, in_specs=[IN_SMEM] + [IN_VMEM] * 5 + [IN_HBM...  5.04 us
    pallas_call x1, Pallas kernels, updated(): pl.pallas_call(write_received, in_specs=[IN_SMEM] + [IN_VMEM] * 6 + [IN_H...  2.33 us
  transfers between devices with their start and end apart: 19, of which 10 were waited for; matrix products, arithmetic and copies ran while one was open for 0% of the time, Pallas kernels for 13%

profile of v4, /device:TPU:1, one launch (start us, length us, event | category | flops | bytes accessed | tf_op | source)
XLA Modules:
  0.0 105.2 jit_solution(16308340392779217296)
XLA Ops:
  0.7 2.7 %shard_map.212 = bf16[4,4,8,8,640]{4,3,2,1,0:T(8,128)(2,1)S(1)} custom-call(s32[2]{0:T(128)S(1)} %pad_add_fusion.1.where_ref, bf16[2,2048,512]{2,1,0:T(8,128)(2,1)} %bitcast.22, bf16[2,64,2048]{2,1,0:T(8,128)(2,1)} %bitcast.24, bf16[2,2048]{1,0:T(2,128)(2,1)} %bitcast.26), custom_call_target="tpu_custom_call" | custom-call | tf_op jit(solution)/shard_map/pallas_call | solution.py:131
  3.4 3.3 %collective-permute-start = (bf16[4,4,8,8,640]{4,3,2,1,0:T(8,128)(2,1)S(1)}, bf16[4,4,8,8,640]{4,3,2,1,0:T(8,128)(2,1)S(1)}, u32[]{:S(2)}, u32[]{:S(2)}) collective-permute-start(bf16[4,4,8,8,640]{4,3,2,1,0:T(8,128)(2,1)S(1)} %shard_map.212), channel_id=1, source_target_pairs={{0,2},{2,0},{1,3},{3,1},{4,6},{6,4},{5,7},{7,5},{8,10},{10,8},{9,1... | collective-permute-start | bytes 3932168 | tf_op jit(solution)/shard_map/ppermute | solution.py:59
  6.8 2.7 %shard_map.211.kept_ref = bf16[4,4,8,8,640]{4,3,2,1,0:T(8,128)(2,1)S(1)} custom-call(s32[2]{0:T(128)S(1)} %pad_add_fusion.where_ref, bf16[2,2048,512]{2,1,0:T(8,128)(2,1)} %bitcast.23, bf16[2,64,2048]{2,1,0:T(8,128)(2,1)} %bitcast.25, bf16[2,2048]{1,0:T(2,128)(2,1)} %bitcast.27), custom_call_target="tpu_custom_call" | custom-call | tf_op jit(solution)/shard_map/pallas_call | solution.py:131
  9.5 0.3 shard_map.213
  9.9 2.2 %collective-permute-start.2 = (bf16[4,8,8,640]{3,2,1,0:T(8,128)(2,1)S(1)}, bf16[4,8,8,640]{3,2,1,0:T(8,128)(2,1)S(1)}, u32[]{:S(2)}, u32[]{:S(2)}) collective-permute-start(bf16[4,8,8,640]{3,2,1,0:T(8,128)(2,1)S(1)} %get-tuple-element.56), channel_id=1, source_target_pairs={{0,4},{2,18},{1,5},{3,19},{4,0},{6,22},{5,1},{7,23},{8,12},{10,26}... | collective-permute-start | bytes 983048 | tf_op jit(solution)/shard_map/ppermute | solution.py:59
  12.1 1.1 %collective-permute-start.3 = (bf16[4,8,8,640]{3,2,1,0:T(8,128)(2,1)S(1)}, bf16[4,8,8,640]{3,2,1,0:T(8,128)(2,1)S(1)}, u32[]{:S(2)}, u32[]{:S(2)}) collective-permute-start(bf16[4,8,8,640]{3,2,1,0:T(8,128)(2,1)S(1)} %get-tuple-element.57), channel_id=1, source_target_pairs={{0,5},{2,26},{1,0},{3,27},{4,1},{6,30},{5,4},{7,31},{8,13},{10,2},... | collective-permute-start | bytes 983048 | tf_op jit(solution)/shard_map/ppermute | solution.py:59
  13.1 7.7 %collective-permute-done.1.refs_1_ = bf16[4,8,8,640]{3,2,1,0:T(8,128)(2,1)S(1)} collective-permute-done((bf16[4,8,8,640]{3,2,1,0:T(8,128)(2,1)S(1)}, bf16[4,8,8,640]{3,2,1,0:T(8,128)(2,1)S(1)}, u32[]{:S(2)}, u32[]{:S(2)}) %collective-permute-start.1) | collective-permute-done | bytes 327712 | tf_op jit(solution)/shard_map/ppermute | solution.py:59
  20.8 0.6 collective-permute-done.3.refs_3_
  21.7 2.2 %collective-permute-start.5 = (f32[8,8,640]{2,1,0:T(8,128)S(1)}, f32[8,8,640]{2,1,0:T(8,128)S(1)}, u32[]{:S(2)}, u32[]{:S(2)}) collective-permute-start(f32[8,8,640]{2,1,0:T(8,128)S(1)} %get-tuple-element.60), channel_id=1, source_target_pairs={{0,16},{2,6},{1,17},{3,7},{4,20},{6,2},{5,21},{7,3},{8,24},{10,14}... | collective-permute-start | bytes 491528 | tf_op jit(solution)/shard_map/ppermute | solution.py:59
  24.0 1.2 %collective-permute-start.6 = (f32[8,8,640]{2,1,0:T(8,128)S(1)}, f32[8,8,640]{2,1,0:T(8,128)S(1)}, u32[]{:S(2)}, u32[]{:S(2)}) collective-permute-start(f32[8,8,640]{2,1,0:T(8,128)S(1)} %get-tuple-element.61), channel_id=1, source_target_pairs={{0,24},{2,7},{1,25},{3,2},{4,28},{6,3},{5,29},{7,6},{8,0},{10,15},... | collective-permute-start | bytes 491528 | tf_op jit(solution)/shard_map/ppermute | solution.py:59
  25.1 4.0 %collective-permute-done.4.refs_1_ = f32[8,8,640]{2,1,0:T(8,128)S(1)} collective-permute-done((f32[8,8,640]{2,1,0:T(8,128)S(1)}, f32[8,8,640]{2,1,0:T(8,128)S(1)}, u32[]{:S(2)}, u32[]{:S(2)}) %collective-permute-start.4) | collective-permute-done | bytes 163872 | tf_op jit(solution)/shard_map/ppermute | solution.py:59
  29.1 0.6 collective-permute-done.6.refs_3_
  29.7 0.4 collective-permute-start.7
  30.2 2.9 %collective-permute-done.7.refs_1_ = f32[4,8,640]{2,1,0:T(8,128)S(1)} collective-permute-done((f32[4,8,640]{2,1,0:T(8,128)S(1)}, f32[4,8,640]{2,1,0:T(8,128)S(1)}, u32[]{:S(2)}, u32[]{:S(2)}) %collective-permute-start.7) | collective-permute-done | bytes 81952 | tf_op jit(solution)/shard_map/ppermute | solution.py:59
  33.1 2.0 %collective-permute-start.8 = (f32[2,8,640]{2,1,0:T(8,128)S(1)}, f32[2,8,640]{2,1,0:T(8,128)S(1)}, u32[]{:S(2)}, u32[]{:S(2)}) collective-permute-start(f32[2,8,640]{2,1,0:T(8,128)S(1)} %get-tuple-element.65), channel_id=1, source_target_pairs={{0,64},{2,66},{1,65},{3,67},{4,68},{6,70},{5,69},{7,71},{8,72},{10... | collective-permute-start | bytes 122888 | tf_op jit(solution)/shard_map/ppermute | solution.py:59
  35.1 1.9 %collective-permute-done.8.refs_1_ = f32[2,8,640]{2,1,0:T(8,128)S(1)} collective-permute-done((f32[2,8,640]{2,1,0:T(8,128)S(1)}, f32[2,8,640]{2,1,0:T(8,128)S(1)}, u32[]{:S(2)}, u32[]{:S(2)}) %collective-permute-start.8) | collective-permute-done | bytes 40992 | tf_op jit(solution)/shard_map/ppermute | solution.py:59
  37.0 5.6 %collective-permute-start.9 = (f32[1,8,640]{2,1,0:T(8,128)S(1)}, f32[1,8,640]{2,1,0:T(8,128)S(1)}, u32[]{:S(2)}, u32[]{:S(2)}) collective-permute-start(f32[1,8,640]{2,1,0:T(8,128)S(1)} %get-tuple-element.67), channel_id=1, source_target_pairs={{0,128},{2,130},{1,129},{3,131},{4,132},{6,134},{5,133},{7,135},{8... | collective-permute-start | bytes 61448 | tf_op jit(solution)/shard_map/ppermute | solution.py:59
  42.6 1.2 %collective-permute-done.9.got_ref = f32[1,8,640]{2,1,0:T(8,128)S(1)} collective-permute-done((f32[1,8,640]{2,1,0:T(8,128)S(1)}, f32[1,8,640]{2,1,0:T(8,128)S(1)}, u32[]{:S(2)}, u32[]{:S(2)}) %collective-permute-start.9) | collective-permute-done | bytes 20512 | tf_op jit(solution)/shard_map/ppermute | solution.py:59
  43.8 0.2 shard_map.218
  44.0 28.0 %all_to_all.5 = f16[64,8,640]{2,1,0:T(8,128)(2,1)S(1)} all-to-all(f16[64,8,640]{2,1,0:T(8,128)(2,1)S(1)} %broadcast_in_dim.2), channel_id=1, replica_groups=mesh['z'=8,'y'=4,'xh'=2,'c'=2,'xl'=2] {'xh','y','z'}, dimensions={0} | all-to-all | bytes 1310720 | tf_op jit(solution)/shard_map/all_to_all | solution.py:471
  72.1 8.3 %collective-permute-start.13 = (f16[64,8,640]{2,1,0:T(8,128)(2,1)S(1)}, f16[64,8,640]{2,1,0:T(8,128)(2,1)S(1)}, u32[]{:S(2)}, u32[]{:S(2)}) collective-permute-start(f16[64,8,640]{2,1,0:T(8,128)(2,1)S(1)} %all_to_all.5), channel_id=1, source_target_pairs={{0,2},{2,0},{1,3},{3,1},{4,6},{6,4},{5,7},{7,5},{8,10},{10,8},{9,1... | collective-permute-start | bytes 1966088 | tf_op jit(solution)/shard_map/ppermute | solution.py:59
  80.7 1.3 %collective-permute-start.11 = (f32[8,128]{1,0:T(8,128)S(1)}, f32[8,128]{1,0:T(8,128)S(1)}, u32[]{:S(2)}, u32[]{:S(2)}) collective-permute-start(f32[8,128]{1,0:T(8,128)S(1)} %shard_map.219.refs_0_), channel_id=1, source_target_pairs={{0,1},{2,3},{1,0},{3,2},{4,5},{6,7},{5,4},{7,6},{8,9},{10,11},{9,8... | collective-permute-start | bytes 12296 | tf_op jit(solution)/shard_map/ppermute | solution.py:59
  82.0 0.8 collective-permute-start.10
  82.9 0.8 collective-permute-done.12.refs_3_
  83.7 5.0 %shard_map.220 = (f32[1024,512]{1,0:T(8,128)}, f32[1024,512]{1,0:T(8,128)}, f32[1024,512]{1,0:T(8,128)}, f32[64,1024]{1,0:T(8,128)}, f32[64,1024]{1,0:T(8,128)},...) custom-call(s32[2]{0:T(128)S(1)} %pad_add_fusion.2.where_ref, ...), custom_call_target="tpu_custom_call" | custom-call | flops 7000000 | bytes 8000000 | tf_op jit(solution)/shard_map/pallas_call | solution.py:402
  88.7 0.9 collective-permute-start.14
  89.6 1.1 %collective-permute-start.15 = (bf16[288,512]{1,0:T(8,128)(2,1)S(1)}, bf16[288,512]{1,0:T(8,128)(2,1)S(1)}, u32[]{:S(2)}, u32[]{:S(2)}) collective-permute-start(bf16[288,512]{1,0:T(8,128)(2,1)S(1)} %get-tuple-element.86), channel_id=1, source_target_pairs={{0,5},{2,7},{1,4},{3,6},{4,1},{6,3},{5,0},{7,2},{8,13},{10,15},{9,... | collective-permute-start | bytes 884744 | tf_op jit(solution)/shard_map/ppermute | solution.py:59
  90.9 5.7 %shard_map.221 = (f32[1024,512]{1,0:T(8,128)}, f32[1024,512]{1,0:T(8,128)}, f32[1024,512]{1,0:T(8,128)}, f32[64,1024]{1,0:T(8,128)}, f32[64,1024]{1,0:T(8,128)},...) custom-call(s32[2]{0:T(128)S(1)} %pad_add_fusion.3.where_ref, ...), custom_call_target="tpu_custom_call", output_to_operand_aliasing={{0}: (16, {}), {1}: (17, {}), {2}: (18, {}), {3}: (19, {}),... | custom-call | flops 7000000 | bytes 8000000 | tf_op jit(solution)/shard_map/pallas_call | solution.py:412
  96.6 0.8 collective-permute-done.15.far1
  97.4 2.9 %collective-permute-start.16 = (bf16[288,512]{1,0:T(8,128)(2,1)S(1)}, bf16[288,512]{1,0:T(8,128)(2,1)S(1)}, u32[]{:S(2)}, u32[]{:S(2)}) collective-permute-start(bf16[288,512]{1,0:T(8,128)(2,1)S(1)} %collective-permute-done.14.far0), channel_id=1, source_target_pairs={{0,2},{2,0},{1,3},{3,1},{4,6},{6,4},{5,7},{7,5},{8,10},{10,8},{9,1... | collective-permute-start | bytes 884744 | tf_op jit(solution)/shard_map/ppermute | solution.py:59
  100.2 2.4 %collective-permute-done.18.gain_far_ref = bf16[8,128]{1,0:T(8,128)(2,1)S(1)} collective-permute-done((bf16[8,128]{1,0:T(8,128)(2,1)S(1)}, bf16[8,128]{1,0:T(8,128)(2,1)S(1)}, u32[]{:S(2)}, u32[]{:S(2)}) %collective-permute-start.18) | collective-permute-done | bytes 2080 | tf_op jit(solution)/shard_map/ppermute | solution.py:59
  102.7 2.3 %shard_map.222 = (bf16[2048,512]{1,0:T(8,128)(2,1)}, bf16[64,2048]{1,0:T(8,128)(2,1)}, bf16[16,128]{1,0:T(8,128)(2,1)}) custom-call(s32[2]{0:T(128)S(1)} %pad_add_fusion.2.where_ref, bf16[288,512]{1,0:T(8,128)(2,1)S(1)} %collective-permute-done.14.far0, ...), custom_call_target="tpu_custom_call", output_to_operand_aliasing={{0}: (7, {}), {1}: (8, {})} | custom-call | tf_op jit(solution)/shard_map/pallas_call | solution.py:429
  (33 shorter events, 1.2 us)
Async XLA Ops:
  3.4 6.1 %collective-permute-start = (bf16[4,4,8,8,640]{4,3,2,1,0:T(8,128)(2,1)S(1)}, bf16[4,4,8,8,640]{4,3,2,1,0:T(8,128)(2,1)S(1)}, u32[]{:S(2)}, u32[]{:S(2)}) collective-permute-start(bf16[4,4,8,8,640]{4,3,2,1,0:T(8,128)(2,1)S(1)} %shard_map.212), channel_id=1, source_target_pairs={{0,2},{2,0},{1,3},{3,1},{4,6},{6,4},{5,7},{7,5},{8,10},{10,8},{9,1... | collective-permute-start | bytes 3932168 | tf_op jit(solution)/shard_map/ppermute | solution.py:59
  9.8 11.0 %collective-permute-start.1 = (bf16[4,8,8,640]{3,2,1,0:T(8,128)(2,1)S(1)}, bf16[4,8,8,640]{3,2,1,0:T(8,128)(2,1)S(1)}, u32[]{:S(2)}, u32[]{:S(2)}) collective-permute-start(bf16[4,8,8,640]{3,2,1,0:T(8,128)(2,1)S(1)} %get-tuple-element.55), channel_id=1, source_target_pairs={{0,1},{2,10},{1,4},{3,11},{4,5},{6,14},{5,0},{7,15},{8,9},{10,18},... | collective-permute-start | bytes 983048 | tf_op jit(solution)/shard_map/ppermute | solution.py:59
  9.9 10.9 %collective-permute-start.2 = (bf16[4,8,8,640]{3,2,1,0:T(8,128)(2,1)S(1)}, bf16[4,8,8,640]{3,2,1,0:T(8,128)(2,1)S(1)}, u32[]{:S(2)}, u32[]{:S(2)}) collective-permute-start(bf16[4,8,8,640]{3,2,1,0:T(8,128)(2,1)S(1)} %get-tuple-element.56), channel_id=1, source_target_pairs={{0,4},{2,18},{1,5},{3,19},{4,0},{6,22},{5,1},{7,23},{8,12},{10,26}... | collective-permute-start | bytes 983048 | tf_op jit(solution)/shard_map/ppermute | solution.py:59
  12.1 9.4 %collective-permute-start.3 = (bf16[4,8,8,640]{3,2,1,0:T(8,128)(2,1)S(1)}, bf16[4,8,8,640]{3,2,1,0:T(8,128)(2,1)S(1)}, u32[]{:S(2)}, u32[]{:S(2)}) collective-permute-start(bf16[4,8,8,640]{3,2,1,0:T(8,128)(2,1)S(1)} %get-tuple-element.57), channel_id=1, source_target_pairs={{0,5},{2,26},{1,0},{3,27},{4,1},{6,30},{5,4},{7,31},{8,13},{10,2},... | collective-permute-start | bytes 983048 | tf_op jit(solution)/shard_map/ppermute | solution.py:59
  21.6 7.5 %collective-permute-start.4 = (f32[8,8,640]{2,1,0:T(8,128)S(1)}, f32[8,8,640]{2,1,0:T(8,128)S(1)}, u32[]{:S(2)}, u32[]{:S(2)}) collective-permute-start(f32[8,8,640]{2,1,0:T(8,128)S(1)} %get-tuple-element.59), channel_id=1, source_target_pairs={{0,8},{2,3},{1,9},{3,6},{4,12},{6,7},{5,13},{7,2},{8,16},{10,11},{... | collective-permute-start | bytes 491528 | tf_op jit(solution)/shard_map/ppermute | solution.py:59
  21.7 7.4 %collective-permute-start.5 = (f32[8,8,640]{2,1,0:T(8,128)S(1)}, f32[8,8,640]{2,1,0:T(8,128)S(1)}, u32[]{:S(2)}, u32[]{:S(2)}) collective-permute-start(f32[8,8,640]{2,1,0:T(8,128)S(1)} %get-tuple-element.60), channel_id=1, source_target_pairs={{0,16},{2,6},{1,17},{3,7},{4,20},{6,2},{5,21},{7,3},{8,24},{10,14}... | collective-permute-start | bytes 491528 | tf_op jit(solution)/shard_map/ppermute | solution.py:59
  24.0 5.8 %collective-permute-start.6 = (f32[8,8,640]{2,1,0:T(8,128)S(1)}, f32[8,8,640]{2,1,0:T(8,128)S(1)}, u32[]{:S(2)}, u32[]{:S(2)}) collective-permute-start(f32[8,8,640]{2,1,0:T(8,128)S(1)} %get-tuple-element.61), channel_id=1, source_target_pairs={{0,24},{2,7},{1,25},{3,2},{4,28},{6,3},{5,29},{7,6},{8,0},{10,15},... | collective-permute-start | bytes 491528 | tf_op jit(solution)/shard_map/ppermute | solution.py:59
  29.7 3.4 %collective-permute-start.7 = (f32[4,8,640]{2,1,0:T(8,128)S(1)}, f32[4,8,640]{2,1,0:T(8,128)S(1)}, u32[]{:S(2)}, u32[]{:S(2)}) collective-permute-start(f32[4,8,640]{2,1,0:T(8,128)S(1)} %get-tuple-element.63), channel_id=1, source_target_pairs={{0,32},{2,34},{1,33},{3,35},{4,36},{6,38},{5,37},{7,39},{8,40},{10... | collective-permute-start | bytes 245768 | tf_op jit(solution)/shard_map/ppermute | solution.py:59
  33.1 3.8 %collective-permute-start.8 = (f32[2,8,640]{2,1,0:T(8,128)S(1)}, f32[2,8,640]{2,1,0:T(8,128)S(1)}, u32[]{:S(2)}, u32[]{:S(2)}) collective-permute-start(f32[2,8,640]{2,1,0:T(8,128)S(1)} %get-tuple-element.65), channel_id=1, source_target_pairs={{0,64},{2,66},{1,65},{3,67},{4,68},{6,70},{5,69},{7,71},{8,72},{10... | collective-permute-start | bytes 122888 | tf_op jit(solution)/shard_map/ppermute | solution.py:59
  37.0 6.8 %collective-permute-start.9 = (f32[1,8,640]{2,1,0:T(8,128)S(1)}, f32[1,8,640]{2,1,0:T(8,128)S(1)}, u32[]{:S(2)}, u32[]{:S(2)}) collective-permute-start(f32[1,8,640]{2,1,0:T(8,128)S(1)} %get-tuple-element.67), channel_id=1, source_target_pairs={{0,128},{2,130},{1,129},{3,131},{4,132},{6,134},{5,133},{7,135},{8... | collective-permute-start | bytes 61448 | tf_op jit(solution)/shard_map/ppermute | solution.py:59
  72.1 18.7 %collective-permute-start.13 = (f16[64,8,640]{2,1,0:T(8,128)(2,1)S(1)}, f16[64,8,640]{2,1,0:T(8,128)(2,1)S(1)}, u32[]{:S(2)}, u32[]{:S(2)}) collective-permute-start(f16[64,8,640]{2,1,0:T(8,128)(2,1)S(1)} %all_to_all.5), channel_id=1, source_target_pairs={{0,2},{2,0},{1,3},{3,1},{4,6},{6,4},{5,7},{7,5},{8,10},{10,8},{9,1... | collective-permute-start | bytes 1966088 | tf_op jit(solution)/shard_map/ppermute | solution.py:59
  80.6 3.1 %collective-permute-start.12 = (f32[8,128]{1,0:T(8,128)S(1)}, f32[8,128]{1,0:T(8,128)S(1)}, u32[]{:S(2)}, u32[]{:S(2)}) collective-permute-start(f32[8,128]{1,0:T(8,128)S(1)} %shard_map.219.refs_0_), channel_id=1, source_target_pairs={{0,3},{2,1},{1,2},{3,0},{4,7},{6,5},{5,6},{7,4},{8,11},{10,9},{9,1... | collective-permute-start | bytes 12296 | tf_op jit(solution)/shard_map/ppermute | solution.py:59
  80.7 3.0 %collective-permute-start.11 = (f32[8,128]{1,0:T(8,128)S(1)}, f32[8,128]{1,0:T(8,128)S(1)}, u32[]{:S(2)}, u32[]{:S(2)}) collective-permute-start(f32[8,128]{1,0:T(8,128)S(1)} %shard_map.219.refs_0_), channel_id=1, source_target_pairs={{0,1},{2,3},{1,0},{3,2},{4,5},{6,7},{5,4},{7,6},{8,9},{10,11},{9,8... | collective-permute-start | bytes 12296 | tf_op jit(solution)/shard_map/ppermute | solution.py:59
  82.0 1.7 %collective-permute-start.10 = (f32[8,128]{1,0:T(8,128)S(1)}, f32[8,128]{1,0:T(8,128)S(1)}, u32[]{:S(2)}, u32[]{:S(2)}) collective-permute-start(f32[8,128]{1,0:T(8,128)S(1)} %shard_map.219.refs_0_), channel_id=1, source_target_pairs={{0,2},{2,0},{1,3},{3,1},{4,6},{6,4},{5,7},{7,5},{8,10},{10,8},{9,1... | collective-permute-start | bytes 12296 | tf_op jit(solution)/shard_map/ppermute | solution.py:59
  82.9 8.0 %copy-start = (f32[1024]{0:T(1024)S(1)}, f32[1024]{0:T(1024)}, u32[]{:S(2)}) copy-start(f32[1024]{0:T(1024)} %param.21) | copy-start | bytes 12292
  82.9 8.0 %copy-start.1 = (f32[1024]{0:T(1024)S(1)}, f32[1024]{0:T(1024)}, u32[]{:S(2)}) copy-start(f32[1024]{0:T(1024)} %param.22) | copy-start | bytes 12292
  82.9 8.0 %copy-start.2 = (f32[1024]{0:T(1024)S(1)}, f32[1024]{0:T(1024)}, u32[]{:S(2)}) copy-start(f32[1024]{0:T(1024)} %param.23) | copy-start | bytes 12292
  88.7 7.9 %collective-permute-start.14 = (bf16[288,512]{1,0:T(8,128)(2,1)S(1)}, bf16[288,512]{1,0:T(8,128)(2,1)S(1)}, u32[]{:S(2)}, u32[]{:S(2)}) collective-permute-start(bf16[288,512]{1,0:T(8,128)(2,1)S(1)} %get-tuple-element.85), channel_id=1, source_target_pairs={{0,1},{2,3},{1,0},{3,2},{4,5},{6,7},{5,4},{7,6},{8,9},{10,11},{9,8... | collective-permute-start | bytes 884744 | tf_op jit(solution)/shard_map/ppermute | solution.py:59
  89.6 7.8 %collective-permute-start.15 = (bf16[288,512]{1,0:T(8,128)(2,1)S(1)}, bf16[288,512]{1,0:T(8,128)(2,1)S(1)}, u32[]{:S(2)}, u32[]{:S(2)}) collective-permute-start(bf16[288,512]{1,0:T(8,128)(2,1)S(1)} %get-tuple-element.86), channel_id=1, source_target_pairs={{0,5},{2,7},{1,4},{3,6},{4,1},{6,3},{5,0},{7,2},{8,13},{10,15},{9,... | collective-permute-start | bytes 884744 | tf_op jit(solution)/shard_map/ppermute | solution.py:59
  97.4 5.3 %collective-permute-start.16 = (bf16[288,512]{1,0:T(8,128)(2,1)S(1)}, bf16[288,512]{1,0:T(8,128)(2,1)S(1)}, u32[]{:S(2)}, u32[]{:S(2)}) collective-permute-start(bf16[288,512]{1,0:T(8,128)(2,1)S(1)} %collective-permute-done.14.far0), channel_id=1, source_target_pairs={{0,2},{2,0},{1,3},{3,1},{4,6},{6,4},{5,7},{7,5},{8,10},{10,8},{9,1... | collective-permute-start | bytes 884744 | tf_op jit(solution)/shard_map/ppermute | solution.py:59
  100.2 2.4 %collective-permute-start.17 = (bf16[288,512]{1,0:T(8,128)(2,1)S(1)}, bf16[288,512]{1,0:T(8,128)(2,1)S(1)}, u32[]{:S(2)}, u32[]{:S(2)}) collective-permute-start(bf16[288,512]{1,0:T(8,128)(2,1)S(1)} %collective-permute-done.15.far1), channel_id=1, source_target_pairs={{0,2},{2,0},{1,3},{3,1},{4,6},{6,4},{5,7},{7,5},{8,10},{10,8},{9,1... | collective-permute-start | bytes 884744 | tf_op jit(solution)/shard_map/ppermute | solution.py:59
  100.2 2.4 %collective-permute-start.18 = (bf16[8,128]{1,0:T(8,128)(2,1)S(1)}, bf16[8,128]{1,0:T(8,128)(2,1)S(1)}, u32[]{:S(2)}, u32[]{:S(2)}) collective-permute-start(bf16[8,128]{1,0:T(8,128)(2,1)S(1)} %get-tuple-element.90.gain_ref), channel_id=1, source_target_pairs={{0,1},{2,3},{1,0},{3,2},{4,5},{6,7},{5,4},{7,6},{8,9},{10,11},{9,8... | collective-permute-start | bytes 6152 | tf_op jit(solution)/shard_map/ppermute | solution.py:59

commit v5 on v4

--- a/solution.py
+++ b/solution.py
@@ -40,15 +40,20 @@
     ]
 
 
-def along(stage, shift):
+def along(shift):
     def target(z, y, x, c):
-        if c == stage:
+        if c == 0:
             return z, y, (x + shift) % 4, c
         return z, (y + shift) % 4, x, c
 
     return permutation(target)
 
 
+SECOND_GROUPS = [
+    [place(z, q, p, c) if c == 0 else place(z, p, q, c) for q in range(4) for z in range(8)]
+    for c in range(2)
+    for p in range(4)
+]
 SIBLING = permutation(lambda z, y, x, c: (z, y, x, 1 - c))
 PARTNER = permutation(lambda z, y, x, c: (z, y, x ^ 1, c))
 OTHER_PARTNER = permutation(lambda z, y, x, c: (z, y, x ^ 3, c))
@@ -141,7 +146,7 @@
             pltpu.VMEM((2, 8, 8, LANES), jnp.float32),
             pltpu.SemaphoreType.DMA((33,)),
         ],
-        compiler_params=pltpu.CompilerParams(vmem_limit_bytes=16 * 1024 * 1024),
+        compiler_params=pltpu.CompilerParams(vmem_limit_bytes=4 * 1024 * 1024),
     )(jnp.stack([t, p]), *[pltpu.with_memory_space_constraint(g, pltpu.HBM) for g in grads])
 
 
@@ -153,7 +158,7 @@
         + [pl.BlockSpec(memory_space=pltpu.VMEM)] * len(operands),
         out_specs=[pl.BlockSpec(memory_space=pltpu.VMEM)] * len(shapes),
         out_shape=[jax.ShapeDtypeStruct(*shape) for shape in shapes],
-        compiler_params=pltpu.CompilerParams(vmem_limit_bytes=8 * 1024 * 1024),
+        compiler_params=pltpu.CompilerParams(vmem_limit_bytes=2 * 1024 * 1024),
     )(*scalars, *operands)
 
 
@@ -164,54 +169,57 @@
             outs[k][q] = total.astype(jnp.bfloat16)
 
 
-def add_rows(where_ref, *refs):
-    terms, outs = refs[:4], refs[4:]
-    for k in range(4):
-        at = (where_ref[0] + k) % 4
-        total = terms[0][at].astype(jnp.float32)
-        for term in terms[1:]:
-            total = total + term[at].astype(jnp.float32)
-        outs[k][...] = total
-
-
-def add_split(where_ref, *refs):
-    terms, (kept_ref, sent_ref) = refs[:-2], refs[-2:]
-    bit = where_ref[0]
-    for i in range(kept_ref.shape[0]):
-        for out_ref, b in ((kept_ref, bit), (sent_ref, 1 - bit)):
-            at = 2 * i + b
-            total = terms[0][at]
-            for term in terms[1:]:
-                total = total + term[at]
-            out_ref[i] = total
-
-
-def reduce_along_z(z, terms):
-    for step in range(3):
-        shape = ((4 >> step, 8, ROW), jnp.float32)
-        kept, sent = in_vmem(add_split, terms, [shape] * 2, [(z >> step) & 1])
-        pairs = permutation(lambda z, y, x, c, step=step: (z ^ (1 << step), y, x, c))
-        terms = [kept, send(sent, pairs)]
-    return terms
-
-
 def spare_lanes(parity):
     lane = lax.broadcasted_iota(jnp.int32, (8, LANES), 1)
     return lane // 64 + parity == 1
 
 
-def encode(where_ref, kept_ref, got_ref, out_ref):
-    own = kept_ref[0] + got_ref[0]
-    largest = jnp.max(jnp.max(jnp.abs(own), axis=1, keepdims=True), axis=0, keepdims=True)
+def exponent_of(largest):
     largest = jnp.maximum(jnp.broadcast_to(largest, (8, LANES)), 1e-30)
-    exponent = jnp.floor(jnp.log(largest) * (1.0 / math.log(2.0))) - 13.0
+    return jnp.floor(jnp.log(largest) * (1.0 / math.log(2.0))) - 13.0
+
+
+def largest_of(x):
+    return jnp.max(jnp.max(jnp.abs(x), axis=1, keepdims=True), axis=0, keepdims=True)
+
+
+def sum_encoded(where_ref, *refs):
+    terms, out_ref = refs[:4], refs[4]
+    largest = jnp.zeros((8, ROW), jnp.float32)
+    for q in range(4):
+        for z in range(8):
+            total = terms[0][q, z].astype(jnp.float32)
+            for term in terms[1:]:
+                total = total + term[q, z].astype(jnp.float32)
+            out_ref[q * 8 + z] = total
+            largest = jnp.maximum(largest, jnp.abs(total))
+    exponent = exponent_of(largest_of(largest))
+    scale = jnp.concatenate([jnp.exp2(-exponent)] * 5, axis=1)
+    row = lax.broadcasted_iota(jnp.int32, (8, LANES), 0)
+    for b in range(32):
+        own = out_ref[b] * scale
+        spare = spare_lanes(b % 2) & (row == 7)
+        out_ref[b, :, :KEY_WIDTH] = own[:, :KEY_WIDTH]
+        out_ref[b, :, KEY_WIDTH:] = jnp.where(spare, exponent, own[:, KEY_WIDTH:])
+
+
+def encode(where_ref, blocks_ref, out_ref):
+    parity = where_ref[0]
+    row = lax.broadcasted_iota(jnp.int32, (8, LANES), 0)
+    own = jnp.zeros((8, ROW), jnp.float32)
+    for b in range(32):
+        block = blocks_ref[b]
+        scale = scale_of(block[:, KEY_WIDTH:], parity)
+        own = own + block * jnp.concatenate([scale] * 5, axis=1)
+    spare = spare_lanes(parity) & (row >= 5)
+    key, tile = own[:, :KEY_WIDTH], jnp.where(spare, 0.0, own[:, KEY_WIDTH:])
+    own = jnp.concatenate([key, tile], axis=1)
+    exponent = exponent_of(largest_of(own))
     own = own * jnp.concatenate([jnp.exp2(-exponent)] * 5, axis=1)
     squares = jnp.sum(jnp.sum(own * own, axis=1, keepdims=True), axis=0, keepdims=True)
     squares = jnp.broadcast_to(squares, (8, LANES)) * 2.0**-30
     digit = squares.astype(jnp.bfloat16).astype(jnp.float32)
-    row = lax.broadcasted_iota(jnp.int32, (8, LANES), 0)
     notes = jnp.where(row == 7, exponent, jnp.where(row == 6, digit, (squares - digit) * 256.0))
-    spare = spare_lanes(where_ref[0]) & (row >= 5)
     out_ref[:, :KEY_WIDTH] = own[:, :KEY_WIDTH]
     out_ref[:, KEY_WIDTH:] = jnp.where(spare, notes, own[:, KEY_WIDTH:])
 
@@ -227,11 +235,11 @@
     out_ref[...] = jnp.broadcast_to(jnp.sum(total, axis=1, keepdims=True), (8, LANES))
 
 
-def scale_of(tile, z):
+def scale_of(tile, parity):
     line = tile[7:8]
     turned = jnp.concatenate([line[:, 64:], line[:, :64]], axis=1)
     lane = lax.broadcasted_iota(jnp.int32, (1, LANES), 1)
-    line = jnp.where(lane < 64, turned, line) if z % 2 == 0 else jnp.where(lane < 64, line, turned)
+    line = jnp.where(lane // 64 + parity == 1, line, turned)
     return jnp.exp2(jnp.broadcast_to(line, (8, LANES)))
 
 
@@ -250,51 +258,45 @@
     return clip_limit / jnp.maximum(jnp.sqrt(total), clip_limit)
 
 
-def update_rows(t, half, factor, blocks_ref, ins, outs, messages, keys, routers, sems):
-    key_ins, router_ins = ins[:3], ins[3:]
+def update_rows(where_ref, squares, blocks_ref, ins, outs, messages, keys, routers, sems):
+    t, half = where_ref[0], where_ref[1]
+    factor = clip_factor(squares)
+    key_ins, router_ins, gain_ins = ins[:3], ins[3:6], ins[6:]
     key_outs, router_outs, key_weight, router_weight = outs[:3], outs[3:6], outs[6], outs[7]
+    gain_outs = outs[8:]
     low = lax.broadcasted_iota(jnp.int32, (8, LANES), 1) < 64
 
     def key_rows(g, base=0):
         return pl.ds(pl.multiple_of(base + t * 512 + g * 64, 64), 64)
 
     router_rows = pl.ds(pl.multiple_of(t * 32, 32), 32)
-    loads = [
-        [
-            pltpu.make_async_copy(
-                key_ins[a].at[key_rows(g)], keys.at[a, pl.ds(g * 64, 64)], sems.at[g * 3 + a]
-            )
-            for a in range(3)
-        ]
-        for g in range(8)
-    ]
-    router_loads = [
-        pltpu.make_async_copy(router_ins[a].at[router_rows], routers.at[a], sems.at[24 + a])
-        for a in range(3)
-    ]
-    for copy in loads[0] + router_loads + [c for load in loads[1:] for c in load]:
-        copy.start()
     stores = []
 
     def store(source, target):
-        copy = pltpu.make_async_copy(source, target, sems.at[27 + len(stores)])
+        copy = pltpu.make_async_copy(source, target, sems.at[len(stores)])
         copy.start()
         stores.append(copy)
 
-    for copy in router_loads:
-        copy.wait()
+    row = lax.broadcasted_iota(jnp.int32, (8, LANES), 0)
+    scaled = jnp.zeros((8, LANES), jnp.float32)
+    for z in range(8):
+        tile = blocks_ref[z, :, KEY_WIDTH:]
+        scaled = jnp.where(row == z, gain_line(tile * (scale_of(tile, z % 2) * factor), z), scaled)
+    new = adamw(*[gain[...] for gain in gain_ins], scaled, 0.0)
+    for a in range(3):
+        gain_outs[a][...] = new[a]
+    messages[0][pl.ds(288, 8), :LANES] = new[0].astype(jnp.bfloat16)
     for g in range(8):
-        for copy in loads[g]:
-            copy.wait()
         message, at = messages[g // 4], g % 4
         tiles = []
         for z in range(8):
             tile = blocks_ref[g * 8 + z, :, KEY_WIDTH:]
-            scale = scale_of(tile, z) * factor
+            scale = scale_of(tile, z % 2) * factor
             tiles.append(tile * scale)
             scaled = blocks_ref[g * 8 + z, :, :KEY_WIDTH] * jnp.concatenate([scale] * 4, axis=1)
             rows = pl.ds(g * 64 + z * 8, 8)
-            new = adamw(keys[0, rows], keys[1, rows], keys[2, rows], scaled, 0.1)
+            old = pl.ds(pl.multiple_of(t * 512 + g * 64 + z * 8, 8), 8)
+            new = adamw(*[key[old] for key in key_ins], scaled, 0.1)
             for a in range(3):
                 keys[a, rows] = new[a]
             message[pl.ds(at * 64 + z * 8, 8)] = new[0].astype(jnp.bfloat16)
@@ -302,9 +304,8 @@
             [jnp.where(low, tiles[2 * i], tiles[2 * i + 1]) for i in range(4)], axis=1
         )
         rows, columns = pl.ds(g // 2 * 8, 8), pl.ds(g % 2 * 512, 512)
-        new = adamw(
-            routers[0, rows, columns], routers[1, rows, columns], routers[2, rows, columns], scaled, 0.1
-        )
+        old = pl.ds(pl.multiple_of(t * 32 + g // 2 * 8, 8), 8)
+        new = adamw(*[router[old, columns] for router in router_ins], scaled, 0.1)
         for a in range(3):
             routers[a, rows, columns] = new[a]
         message[pl.ds(256 + at * 8, 8)] = new[0].astype(jnp.bfloat16)
@@ -328,34 +329,20 @@
 
 
 def update_first(where_ref, *refs):
-    squares, blocks_ref, ins = refs[:4], refs[4], refs[5:11]
-    outs, messages, scratch = refs[11:19], refs[19:21], refs[21:]
-    factor = clip_factor(squares)
-    update_rows(where_ref[0], where_ref[1], factor, blocks_ref, ins, outs, messages, *scratch)
+    squares, blocks_ref, ins = refs[:4], refs[4], refs[5:14]
+    outs, messages, scratch = refs[14:25], refs[25:27], refs[27:]
+    update_rows(where_ref, squares, blocks_ref, ins, outs, messages, *scratch)
 
 
 def update_second(where_ref, *refs):
-    squares, blocks_ref, first_ref, ins, gains = refs[:4], refs[4], refs[5], refs[6:12], refs[12:15]
-    outs, gain_outs, scratch = refs[23:31], refs[31:35], refs[35:]
-    messages, scratch = scratch[:2], scratch[2:]
-    factor = clip_factor(squares)
-    row = lax.broadcasted_iota(jnp.int32, (8, LANES), 0)
-    scaled = jnp.zeros((8, LANES), jnp.float32)
-    for z in range(8):
-        tile = jnp.where(
-            where_ref[0] == 0, blocks_ref[z, :, KEY_WIDTH:], first_ref[z, :, KEY_WIDTH:]
-        )
-        line = gain_line(tile * (scale_of(tile, z) * factor), z)
-        scaled = jnp.where(row == z, line, scaled)
-    new = adamw(*[gain[...] for gain in gains], scaled, 0.0)
-    for a in range(3):
-        gain_outs[a][...] = new[a]
-    gain_outs[3][...] = new[0].astype(jnp.bfloat16)
-    update_rows(where_ref[0], where_ref[1], factor, blocks_ref, ins, outs, messages, *scratch)
-
-
-def write_received(where_ref, far0, far1, near0, near1, gain_ref, gain_far_ref, *refs):
-    key_weight, router_weight, gain_out, sems = refs[2:]
+    squares, blocks_ref, ins = refs[:4], refs[4], refs[5:14]
+    outs, scratch = refs[22:33], refs[33:]
+    update_rows(where_ref, squares, blocks_ref, ins, outs, scratch[:2], *scratch[2:])
+
+
+def write_received(where_ref, far0, far1, near0, near1, *refs):
+    first_gains, second_gains = refs[:3], refs[3:6]
+    key_weight, router_weight, gain_outs, gain_weight, sems = *refs[8:10], refs[10:13], *refs[13:]
     t, half = where_ref[0], where_ref[1]
     stores = []
 
@@ -368,9 +355,13 @@
     write_message(t, 1 - half, 1, far1, key_weight, router_weight, store)
     write_message(1 - t, 1 - half, 0, near0, key_weight, router_weight, store)
     write_message(1 - t, 1 - half, 1, near1, key_weight, router_weight, store)
-    mine, far = gain_ref[...].astype(jnp.float32), gain_far_ref[...].astype(jnp.float32)
-    gain_out[:8] = jnp.where(half == 0, mine, far).astype(jnp.bfloat16)
-    gain_out[8:] = jnp.where(half == 0, far, mine).astype(jnp.bfloat16)
+    for a in range(3):
+        gain_outs[a][...] = jnp.where(t == 0, first_gains[a][...], second_gains[a][...])
+    rows = pl.ds(288, 8)
+    far, near = far0[rows, :LANES].astype(jnp.float32), near0[rows, :LANES].astype(jnp.float32)
+    far, mine = jnp.where(t == 0, far, near), gain_outs[0][...]
+    gain_weight[:8] = jnp.where(half == 0, mine, far).astype(jnp.bfloat16)
+    gain_weight[8:] = jnp.where(half == 0, far, mine).astype(jnp.bfloat16)
     for copy in stores:
         copy.wait()
 
@@ -378,7 +369,7 @@
 IN_VMEM = pl.BlockSpec(memory_space=pltpu.VMEM)
 IN_HBM = pl.BlockSpec(memory_space=pltpu.HBM)
 IN_SMEM = pl.BlockSpec(memory_space=pltpu.SMEM)
-MESSAGE = ((288, KEY_WIDTH), jnp.bfloat16)
+MESSAGES = [((296, KEY_WIDTH), jnp.bfloat16), ((288, KEY_WIDTH), jnp.bfloat16)]
 
 
 def in_hbm(arrays):
@@ -391,51 +382,49 @@
         jax.ShapeDtypeStruct((D, KEY_WIDTH), jnp.bfloat16),
         jax.ShapeDtypeStruct((EXPERTS, D), jnp.bfloat16),
     ]
+    gain_shapes = [jax.ShapeDtypeStruct((8, LANES), jnp.float32)] * 3
     scratch = [
         pltpu.VMEM((3, 512, KEY_WIDTH), jnp.float32),
         pltpu.VMEM((3, 32, 1024), jnp.float32),
-        pltpu.SemaphoreType.DMA((64,)),
+        pltpu.SemaphoreType.DMA((37,)),
     ]
-    params = pltpu.CompilerParams(vmem_limit_bytes=24 * 1024 * 1024)
+    params = pltpu.CompilerParams(vmem_limit_bytes=6 * 1024 * 1024)
     cost = pl.CostEstimate(flops=7_000_000, bytes_accessed=8_000_000, transcendentals=600_000)
-    states = in_hbm(states)
-    *outs, sent0, sent1 = pl.pallas_call(
+    outs = pl.pallas_call(
         update_first,
-        in_specs=[IN_SMEM] + [IN_VMEM] * 5 + [IN_HBM] * 6,
-        out_specs=[IN_HBM] * 8 + [IN_VMEM] * 2,
-        out_shape=shapes + [jax.ShapeDtypeStruct(*MESSAGE)] * 2,
+        in_specs=[IN_SMEM] + [IN_VMEM] * 14,
+        out_specs=[IN_HBM] * 8 + [IN_VMEM] * 5,
+        out_shape=shapes + gain_shapes + [jax.ShapeDtypeStruct(*m) for m in MESSAGES],
         scratch_shapes=scratch,
         compiler_params=params,
         cost_estimate=cost,
-    )(jnp.stack([core, half]), *squares, parts, *states)
-    far = [send(sent0, PARTNER), send(sent1, OTHER_PARTNER)]
+    )(jnp.stack([core, half]), *squares, parts, *states, *gains)
+    outs, first_gains, sent = outs[:8], outs[8:11], outs[11:]
+    far = [send(sent[0], PARTNER), send(sent[1], OTHER_PARTNER)]
     outs = pl.pallas_call(
         update_second,
-        in_specs=[IN_SMEM] + [IN_VMEM] * 6 + [IN_HBM] * 6 + [IN_VMEM] * 3 + [IN_HBM] * 8,
-        out_specs=[IN_HBM] * 8 + [IN_VMEM] * 4,
-        out_shape=shapes
-        + [jax.ShapeDtypeStruct((8, LANES), jnp.float32)] * 3
-        + [jax.ShapeDtypeStruct((8, LANES), jnp.bfloat16)],
-        input_output_aliases={16 + i: i for i in range(8)},
-        scratch_shapes=[pltpu.VMEM(*MESSAGE)] * 2 + scratch,
+        in_specs=[IN_SMEM] + [IN_VMEM] * 14 + [IN_HBM] * 8,
+        out_specs=[IN_HBM] * 8 + [IN_VMEM] * 3,
+        out_shape=shapes + gain_shapes,
+        input_output_aliases={15 + i: i for i in range(8)},
+        scratch_shapes=[pltpu.VMEM(*m) for m in MESSAGES] + scratch,
         compiler_params=params,
         cost_estimate=cost,
-    )(jnp.stack([1 - core, half]), *squares, other, parts, *states, *gains, *outs)
-    outs, gain_new, gain_low = outs[:8], outs[8:11], outs[11]
-    far0, far1, gain_low = lax.optimization_barrier((*far, gain_low))
-    far = [far0, far1]
-    gain_far = send(gain_low, PARTNER)
+    )(jnp.stack([1 - core, half]), *squares, other, *states, *gains, *outs)
+    outs, second_gains = outs[:8], outs[8:]
+    far0, far1, gain_new = lax.optimization_barrier((*far, second_gains[0]))
+    far, second_gains = [far0, far1], [gain_new, *second_gains[1:]]
     near = [send(a, SIBLING) for a in far]
-    key_weight, router_weight, gain_weight = pl.pallas_call(
+    key_weight, router_weight, *gains, gain_weight = pl.pallas_call(
         write_received,
-        in_specs=[IN_SMEM] + [IN_VMEM] * 6 + [IN_HBM] * 2,
-        out_specs=[IN_HBM] * 2 + [IN_VMEM],
-        out_shape=shapes[6:] + [jax.ShapeDtypeStruct((16, LANES), jnp.bfloat16)],
-        input_output_aliases={7: 0, 8: 1},
+        in_specs=[IN_SMEM] + [IN_VMEM] * 10 + [IN_HBM] * 2,
+        out_specs=[IN_HBM] * 2 + [IN_VMEM] * 4,
+        out_shape=shapes[6:] + gain_shapes + [jax.ShapeDtypeStruct((16, LANES), jnp.bfloat16)],
+        input_output_aliases={11: 0, 12: 1},
         scratch_shapes=[pltpu.SemaphoreType.DMA((20,))],
-        compiler_params=pltpu.CompilerParams(vmem_limit_bytes=8 * 1024 * 1024),
-    )(jnp.stack([core, half]), *far, *near, gain_low, gain_far, *outs[6:])
-    return outs[:6], gain_new, key_weight, router_weight, gain_weight
+        compiler_params=pltpu.CompilerParams(vmem_limit_bytes=2 * 1024 * 1024),
+    )(jnp.stack([core, half]), *far, *near, *first_gains, *second_gains, *outs[6:])
+    return outs[:6], gains, key_weight, router_weight, gain_weight
 
 
 def on_device(
@@ -463,11 +452,13 @@
     got = send(pack(1 - core, second_place, grads), SIBLING)
     kept = pack(core, first_place, grads)
     parts = in_vmem(add_pair, [kept, got], [((4, 8, 8, ROW), jnp.bfloat16)] * 4)
-    parts = [parts[0]] + [send(parts[k], along(0, k)) for k in (1, 2, 3)]
-    parts = in_vmem(add_rows, parts, [((8, 8, ROW), jnp.float32)] * 4, [second_place])
-    parts = [parts[0]] + [send(parts[k], along(1, k)) for k in (1, 2, 3)]
-    terms = reduce_along_z(z, parts)
-    [code] = in_vmem(encode, terms, [((8, ROW), jnp.float32)], [z & 1])
+    states = [key_master, key_first, key_second, router_master, router_first, router_second]
+    parts = [parts[0]] + [send(parts[k], along(k)) for k in (1, 2, 3)]
+    [code] = in_vmem(sum_encoded, parts, [((32, 8, ROW), jnp.float32)], [z])
+    code = lax.all_to_all(
+        code.astype(jnp.float16), ALL, 0, 0, axis_index_groups=SECOND_GROUPS, tiled=True
+    )
+    [code] = in_vmem(encode, [code.astype(jnp.float32)], [((8, ROW), jnp.float32)], [z & 1])
     parts = lax.all_to_all(
         jnp.broadcast_to(code.astype(jnp.float16)[None], (64, 8, ROW)),
         ("xh", "y", "z"),
@@ -485,7 +476,7 @@
         squares,
         parts,
         other,
-        [key_master, key_first, key_second, router_master, router_first, router_second],
+        states,
         [gain.reshape(8, LANES) for gain in (gain_master, gain_first, gain_second)],
     )
     gains = [gain.reshape(1024) for gain in gains]

time: 105 us -> 99.1 us (0.944)
  starting transfers between devices: 33.4 us -> 29.1 us
  Pallas kernels: 19.2 us -> 16 us
    ppermute x19 -> x12, starting transfers between devices: 33.4 us -> 19.3 us  [send(): return lax.ppermute(x, ALL, pairs)]
    all_to_all x0 -> x1, waiting for transfers between devices: none -> 9.93 us  [on_device(): lax.all_to_all(code.astype(jnp.float16), ALL, 0, 0, axis_index_groups=SEC...]
    all_to_all x0 -> x1, starting transfers between devices: none -> 9.76 us  [on_device(): lax.all_to_all(code.astype(jnp.float16), ALL, 0, 0, axis_index_groups=SEC...]
    ppermute x19 -> x12, waiting for transfers between devices: 22.9 us -> 13.4 us  [send(): return lax.ppermute(x, ALL, pairs)]
    pallas_call x3, Pallas kernels: 13 us -> 9.57 us  [the longest x1 3.62 us: updated(): pl.pallas_call(update_second, in_specs=[IN_SMEM] + [IN_VMEM] * 14 + [IN_H...]
  transfers between devices with their start and end apart: 19 -> 13, of which waited for: 10 -> 6; matrix products, arithmetic and copies ran while one was open for 0% -> 0% of each run, Pallas kernels for 13% -> 10%
where the time goes in v5:
time: 99.1 us; the launch traced here: 98.8 us
  starting transfers between devices  29.1 us (29%)
  blocking collectives  27.8 us (28%)
  waiting for transfers between devices  23.3 us (24%)
  Pallas kernels  16 us (16%)
  other arithmetic  1.29 us (1%)
  between operations  1.07 us (1%)
    all_to_all x1, blocking collectives, on_device(): lax.all_to_all(jnp.broadcast_to(code.astype(jnp.float16)[None], (64, 8, R...  27.8 us
    ppermute x12, starting transfers between devices, send(): return lax.ppermute(x, ALL, pairs)  19.3 us
    ppermute x12, waiting for transfers between devices, send(): return lax.ppermute(x, ALL, pairs)  13.4 us
    all_to_all x1, waiting for transfers between devices, on_device(): lax.all_to_all(code.astype(jnp.float16), ALL, 0, 0, axis_index_groups=SEC...  9.93 us
    all_to_all x1, starting transfers between devices, on_device(): lax.all_to_all(code.astype(jnp.float16), ALL, 0, 0, axis_index_groups=SEC...  9.76 us
    pallas_call x2, Pallas kernels, pack(): pl.pallas_call(pack_local, in_specs=[pl.BlockSpec(memory_space=pltpu.SMEM...  5.32 us
    pallas_call x1, Pallas kernels, updated(): pl.pallas_call(update_second, in_specs=[IN_SMEM] + [IN_VMEM] * 14 + [IN_H...  3.62 us
    pallas_call x1, Pallas kernels, updated(): pl.pallas_call(update_first, in_specs=[IN_SMEM] + [IN_VMEM] * 14, out_spe...  3.61 us
  transfers between devices with their start and end apart: 13, of which 6 were waited for; matrix products, arithmetic and copies ran while one was open for 0% of the time, Pallas kernels for 10%

profile of v5, /device:TPU:1, one launch (start us, length us, event | category | flops | bytes accessed | tf_op | source)
XLA Modules:
  0.0 98.8 jit_solution(13798594911600885756)
XLA Ops:
  0.7 0.1 pad_add_fusion.1.where_ref
  0.7 2.7 %shard_map.212 = bf16[4,4,8,8,640]{4,3,2,1,0:T(8,128)(2,1)S(1)} custom-call(s32[2]{0:T(128)S(1)} %pad_add_fusion.1.where_ref, bf16[2,2048,512]{2,1,0:T(8,128)(2,1)} %bitcast.23, bf16[2,64,2048]{2,1,0:T(8,128)(2,1)} %bitcast.25, bf16[2,2048]{1,0:T(2,128)(2,1)} %bitcast.27), custom_call_target="tpu_custom_call" | custom-call | tf_op jit(solution)/shard_map/pallas_call | solution.py:136
  3.4 3.3 %collective-permute-start = (bf16[4,4,8,8,640]{4,3,2,1,0:T(8,128)(2,1)S(1)}, bf16[4,4,8,8,640]{4,3,2,1,0:T(8,128)(2,1)S(1)}, u32[]{:S(2)}, u32[]{:S(2)}) collective-permute-start(bf16[4,4,8,8,640]{4,3,2,1,0:T(8,128)(2,1)S(1)} %shard_map.212), channel_id=1, source_target_pairs={{0,2},{2,0},{1,3},{3,1},{4,6},{6,4},{5,7},{7,5},{8,10},{10,8},{9,1... | collective-permute-start | bytes 3932168 | tf_op jit(solution)/shard_map/ppermute | solution.py:64
  6.7 0.1 pad_add_fusion.where_ref
  6.8 2.7 %shard_map.211.kept_ref = bf16[4,4,8,8,640]{4,3,2,1,0:T(8,128)(2,1)S(1)} custom-call(s32[2]{0:T(128)S(1)} %pad_add_fusion.where_ref, bf16[2,2048,512]{2,1,0:T(8,128)(2,1)} %bitcast.24, bf16[2,64,2048]{2,1,0:T(8,128)(2,1)} %bitcast.26, bf16[2,2048]{1,0:T(2,128)(2,1)} %bitcast.28), custom_call_target="tpu_custom_call" | custom-call | tf_op jit(solution)/shard_map/pallas_call | solution.py:136
  9.5 0.3 shard_map.213
  9.8 0.1 collective-permute-start.1
  9.9 2.2 %collective-permute-start.2 = (bf16[4,8,8,640]{3,2,1,0:T(8,128)(2,1)S(1)}, bf16[4,8,8,640]{3,2,1,0:T(8,128)(2,1)S(1)}, u32[]{:S(2)}, u32[]{:S(2)}) collective-permute-start(bf16[4,8,8,640]{3,2,1,0:T(8,128)(2,1)S(1)} %get-tuple-element.51), channel_id=1, source_target_pairs={{0,4},{2,18},{1,5},{3,19},{4,0},{6,22},{5,1},{7,23},{8,12},{10,26}... | collective-permute-start | bytes 983048 | tf_op jit(solution)/shard_map/ppermute | solution.py:64
  12.1 1.1 %collective-permute-start.3 = (bf16[4,8,8,640]{3,2,1,0:T(8,128)(2,1)S(1)}, bf16[4,8,8,640]{3,2,1,0:T(8,128)(2,1)S(1)}, u32[]{:S(2)}, u32[]{:S(2)}) collective-permute-start(bf16[4,8,8,640]{3,2,1,0:T(8,128)(2,1)S(1)} %get-tuple-element.52), channel_id=1, source_target_pairs={{0,5},{2,26},{1,0},{3,27},{4,1},{6,30},{5,4},{7,31},{8,13},{10,2},... | collective-permute-start | bytes 983048 | tf_op jit(solution)/shard_map/ppermute | solution.py:64
  13.1 7.7 %collective-permute-done.1.refs_1_ = bf16[4,8,8,640]{3,2,1,0:T(8,128)(2,1)S(1)} collective-permute-done((bf16[4,8,8,640]{3,2,1,0:T(8,128)(2,1)S(1)}, bf16[4,8,8,640]{3,2,1,0:T(8,128)(2,1)S(1)}, u32[]{:S(2)}, u32[]{:S(2)}) %collective-permute-start.1) | collective-permute-done | bytes 327712 | tf_op jit(solution)/shard_map/ppermute | solution.py:64
  20.8 0.6 collective-permute-done.3.refs_3_
  21.4 0.3 shard_map.214
  21.8 0.8 convert_element_type.15
  22.6 9.8 %all-to-all-start = ((f16[32,8,640]{2,1,0:T(8,128)(2,1)}), f16[32,8,640]{2,1,0:T(8,128)(2,1)S(1)}, u32[]{:S(2)}, u32[]{:S(2)}) async-start(f16[32,8,640]{2,1,0:T(8,128)(2,1)} %convert_element_type.15), calls=%async_computation | async-start | bytes 655360 | tf_op jit(solution)/shard_map/all_to_all | solution.py:458
  32.3 9.9 %all-to-all-done = f16[32,8,640]{2,1,0:T(8,128)(2,1)S(1)} async-done(((f16[32,8,640]{2,1,0:T(8,128)(2,1)}), f16[32,8,640]{2,1,0:T(8,128)(2,1)S(1)}, u32[]{:S(2)}, u32[]{:S(2)}) %all-to-all-start) | async-done | bytes 327712 | tf_op jit(solution)/shard_map/all_to_all | solution.py:458
  42.3 0.3 shard_map.215
  42.8 27.8 %all_to_all.10 = f16[64,8,640]{2,1,0:T(8,128)(2,1)S(1)} all-to-all(f16[64,8,640]{2,1,0:T(8,128)(2,1)S(1)} %broadcast_in_dim.2), channel_id=1, replica_groups=mesh['z'=8,'y'=4,'xh'=2,'c'=2,'xl'=2] {'xh','y','z'}, dimensions={0} | all-to-all | bytes 1310720 | tf_op jit(solution)/shard_map/all_to_all | solution.py:462
  70.6 5.5 %collective-permute-start.7 = (f16[64,8,640]{2,1,0:T(8,128)(2,1)S(1)}, f16[64,8,640]{2,1,0:T(8,128)(2,1)S(1)}, u32[]{:S(2)}, u32[]{:S(2)}) collective-permute-start(f16[64,8,640]{2,1,0:T(8,128)(2,1)S(1)} %all_to_all.10), channel_id=1, source_target_pairs={{0,2},{2,0},{1,3},{3,1},{4,6},{6,4},{5,7},{7,5},{8,10},{10,8},{9,1... | collective-permute-start | bytes 1966088 | tf_op jit(solution)/shard_map/ppermute | solution.py:64
  76.1 0.1 convert_element_type.18.blocks_ref.refs_4_
  76.2 0.2 shard_map.216.refs_0_
  76.4 1.3 %collective-permute-start.5 = (f32[8,128]{1,0:T(8,128)S(1)}, f32[8,128]{1,0:T(8,128)S(1)}, u32[]{:S(2)}, u32[]{:S(2)}) collective-permute-start(f32[8,128]{1,0:T(8,128)S(1)} %shard_map.216.refs_0_), channel_id=1, source_target_pairs={{0,1},{2,3},{1,0},{3,2},{4,5},{6,7},{5,4},{7,6},{8,9},{10,11},{9,8... | collective-permute-start | bytes 12296 | tf_op jit(solution)/shard_map/ppermute | solution.py:64
  77.7 0.8 collective-permute-start.4
  78.6 0.8 collective-permute-done.6.refs_3_
  79.5 3.6 %shard_map.217 = (f32[1024,512]{1,0:T(8,128)}, f32[1024,512]{1,0:T(8,128)}, f32[1024,512]{1,0:T(8,128)}, f32[64,1024]{1,0:T(8,128)}, f32[64,1024]{1,0:T(8,128)},...) custom-call(s32[2]{0:T(128)S(1)} %pad_add_fusion.2.where_ref, ...), custom_call_target="tpu_custom_call" | custom-call | flops 7000000 | bytes 8000000 | tf_op jit(solution)/shard_map/pallas_call | solution.py:393
  83.1 0.9 collective-permute-start.8
  84.0 1.4 %collective-permute-start.9 = (bf16[288,512]{1,0:T(8,128)(2,1)S(1)}, bf16[288,512]{1,0:T(8,128)(2,1)S(1)}, u32[]{:S(2)}, u32[]{:S(2)}) collective-permute-start(bf16[288,512]{1,0:T(8,128)(2,1)S(1)} %get-tuple-element.68), channel_id=1, source_target_pairs={{0,5},{2,7},{1,4},{3,6},{4,1},{6,3},{5,0},{7,2},{8,13},{10,15},{9,... | collective-permute-start | bytes 884744 | tf_op jit(solution)/shard_map/ppermute | solution.py:64
  85.4 0.1 convert_element_type.19.refs_4_
  85.5 3.6 %shard_map.218 = (f32[1024,512]{1,0:T(8,128)}, f32[1024,512]{1,0:T(8,128)}, f32[1024,512]{1,0:T(8,128)}, f32[64,1024]{1,0:T(8,128)}, f32[64,1024]{1,0:T(8,128)},...) custom-call(s32[2]{0:T(128)S(1)} %pad_add_fusion.3.where_ref, ...), custom_call_target="tpu_custom_call", output_to_operand_aliasing={{0}: (15, {}), {1}: (16, {}), {2}: (17, {}), {3}: (18, {}),... | custom-call | flops 7000000 | bytes 8000000 | tf_op jit(solution)/shard_map/pallas_call | solution.py:404
  89.1 2.6 %collective-permute-done.9.far1 = bf16[288,512]{1,0:T(8,128)(2,1)S(1)} collective-permute-done((bf16[288,512]{1,0:T(8,128)(2,1)S(1)}, bf16[288,512]{1,0:T(8,128)(2,1)S(1)}, u32[]{:S(2)}, u32[]{:S(2)}) %collective-permute-start.9) | collective-permute-done | bytes 294944 | tf_op jit(solution)/shard_map/ppermute | solution.py:64
  91.8 2.9 %collective-permute-start.10 = (bf16[296,512]{1,0:T(8,128)(2,1)S(1)}, bf16[296,512]{1,0:T(8,128)(2,1)S(1)}, u32[]{:S(2)}, u32[]{:S(2)}) collective-permute-start(bf16[296,512]{1,0:T(8,128)(2,1)S(1)} %collective-permute-done.8.far0), channel_id=1, source_target_pairs={{0,2},{2,0},{1,3},{3,1},{4,6},{6,4},{5,7},{7,5},{8,10},{10,8},{9,1... | collective-permute-start | bytes 909320 | tf_op jit(solution)/shard_map/ppermute | solution.py:64
  94.6 1.6 %collective-permute-done.11.near1 = bf16[288,512]{1,0:T(8,128)(2,1)S(1)} collective-permute-done((bf16[288,512]{1,0:T(8,128)(2,1)S(1)}, bf16[288,512]{1,0:T(8,128)(2,1)S(1)}, u32[]{:S(2)}, u32[]{:S(2)}) %collective-permute-start.11) | collective-permute-done | bytes 294944 | tf_op jit(solution)/shard_map/ppermute | solution.py:64
  96.3 2.3 %shard_map.219 = (bf16[2048,512]{1,0:T(8,128)(2,1)}, bf16[64,2048]{1,0:T(8,128)(2,1)}, f32[8,128]{1,0:T(8,128)}, f32[8,128]{1,0:T(8,128)}, f32[8,128]{1,0:T(8,128)}, /*index=5*/bf16[16,128]{1,0:T(8,128)(2,1)}) custom-call(s32[2]{0:T(128)S(1)} %pad_add_fusion.2.where_ref, ...), custom_call_target="tpu_custom_call", output_to_operand_aliasing={{0}: (11, {}), {1}: (12, {})} | custom-call | tf_op jit(solution)/shard_map/pallas_call | solution.py:418
  (32 shorter events, 0.4 us)
Async XLA Ops:
  3.4 6.1 %collective-permute-start = (bf16[4,4,8,8,640]{4,3,2,1,0:T(8,128)(2,1)S(1)}, bf16[4,4,8,8,640]{4,3,2,1,0:T(8,128)(2,1)S(1)}, u32[]{:S(2)}, u32[]{:S(2)}) collective-permute-start(bf16[4,4,8,8,640]{4,3,2,1,0:T(8,128)(2,1)S(1)} %shard_map.212), channel_id=1, source_target_pairs={{0,2},{2,0},{1,3},{3,1},{4,6},{6,4},{5,7},{7,5},{8,10},{10,8},{9,1... | collective-permute-start | bytes 3932168 | tf_op jit(solution)/shard_map/ppermute | solution.py:64
  9.8 11.0 %collective-permute-start.1 = (bf16[4,8,8,640]{3,2,1,0:T(8,128)(2,1)S(1)}, bf16[4,8,8,640]{3,2,1,0:T(8,128)(2,1)S(1)}, u32[]{:S(2)}, u32[]{:S(2)}) collective-permute-start(bf16[4,8,8,640]{3,2,1,0:T(8,128)(2,1)S(1)} %get-tuple-element.50), channel_id=1, source_target_pairs={{0,1},{2,10},{1,4},{3,11},{4,5},{6,14},{5,0},{7,15},{8,9},{10,18},... | collective-permute-start | bytes 983048 | tf_op jit(solution)/shard_map/ppermute | solution.py:64
  9.9 10.9 %collective-permute-start.2 = (bf16[4,8,8,640]{3,2,1,0:T(8,128)(2,1)S(1)}, bf16[4,8,8,640]{3,2,1,0:T(8,128)(2,1)S(1)}, u32[]{:S(2)}, u32[]{:S(2)}) collective-permute-start(bf16[4,8,8,640]{3,2,1,0:T(8,128)(2,1)S(1)} %get-tuple-element.51), channel_id=1, source_target_pairs={{0,4},{2,18},{1,5},{3,19},{4,0},{6,22},{5,1},{7,23},{8,12},{10,26}... | collective-permute-start | bytes 983048 | tf_op jit(solution)/shard_map/ppermute | solution.py:64
  12.1 9.4 %collective-permute-start.3 = (bf16[4,8,8,640]{3,2,1,0:T(8,128)(2,1)S(1)}, bf16[4,8,8,640]{3,2,1,0:T(8,128)(2,1)S(1)}, u32[]{:S(2)}, u32[]{:S(2)}) collective-permute-start(bf16[4,8,8,640]{3,2,1,0:T(8,128)(2,1)S(1)} %get-tuple-element.52), channel_id=1, source_target_pairs={{0,5},{2,26},{1,0},{3,27},{4,1},{6,30},{5,4},{7,31},{8,13},{10,2},... | collective-permute-start | bytes 983048 | tf_op jit(solution)/shard_map/ppermute | solution.py:64
  22.6 56.9 %copy-start.5 = (f32[64,1024]{1,0:T(8,128)S(1)}, f32[64,1024]{1,0:T(8,128)}, u32[]{:S(2)}) copy-start(f32[64,1024]{1,0:T(8,128)} %refs_10_.3) | copy-start | bytes 786436
  22.6 19.7 %all-to-all-start = ((f16[32,8,640]{2,1,0:T(8,128)(2,1)}), f16[32,8,640]{2,1,0:T(8,128)(2,1)S(1)}, u32[]{:S(2)}, u32[]{:S(2)}) async-start(f16[32,8,640]{2,1,0:T(8,128)(2,1)} %convert_element_type.15), calls=%async_computation | async-start | bytes 655360 | tf_op jit(solution)/shard_map/all_to_all | solution.py:458
  42.3 37.2 %copy-start.2 = (f32[1024,512]{1,0:T(8,128)S(1)}, f32[1024,512]{1,0:T(8,128)}, u32[]{:S(2)}) copy-start(f32[1024,512]{1,0:T(8,128)} %refs_7_.3) | copy-start | bytes 6291460
  42.7 36.8 %copy-start.4 = (f32[64,1024]{1,0:T(8,128)S(1)}, f32[64,1024]{1,0:T(8,128)}, u32[]{:S(2)}) copy-start(f32[64,1024]{1,0:T(8,128)} %refs_9_.3) | copy-start | bytes 786436
  42.7 36.7 %copy-start = (f32[1024,512]{1,0:T(8,128)S(1)}, f32[1024,512]{1,0:T(8,128)}, u32[]{:S(2)}) copy-start(f32[1024,512]{1,0:T(8,128)} %refs_5_.3) | copy-start | bytes 6291460
  42.7 36.7 %copy-start.1 = (f32[1024,512]{1,0:T(8,128)S(1)}, f32[1024,512]{1,0:T(8,128)}, u32[]{:S(2)}) copy-start(f32[1024,512]{1,0:T(8,128)} %refs_6_.3) | copy-start | bytes 6291460
  42.8 36.7 %copy-start.3 = (f32[64,1024]{1,0:T(8,128)S(1)}, f32[64,1024]{1,0:T(8,128)}, u32[]{:S(2)}) copy-start(f32[64,1024]{1,0:T(8,128)} %refs_8_.3) | copy-start | bytes 786436
  42.8 36.7 %copy-start.6 = (f32[1024]{0:T(1024)S(1)}, f32[1024]{0:T(1024)}, u32[]{:S(2)}) copy-start(f32[1024]{0:T(1024)} %param.21) | copy-start | bytes 12292
  42.8 36.7 %copy-start.7 = (f32[1024]{0:T(1024)S(1)}, f32[1024]{0:T(1024)}, u32[]{:S(2)}) copy-start(f32[1024]{0:T(1024)} %param.22) | copy-start | bytes 12292
  42.8 36.7 %copy-start.8 = (f32[1024]{0:T(1024)S(1)}, f32[1024]{0:T(1024)}, u32[]{:S(2)}) copy-start(f32[1024]{0:T(1024)} %param.23) | copy-start | bytes 12292
  70.6 14.8 %collective-permute-start.7 = (f16[64,8,640]{2,1,0:T(8,128)(2,1)S(1)}, f16[64,8,640]{2,1,0:T(8,128)(2,1)S(1)}, u32[]{:S(2)}, u32[]{:S(2)}) collective-permute-start(f16[64,8,640]{2,1,0:T(8,128)(2,1)S(1)} %all_to_all.10), channel_id=1, source_target_pairs={{0,2},{2,0},{1,3},{3,1},{4,6},{6,4},{5,7},{7,5},{8,10},{10,8},{9,1... | collective-permute-start | bytes 1966088 | tf_op jit(solution)/shard_map/ppermute | solution.py:64
  76.4 3.1 %collective-permute-start.6 = (f32[8,128]{1,0:T(8,128)S(1)}, f32[8,128]{1,0:T(8,128)S(1)}, u32[]{:S(2)}, u32[]{:S(2)}) collective-permute-start(f32[8,128]{1,0:T(8,128)S(1)} %shard_map.216.refs_0_), channel_id=1, source_target_pairs={{0,3},{2,1},{1,2},{3,0},{4,7},{6,5},{5,6},{7,4},{8,11},{10,9},{9,1... | collective-permute-start | bytes 12296 | tf_op jit(solution)/shard_map/ppermute | solution.py:64
  76.4 3.0 %collective-permute-start.5 = (f32[8,128]{1,0:T(8,128)S(1)}, f32[8,128]{1,0:T(8,128)S(1)}, u32[]{:S(2)}, u32[]{:S(2)}) collective-permute-start(f32[8,128]{1,0:T(8,128)S(1)} %shard_map.216.refs_0_), channel_id=1, source_target_pairs={{0,1},{2,3},{1,0},{3,2},{4,5},{6,7},{5,4},{7,6},{8,9},{10,11},{9,8... | collective-permute-start | bytes 12296 | tf_op jit(solution)/shard_map/ppermute | solution.py:64
  77.7 1.7 %collective-permute-start.4 = (f32[8,128]{1,0:T(8,128)S(1)}, f32[8,128]{1,0:T(8,128)S(1)}, u32[]{:S(2)}, u32[]{:S(2)}) collective-permute-start(f32[8,128]{1,0:T(8,128)S(1)} %shard_map.216.refs_0_), channel_id=1, source_target_pairs={{0,2},{2,0},{1,3},{3,1},{4,6},{6,4},{5,7},{7,5},{8,10},{10,8},{9,1... | collective-permute-start | bytes 12296 | tf_op jit(solution)/shard_map/ppermute | solution.py:64
  83.1 8.6 %collective-permute-start.8 = (bf16[296,512]{1,0:T(8,128)(2,1)S(1)}, bf16[296,512]{1,0:T(8,128)(2,1)S(1)}, u32[]{:S(2)}, u32[]{:S(2)}) collective-permute-start(bf16[296,512]{1,0:T(8,128)(2,1)S(1)} %get-tuple-element.67), channel_id=1, source_target_pairs={{0,1},{2,3},{1,0},{3,2},{4,5},{6,7},{5,4},{7,6},{8,9},{10,11},{9,8... | collective-permute-start | bytes 909320 | tf_op jit(solution)/shard_map/ppermute | solution.py:64
  84.0 7.8 %collective-permute-start.9 = (bf16[288,512]{1,0:T(8,128)(2,1)S(1)}, bf16[288,512]{1,0:T(8,128)(2,1)S(1)}, u32[]{:S(2)}, u32[]{:S(2)}) collective-permute-start(bf16[288,512]{1,0:T(8,128)(2,1)S(1)} %get-tuple-element.68), channel_id=1, source_target_pairs={{0,5},{2,7},{1,4},{3,6},{4,1},{6,3},{5,0},{7,2},{8,13},{10,15},{9,... | collective-permute-start | bytes 884744 | tf_op jit(solution)/shard_map/ppermute | solution.py:64
  91.8 4.5 %collective-permute-start.10 = (bf16[296,512]{1,0:T(8,128)(2,1)S(1)}, bf16[296,512]{1,0:T(8,128)(2,1)S(1)}, u32[]{:S(2)}, u32[]{:S(2)}) collective-permute-start(bf16[296,512]{1,0:T(8,128)(2,1)S(1)} %collective-permute-done.8.far0), channel_id=1, source_target_pairs={{0,2},{2,0},{1,3},{3,1},{4,6},{6,4},{5,7},{7,5},{8,10},{10,8},{9,1... | collective-permute-start | bytes 909320 | tf_op jit(solution)/shard_map/ppermute | solution.py:64
  94.6 1.6 %collective-permute-start.11 = (bf16[288,512]{1,0:T(8,128)(2,1)S(1)}, bf16[288,512]{1,0:T(8,128)(2,1)S(1)}, u32[]{:S(2)}, u32[]{:S(2)}) collective-permute-start(bf16[288,512]{1,0:T(8,128)(2,1)S(1)} %collective-permute-done.9.far1), channel_id=1, source_target_pairs={{0,2},{2,0},{1,3},{3,1},{4,6},{6,4},{5,7},{7,5},{8,10},{10,8},{9,1... | collective-permute-start | bytes 884744 | tf_op jit(solution)/shard_map/ppermute | solution.py:64

commit v6 on v5

--- a/solution.py
+++ b/solution.py
@@ -67,10 +67,9 @@
 def adamw(master, first_moment, second, scaled, decay_rate):
     first_new = beta_one * first_moment + (1.0 - beta_one) * scaled
     second_new = beta_two * second + (1.0 - beta_two) * scaled * scaled
-    update = (
-        first_new / bias_one / (jnp.sqrt(second_new / bias_two) + epsilon) + decay_rate * master
-    )
-    master_new = master - step_rate * update
+    root = jnp.sqrt(second_new * (1.0 / bias_two)) + epsilon
+    kept = master if decay_rate == 0.0 else master * (1.0 - step_rate * decay_rate)
+    master_new = kept - first_new * (step_rate / bias_one) / root
     return (master_new, first_new, second_new)
 
 
@@ -340,10 +339,7 @@
     update_rows(where_ref, squares, blocks_ref, ins, outs, scratch[:2], *scratch[2:])
 
 
-def write_received(where_ref, far0, far1, near0, near1, *refs):
-    first_gains, second_gains = refs[:3], refs[3:6]
-    key_weight, router_weight, gain_outs, gain_weight, sems = *refs[8:10], refs[10:13], *refs[13:]
-    t, half = where_ref[0], where_ref[1]
+def write_two(t, half, messages, key_weight, router_weight, sems):
     stores = []
 
     def store(source, target):
@@ -351,15 +347,30 @@
         copy.start()
         stores.append(copy)
 
-    write_message(t, 1 - half, 0, far0, key_weight, router_weight, store)
-    write_message(t, 1 - half, 1, far1, key_weight, router_weight, store)
-    write_message(1 - t, 1 - half, 0, near0, key_weight, router_weight, store)
-    write_message(1 - t, 1 - half, 1, near1, key_weight, router_weight, store)
+    for i in range(2):
+        write_message(t, 1 - half, i, messages[i], key_weight, router_weight, store)
+    return stores
+
+
+def write_far(where_ref, far0, far1, *refs):
+    first_gains, second_gains = refs[:3], refs[3:6]
+    key_weight, router_weight, gain_outs, sems = *refs[8:10], refs[10:13], refs[13]
+    stores = write_two(where_ref[0], where_ref[1], (far0, far1), key_weight, router_weight, sems)
     for a in range(3):
-        gain_outs[a][...] = jnp.where(t == 0, first_gains[a][...], second_gains[a][...])
+        first, second = first_gains[a][...], second_gains[a][...]
+        gain_outs[a][...] = jnp.where(where_ref[0] == 0, first, second)
+    for copy in stores:
+        copy.wait()
+
+
+def write_near(where_ref, near0, near1, far0, first_gain, second_gain, *refs):
+    key_weight, router_weight, gain_weight, sems = refs[2:]
+    t, half = where_ref[0], where_ref[1]
+    stores = write_two(1 - t, half, (near0, near1), key_weight, router_weight, sems)
     rows = pl.ds(288, 8)
     far, near = far0[rows, :LANES].astype(jnp.float32), near0[rows, :LANES].astype(jnp.float32)
-    far, mine = jnp.where(t == 0, far, near), gain_outs[0][...]
+    far = jnp.where(t == 0, far, near)
+    mine = jnp.where(t == 0, first_gain[...], second_gain[...])
     gain_weight[:8] = jnp.where(half == 0, mine, far).astype(jnp.bfloat16)
     gain_weight[8:] = jnp.where(half == 0, far, mine).astype(jnp.bfloat16)
     for copy in stores:
@@ -415,15 +426,29 @@
     far0, far1, gain_new = lax.optimization_barrier((*far, second_gains[0]))
     far, second_gains = [far0, far1], [gain_new, *second_gains[1:]]
     near = [send(a, SIBLING) for a in far]
-    key_weight, router_weight, *gains, gain_weight = pl.pallas_call(
-        write_received,
-        in_specs=[IN_SMEM] + [IN_VMEM] * 10 + [IN_HBM] * 2,
-        out_specs=[IN_HBM] * 2 + [IN_VMEM] * 4,
-        out_shape=shapes[6:] + gain_shapes + [jax.ShapeDtypeStruct((16, LANES), jnp.bfloat16)],
-        input_output_aliases={11: 0, 12: 1},
-        scratch_shapes=[pltpu.SemaphoreType.DMA((20,))],
-        compiler_params=pltpu.CompilerParams(vmem_limit_bytes=2 * 1024 * 1024),
-    )(jnp.stack([core, half]), *far, *near, *first_gains, *second_gains, *outs[6:])
+    where = jnp.stack([core, half])
+    sems = [pltpu.SemaphoreType.DMA((10,))]
+    params = pltpu.CompilerParams(vmem_limit_bytes=2 * 1024 * 1024)
+    *weights, gain0, gain1, gain2 = pl.pallas_call(
+        write_far,
+        in_specs=[IN_SMEM] + [IN_VMEM] * 8 + [IN_HBM] * 2,
+        out_specs=[IN_HBM] * 2 + [IN_VMEM] * 3,
+        out_shape=shapes[6:] + gain_shapes,
+        input_output_aliases={9: 0, 10: 1},
+        scratch_shapes=sems,
+        compiler_params=params,
+        cost_estimate=pl.CostEstimate(flops=0, bytes_accessed=2_000_000, transcendentals=0),
+    )(where, *far, *first_gains, *second_gains, *outs[6:])
+    key_weight, router_weight, gain_weight = pl.pallas_call(
+        write_near,
+        in_specs=[IN_SMEM] + [IN_VMEM] * 5 + [IN_HBM] * 2,
+        out_specs=[IN_HBM] * 2 + [IN_VMEM],
+        out_shape=shapes[6:] + [jax.ShapeDtypeStruct((16, LANES), jnp.bfloat16)],
+        input_output_aliases={6: 0, 7: 1},
+        scratch_shapes=sems,
+        compiler_params=params,
+    )(where, *near, far[0], first_gains[0], second_gains[0], *weights)
+    gains = [gain0, gain1, gain2]
     return outs[:6], gains, key_weight, router_weight, gain_weight
 
 
@@ -466,15 +491,16 @@
         0,
         tiled=True,
     )
+    wide_parts = parts.astype(jnp.float32)
+    [squares] = in_vmem(add_squares, [wide_parts], [((8, LANES), jnp.float32)])
+    squares = [squares] + [send(squares, to) for to in (SIBLING, PARTNER, PARTNER_SIBLING)]
+    parts, *squares = lax.optimization_barrier((parts, *squares))
     other = send(parts, SIBLING).astype(jnp.float32)
-    parts = parts.astype(jnp.float32)
-    [squares] = in_vmem(add_squares, [parts], [((8, LANES), jnp.float32)])
-    squares = [squares] + [send(squares, to) for to in (SIBLING, PARTNER, PARTNER_SIBLING)]
     states, gains, key_weight, router_weight, gain_weight = updated(
         core,
         half,
         squares,
-        parts,
+        wide_parts,
         other,
         states,
         [gain.reshape(8, LANES) for gain in (gain_master, gain_first, gain_second)],

time: 99.1 us -> 99.4 us (level)
  Pallas kernels: 16 us -> 17.6 us
  starting transfers between devices: 29.1 us -> 28 us
    pallas_call x1 -> x2, Pallas kernels: 2.34 us -> 4.08 us  [the longest x1 2.04 us: updated(): pl.pallas_call(write_far, in_specs=[IN_SMEM] + [IN_VMEM] * 8 + [IN_HBM] *...]
    ppermute x12, starting transfers between devices: 19.3 us -> 18.3 us  [send(): return lax.ppermute(x, ALL, pairs)]
  transfers between devices with their start and end apart: 13 -> 13, of which waited for: 6 -> 5; matrix products, arithmetic and copies ran while one was open for 0% -> 0% of each run, Pallas kernels for 10% -> 12%
where the time goes in v6:
time: 99.4 us; the launch traced here: 99 us
  starting transfers between devices  28 us (28%)
  blocking collectives  27.8 us (28%)
  waiting for transfers between devices  23.1 us (23%)
  Pallas kernels  17.6 us (18%)
  other arithmetic  1.29 us (1%)
  between operations  1.06 us (1%)
    all_to_all x1, blocking collectives, on_device(): lax.all_to_all(jnp.broadcast_to(code.astype(jnp.float16)[None], (64, 8, R...  27.8 us
    ppermute x12, starting transfers between devices, send(): return lax.ppermute(x, ALL, pairs)  18.3 us
    ppermute x12, waiting for transfers between devices, send(): return lax.ppermute(x, ALL, pairs)  13.2 us
    all_to_all x1, waiting for transfers between devices, on_device(): lax.all_to_all(code.astype(jnp.float16), ALL, 0, 0, axis_index_groups=SEC...  9.93 us
    all_to_all x1, starting transfers between devices, on_device(): lax.all_to_all(code.astype(jnp.float16), ALL, 0, 0, axis_index_groups=SEC...  9.76 us
    pallas_call x2, Pallas kernels, pack(): pl.pallas_call(pack_local, in_specs=[pl.BlockSpec(memory_space=pltpu.SMEM...  5.32 us
    pallas_call x1, Pallas kernels, updated(): pl.pallas_call(update_second, in_specs=[IN_SMEM] + [IN_VMEM] * 14 + [IN_H...  3.54 us
    pallas_call x1, Pallas kernels, updated(): pl.pallas_call(update_first, in_specs=[IN_SMEM] + [IN_VMEM] * 14, out_spe...  3.5 us
  transfers between devices with their start and end apart: 13, of which 5 were waited for; matrix products, arithmetic and copies ran while one was open for 0% of the time, Pallas kernels for 12%

profile of v6, /device:TPU:1, one launch (start us, length us, event | category | flops | bytes accessed | tf_op | source)
XLA Modules:
  0.0 99.0 jit_solution(14727506973889970772)
XLA Ops:
  0.7 0.1 pad_add_fusion.1.where_ref
  0.7 2.7 %shard_map.212 = bf16[4,4,8,8,640]{4,3,2,1,0:T(8,128)(2,1)S(1)} custom-call(s32[2]{0:T(128)S(1)} %pad_add_fusion.1.where_ref, bf16[2,2048,512]{2,1,0:T(8,128)(2,1)} %bitcast.23, bf16[2,64,2048]{2,1,0:T(8,128)(2,1)} %bitcast.25, bf16[2,2048]{1,0:T(2,128)(2,1)} %bitcast.27), custom_call_target="tpu_custom_call" | custom-call | tf_op jit(solution)/shard_map/pallas_call | solution.py:135
  3.4 3.3 %collective-permute-start = (bf16[4,4,8,8,640]{4,3,2,1,0:T(8,128)(2,1)S(1)}, bf16[4,4,8,8,640]{4,3,2,1,0:T(8,128)(2,1)S(1)}, u32[]{:S(2)}, u32[]{:S(2)}) collective-permute-start(bf16[4,4,8,8,640]{4,3,2,1,0:T(8,128)(2,1)S(1)} %shard_map.212), channel_id=1, source_target_pairs={{0,2},{2,0},{1,3},{3,1},{4,6},{6,4},{5,7},{7,5},{8,10},{10,8},{9,1... | collective-permute-start | bytes 3932168 | tf_op jit(solution)/shard_map/ppermute | solution.py:64
  6.7 0.1 pad_add_fusion.where_ref
  6.8 2.7 %shard_map.211.kept_ref = bf16[4,4,8,8,640]{4,3,2,1,0:T(8,128)(2,1)S(1)} custom-call(s32[2]{0:T(128)S(1)} %pad_add_fusion.where_ref, bf16[2,2048,512]{2,1,0:T(8,128)(2,1)} %bitcast.24, bf16[2,64,2048]{2,1,0:T(8,128)(2,1)} %bitcast.26, bf16[2,2048]{1,0:T(2,128)(2,1)} %bitcast.28), custom_call_target="tpu_custom_call" | custom-call | tf_op jit(solution)/shard_map/pallas_call | solution.py:135
  9.5 0.3 shard_map.213
  9.8 0.1 collective-permute-start.1
  9.9 2.2 %collective-permute-start.2 = (bf16[4,8,8,640]{3,2,1,0:T(8,128)(2,1)S(1)}, bf16[4,8,8,640]{3,2,1,0:T(8,128)(2,1)S(1)}, u32[]{:S(2)}, u32[]{:S(2)}) collective-permute-start(bf16[4,8,8,640]{3,2,1,0:T(8,128)(2,1)S(1)} %get-tuple-element.58), channel_id=1, source_target_pairs={{0,4},{2,18},{1,5},{3,19},{4,0},{6,22},{5,1},{7,23},{8,12},{10,26}... | collective-permute-start | bytes 983048 | tf_op jit(solution)/shard_map/ppermute | solution.py:64
  12.1 1.1 %collective-permute-start.3 = (bf16[4,8,8,640]{3,2,1,0:T(8,128)(2,1)S(1)}, bf16[4,8,8,640]{3,2,1,0:T(8,128)(2,1)S(1)}, u32[]{:S(2)}, u32[]{:S(2)}) collective-permute-start(bf16[4,8,8,640]{3,2,1,0:T(8,128)(2,1)S(1)} %get-tuple-element.59), channel_id=1, source_target_pairs={{0,5},{2,26},{1,0},{3,27},{4,1},{6,30},{5,4},{7,31},{8,13},{10,2},... | collective-permute-start | bytes 983048 | tf_op jit(solution)/shard_map/ppermute | solution.py:64
  13.1 7.7 %collective-permute-done.1.refs_1_ = bf16[4,8,8,640]{3,2,1,0:T(8,128)(2,1)S(1)} collective-permute-done((bf16[4,8,8,640]{3,2,1,0:T(8,128)(2,1)S(1)}, bf16[4,8,8,640]{3,2,1,0:T(8,128)(2,1)S(1)}, u32[]{:S(2)}, u32[]{:S(2)}) %collective-permute-start.1) | collective-permute-done | bytes 327712 | tf_op jit(solution)/shard_map/ppermute | solution.py:64
  20.8 0.6 collective-permute-done.3.refs_3_
  21.5 0.3 shard_map.214
  21.8 0.8 convert_element_type.15
  22.6 9.8 %all-to-all-start = ((f16[32,8,640]{2,1,0:T(8,128)(2,1)}), f16[32,8,640]{2,1,0:T(8,128)(2,1)S(1)}, u32[]{:S(2)}, u32[]{:S(2)}) async-start(f16[32,8,640]{2,1,0:T(8,128)(2,1)} %convert_element_type.15), calls=%async_computation | async-start | bytes 655360 | tf_op jit(solution)/shard_map/all_to_all | solution.py:483
  32.3 9.9 %all-to-all-done = f16[32,8,640]{2,1,0:T(8,128)(2,1)S(1)} async-done(((f16[32,8,640]{2,1,0:T(8,128)(2,1)}), f16[32,8,640]{2,1,0:T(8,128)(2,1)S(1)}, u32[]{:S(2)}, u32[]{:S(2)}) %all-to-all-start) | async-done | bytes 327712 | tf_op jit(solution)/shard_map/all_to_all | solution.py:483
  42.3 0.3 shard_map.215
  42.8 27.8 %all_to_all.10 = f16[64,8,640]{2,1,0:T(8,128)(2,1)S(1)} all-to-all(f16[64,8,640]{2,1,0:T(8,128)(2,1)S(1)} %broadcast_in_dim.2), channel_id=1, replica_groups=mesh['z'=8,'y'=4,'xh'=2,'c'=2,'xl'=2] {'xh','y','z'}, dimensions={0} | all-to-all | bytes 1310720 | tf_op jit(solution)/shard_map/all_to_all | solution.py:487
  70.7 0.1 convert_element_type.18.blocks_ref.refs_4_
  70.7 0.2 shard_map.216.refs_0_
  70.9 5.3 %collective-permute-start.6 = (f32[8,128]{1,0:T(8,128)S(1)}, f32[8,128]{1,0:T(8,128)S(1)}, u32[]{:S(2)}, u32[]{:S(2)}) collective-permute-start(f32[8,128]{1,0:T(8,128)S(1)} %shard_map.216.refs_0_), channel_id=1, source_target_pairs={{0,3},{2,1},{1,2},{3,0},{4,7},{6,5},{5,6},{7,4},{8,11},{10,9},{9,1... | collective-permute-start | bytes 12296 | tf_op jit(solution)/shard_map/ppermute | solution.py:64
  76.2 1.6 %collective-permute-start.5 = (f32[8,128]{1,0:T(8,128)S(1)}, f32[8,128]{1,0:T(8,128)S(1)}, u32[]{:S(2)}, u32[]{:S(2)}) collective-permute-start(f32[8,128]{1,0:T(8,128)S(1)} %shard_map.216.refs_0_), channel_id=1, source_target_pairs={{0,1},{2,3},{1,0},{3,2},{4,5},{6,7},{5,4},{7,6},{8,9},{10,11},{9,8... | collective-permute-start | bytes 12296 | tf_op jit(solution)/shard_map/ppermute | solution.py:64
  77.8 1.3 %collective-permute-done.5.refs_2_ = f32[8,128]{1,0:T(8,128)S(1)} collective-permute-done((f32[8,128]{1,0:T(8,128)S(1)}, f32[8,128]{1,0:T(8,128)S(1)}, u32[]{:S(2)}, u32[]{:S(2)}) %collective-permute-start.5) | collective-permute-done | bytes 4128 | tf_op jit(solution)/shard_map/ppermute | solution.py:64
  79.0 1.1 %collective-permute-start.7 = (f16[64,8,640]{2,1,0:T(8,128)(2,1)S(1)}, f16[64,8,640]{2,1,0:T(8,128)(2,1)S(1)}, u32[]{:S(2)}, u32[]{:S(2)}) collective-permute-start(f16[64,8,640]{2,1,0:T(8,128)(2,1)S(1)} %all_to_all.10), channel_id=1, source_target_pairs={{0,2},{2,0},{1,3},{3,1},{4,6},{6,4},{5,7},{7,5},{8,10},{10,8},{9,1... | collective-permute-start | bytes 1966088 | tf_op jit(solution)/shard_map/ppermute | solution.py:64
  80.2 3.5 %shard_map.217 = (f32[1024,512]{1,0:T(8,128)}, f32[1024,512]{1,0:T(8,128)}, f32[1024,512]{1,0:T(8,128)}, f32[64,1024]{1,0:T(8,128)}, f32[64,1024]{1,0:T(8,128)},...) custom-call(s32[2]{0:T(128)S(1)} %pad_add_fusion.2.where_ref, ...), custom_call_target="tpu_custom_call" | custom-call | flops 7000000 | bytes 8000000 | tf_op jit(solution)/shard_map/pallas_call | solution.py:404
  83.8 0.2 collective-permute-start.8
  83.9 2.0 %collective-permute-start.9 = (bf16[288,512]{1,0:T(8,128)(2,1)S(1)}, bf16[288,512]{1,0:T(8,128)(2,1)S(1)}, u32[]{:S(2)}, u32[]{:S(2)}) collective-permute-start(bf16[288,512]{1,0:T(8,128)(2,1)S(1)} %get-tuple-element.80), channel_id=1, source_target_pairs={{0,5},{2,7},{1,4},{3,6},{4,1},{6,3},{5,0},{7,2},{8,13},{10,15},{9,... | collective-permute-start | bytes 884744 | tf_op jit(solution)/shard_map/ppermute | solution.py:64
  86.0 0.1 convert_element_type.19.refs_4_
  86.1 3.5 %shard_map.218 = (f32[1024,512]{1,0:T(8,128)}, f32[1024,512]{1,0:T(8,128)}, f32[1024,512]{1,0:T(8,128)}, f32[64,1024]{1,0:T(8,128)}, f32[64,1024]{1,0:T(8,128)},...) custom-call(s32[2]{0:T(128)S(1)} %pad_add_fusion.3.where_ref, ...), custom_call_target="tpu_custom_call", output_to_operand_aliasing={{0}: (15, {}), {1}: (16, {}), {2}: (17, {}), {3}: (18, {}),... | custom-call | flops 7000000 | bytes 8000000 | tf_op jit(solution)/shard_map/pallas_call | solution.py:415
  89.7 3.6 %collective-permute-done.9.far1 = bf16[288,512]{1,0:T(8,128)(2,1)S(1)} collective-permute-done((bf16[288,512]{1,0:T(8,128)(2,1)S(1)}, bf16[288,512]{1,0:T(8,128)(2,1)S(1)}, u32[]{:S(2)}, u32[]{:S(2)}) %collective-permute-start.9) | collective-permute-done | bytes 294944 | tf_op jit(solution)/shard_map/ppermute | solution.py:64
  93.3 1.5 %collective-permute-start.10 = (bf16[296,512]{1,0:T(8,128)(2,1)S(1)}, bf16[296,512]{1,0:T(8,128)(2,1)S(1)}, u32[]{:S(2)}, u32[]{:S(2)}) collective-permute-start(bf16[296,512]{1,0:T(8,128)(2,1)S(1)} %collective-permute-done.8.far0), channel_id=1, source_target_pairs={{0,2},{2,0},{1,3},{3,1},{4,6},{6,4},{5,7},{7,5},{8,10},{10,8},{9,1... | collective-permute-start | bytes 909320 | tf_op jit(solution)/shard_map/ppermute | solution.py:64
  94.8 2.0 %shard_map.219 = (bf16[2048,512]{1,0:T(8,128)(2,1)}, bf16[64,2048]{1,0:T(8,128)(2,1)}, f32[8,128]{1,0:T(8,128)}, f32[8,128]{1,0:T(8,128)}, f32[8,128]{1,0:T(8,128)}) custom-call(s32[2]{0:T(128)S(1)} %pad_add_fusion.2.where_ref, bf16[296,512]{1,0:T(8,128)(2,1)S(1)} %collective-permute-done.8.far0, ...), custom_call_target="tpu_custom_call", output_to_operand_aliasing={{0}: (9, {}), {1}: (10, {})} | custom-call | bytes 2000000 | tf_op jit(solution)/shard_map/pallas_call | solution.py:432
  96.8 2.0 %shard_map.220 = (bf16[2048,512]{1,0:T(8,128)(2,1)}, bf16[64,2048]{1,0:T(8,128)(2,1)}, bf16[16,128]{1,0:T(8,128)(2,1)}) custom-call(s32[2]{0:T(128)S(1)} %pad_add_fusion.2.where_ref, bf16[296,512]{1,0:T(8,128)(2,1)S(1)} %collective-permute-done.10.near0, ...), custom_call_target="tpu_custom_call", output_to_operand_aliasing={{0}: (6, {}), {1}: (7, {})} | custom-call | tf_op jit(solution)/shard_map/pallas_call | solution.py:442
  (33 shorter events, 0.3 us)
Async XLA Ops:
  3.4 6.1 %collective-permute-start = (bf16[4,4,8,8,640]{4,3,2,1,0:T(8,128)(2,1)S(1)}, bf16[4,4,8,8,640]{4,3,2,1,0:T(8,128)(2,1)S(1)}, u32[]{:S(2)}, u32[]{:S(2)}) collective-permute-start(bf16[4,4,8,8,640]{4,3,2,1,0:T(8,128)(2,1)S(1)} %shard_map.212), channel_id=1, source_target_pairs={{0,2},{2,0},{1,3},{3,1},{4,6},{6,4},{5,7},{7,5},{8,10},{10,8},{9,1... | collective-permute-start | bytes 3932168 | tf_op jit(solution)/shard_map/ppermute | solution.py:64
  9.8 11.0 %collective-permute-start.1 = (bf16[4,8,8,640]{3,2,1,0:T(8,128)(2,1)S(1)}, bf16[4,8,8,640]{3,2,1,0:T(8,128)(2,1)S(1)}, u32[]{:S(2)}, u32[]{:S(2)}) collective-permute-start(bf16[4,8,8,640]{3,2,1,0:T(8,128)(2,1)S(1)} %get-tuple-element.57), channel_id=1, source_target_pairs={{0,1},{2,10},{1,4},{3,11},{4,5},{6,14},{5,0},{7,15},{8,9},{10,18},... | collective-permute-start | bytes 983048 | tf_op jit(solution)/shard_map/ppermute | solution.py:64
  9.9 10.9 %collective-permute-start.2 = (bf16[4,8,8,640]{3,2,1,0:T(8,128)(2,1)S(1)}, bf16[4,8,8,640]{3,2,1,0:T(8,128)(2,1)S(1)}, u32[]{:S(2)}, u32[]{:S(2)}) collective-permute-start(bf16[4,8,8,640]{3,2,1,0:T(8,128)(2,1)S(1)} %get-tuple-element.58), channel_id=1, source_target_pairs={{0,4},{2,18},{1,5},{3,19},{4,0},{6,22},{5,1},{7,23},{8,12},{10,26}... | collective-permute-start | bytes 983048 | tf_op jit(solution)/shard_map/ppermute | solution.py:64
  12.1 9.4 %collective-permute-start.3 = (bf16[4,8,8,640]{3,2,1,0:T(8,128)(2,1)S(1)}, bf16[4,8,8,640]{3,2,1,0:T(8,128)(2,1)S(1)}, u32[]{:S(2)}, u32[]{:S(2)}) collective-permute-start(bf16[4,8,8,640]{3,2,1,0:T(8,128)(2,1)S(1)} %get-tuple-element.59), channel_id=1, source_target_pairs={{0,5},{2,26},{1,0},{3,27},{4,1},{6,30},{5,4},{7,31},{8,13},{10,2},... | collective-permute-start | bytes 983048 | tf_op jit(solution)/shard_map/ppermute | solution.py:64
  22.6 57.6 %copy-start.5 = (f32[64,1024]{1,0:T(8,128)S(1)}, f32[64,1024]{1,0:T(8,128)}, u32[]{:S(2)}) copy-start(f32[64,1024]{1,0:T(8,128)} %refs_10_.3) | copy-start | bytes 786436
  22.6 19.7 %all-to-all-start = ((f16[32,8,640]{2,1,0:T(8,128)(2,1)}), f16[32,8,640]{2,1,0:T(8,128)(2,1)S(1)}, u32[]{:S(2)}, u32[]{:S(2)}) async-start(f16[32,8,640]{2,1,0:T(8,128)(2,1)} %convert_element_type.15), calls=%async_computation | async-start | bytes 655360 | tf_op jit(solution)/shard_map/all_to_all | solution.py:483
  42.3 37.9 %copy-start.2 = (f32[1024,512]{1,0:T(8,128)S(1)}, f32[1024,512]{1,0:T(8,128)}, u32[]{:S(2)}) copy-start(f32[1024,512]{1,0:T(8,128)} %refs_7_.3) | copy-start | bytes 6291460
  42.7 37.5 %copy-start.4 = (f32[64,1024]{1,0:T(8,128)S(1)}, f32[64,1024]{1,0:T(8,128)}, u32[]{:S(2)}) copy-start(f32[64,1024]{1,0:T(8,128)} %refs_9_.3) | copy-start | bytes 786436
  42.7 37.5 %copy-start = (f32[1024,512]{1,0:T(8,128)S(1)}, f32[1024,512]{1,0:T(8,128)}, u32[]{:S(2)}) copy-start(f32[1024,512]{1,0:T(8,128)} %refs_5_.3) | copy-start | bytes 6291460
  42.8 37.4 %copy-start.1 = (f32[1024,512]{1,0:T(8,128)S(1)}, f32[1024,512]{1,0:T(8,128)}, u32[]{:S(2)}) copy-start(f32[1024,512]{1,0:T(8,128)} %refs_6_.3) | copy-start | bytes 6291460
  42.8 37.4 %copy-start.3 = (f32[64,1024]{1,0:T(8,128)S(1)}, f32[64,1024]{1,0:T(8,128)}, u32[]{:S(2)}) copy-start(f32[64,1024]{1,0:T(8,128)} %refs_8_.3) | copy-start | bytes 786436
  42.8 37.4 %copy-start.6 = (f32[1024]{0:T(1024)S(1)}, f32[1024]{0:T(1024)}, u32[]{:S(2)}) copy-start(f32[1024]{0:T(1024)} %param.21) | copy-start | bytes 12292
  42.8 37.4 %copy-start.7 = (f32[1024]{0:T(1024)S(1)}, f32[1024]{0:T(1024)}, u32[]{:S(2)}) copy-start(f32[1024]{0:T(1024)} %param.22) | copy-start | bytes 12292
  42.8 37.4 %copy-start.8 = (f32[1024]{0:T(1024)S(1)}, f32[1024]{0:T(1024)}, u32[]{:S(2)}) copy-start(f32[1024]{0:T(1024)} %param.23) | copy-start | bytes 12292
  70.9 6.8 %collective-permute-start.6 = (f32[8,128]{1,0:T(8,128)S(1)}, f32[8,128]{1,0:T(8,128)S(1)}, u32[]{:S(2)}, u32[]{:S(2)}) collective-permute-start(f32[8,128]{1,0:T(8,128)S(1)} %shard_map.216.refs_0_), channel_id=1, source_target_pairs={{0,3},{2,1},{1,2},{3,0},{4,7},{6,5},{5,6},{7,4},{8,11},{10,9},{9,1... | collective-permute-start | bytes 12296 | tf_op jit(solution)/shard_map/ppermute | solution.py:64
  76.2 2.9 %collective-permute-start.5 = (f32[8,128]{1,0:T(8,128)S(1)}, f32[8,128]{1,0:T(8,128)S(1)}, u32[]{:S(2)}, u32[]{:S(2)}) collective-permute-start(f32[8,128]{1,0:T(8,128)S(1)} %shard_map.216.refs_0_), channel_id=1, source_target_pairs={{0,1},{2,3},{1,0},{3,2},{4,5},{6,7},{5,4},{7,6},{8,9},{10,11},{9,8... | collective-permute-start | bytes 12296 | tf_op jit(solution)/shard_map/ppermute | solution.py:64
  77.7 1.3 %collective-permute-start.4 = (f32[8,128]{1,0:T(8,128)S(1)}, f32[8,128]{1,0:T(8,128)S(1)}, u32[]{:S(2)}, u32[]{:S(2)}) collective-permute-start(f32[8,128]{1,0:T(8,128)S(1)} %shard_map.216.refs_0_), channel_id=1, source_target_pairs={{0,2},{2,0},{1,3},{3,1},{4,6},{6,4},{5,7},{7,5},{8,10},{10,8},{9,1... | collective-permute-start | bytes 12296 | tf_op jit(solution)/shard_map/ppermute | solution.py:64
  79.0 7.0 %collective-permute-start.7 = (f16[64,8,640]{2,1,0:T(8,128)(2,1)S(1)}, f16[64,8,640]{2,1,0:T(8,128)(2,1)S(1)}, u32[]{:S(2)}, u32[]{:S(2)}) collective-permute-start(f16[64,8,640]{2,1,0:T(8,128)(2,1)S(1)} %all_to_all.10), channel_id=1, source_target_pairs={{0,2},{2,0},{1,3},{3,1},{4,6},{6,4},{5,7},{7,5},{8,10},{10,8},{9,1... | collective-permute-start | bytes 1966088 | tf_op jit(solution)/shard_map/ppermute | solution.py:64
  83.8 9.5 %collective-permute-start.8 = (bf16[296,512]{1,0:T(8,128)(2,1)S(1)}, bf16[296,512]{1,0:T(8,128)(2,1)S(1)}, u32[]{:S(2)}, u32[]{:S(2)}) collective-permute-start(bf16[296,512]{1,0:T(8,128)(2,1)S(1)} %get-tuple-element.79), channel_id=1, source_target_pairs={{0,1},{2,3},{1,0},{3,2},{4,5},{6,7},{5,4},{7,6},{8,9},{10,11},{9,8... | collective-permute-start | bytes 909320 | tf_op jit(solution)/shard_map/ppermute | solution.py:64
  83.9 9.3 %collective-permute-start.9 = (bf16[288,512]{1,0:T(8,128)(2,1)S(1)}, bf16[288,512]{1,0:T(8,128)(2,1)S(1)}, u32[]{:S(2)}, u32[]{:S(2)}) collective-permute-start(bf16[288,512]{1,0:T(8,128)(2,1)S(1)} %get-tuple-element.80), channel_id=1, source_target_pairs={{0,5},{2,7},{1,4},{3,6},{4,1},{6,3},{5,0},{7,2},{8,13},{10,15},{9,... | collective-permute-start | bytes 884744 | tf_op jit(solution)/shard_map/ppermute | solution.py:64
  93.3 3.5 %collective-permute-start.10 = (bf16[296,512]{1,0:T(8,128)(2,1)S(1)}, bf16[296,512]{1,0:T(8,128)(2,1)S(1)}, u32[]{:S(2)}, u32[]{:S(2)}) collective-permute-start(bf16[296,512]{1,0:T(8,128)(2,1)S(1)} %collective-permute-done.8.far0), channel_id=1, source_target_pairs={{0,2},{2,0},{1,3},{3,1},{4,6},{6,4},{5,7},{7,5},{8,10},{10,8},{9,1... | collective-permute-start | bytes 909320 | tf_op jit(solution)/shard_map/ppermute | solution.py:64
  94.8 2.1 %collective-permute-start.11 = (bf16[288,512]{1,0:T(8,128)(2,1)S(1)}, bf16[288,512]{1,0:T(8,128)(2,1)S(1)}, u32[]{:S(2)}, u32[]{:S(2)}) collective-permute-start(bf16[288,512]{1,0:T(8,128)(2,1)S(1)} %collective-permute-done.9.far1), channel_id=1, source_target_pairs={{0,2},{2,0},{1,3},{3,1},{4,6},{6,4},{5,7},{7,5},{8,10},{10,8},{9,1... | collective-permute-start | bytes 884744 | tf_op jit(solution)/shard_map/ppermute | solution.py:64

commit v7 on v5

--- a/solution.py
+++ b/solution.py
@@ -67,10 +67,9 @@
 def adamw(master, first_moment, second, scaled, decay_rate):
     first_new = beta_one * first_moment + (1.0 - beta_one) * scaled
     second_new = beta_two * second + (1.0 - beta_two) * scaled * scaled
-    update = (
-        first_new / bias_one / (jnp.sqrt(second_new / bias_two) + epsilon) + decay_rate * master
-    )
-    master_new = master - step_rate * update
+    root = jnp.sqrt(second_new * (1.0 / bias_two)) + epsilon
+    kept = master if decay_rate == 0.0 else master * (1.0 - step_rate * decay_rate)
+    master_new = kept - first_new * (step_rate / bias_one) / root
     return (master_new, first_new, second_new)
 
 
@@ -258,25 +257,12 @@
     return clip_limit / jnp.maximum(jnp.sqrt(total), clip_limit)
 
 
-def update_rows(where_ref, squares, blocks_ref, ins, outs, messages, keys, routers, sems):
-    t, half = where_ref[0], where_ref[1]
+def update_rows(where_ref, squares, blocks_ref, ins, outs, after_group=None):
+    t = where_ref[0]
     factor = clip_factor(squares)
     key_ins, router_ins, gain_ins = ins[:3], ins[3:6], ins[6:]
-    key_outs, router_outs, key_weight, router_weight = outs[:3], outs[3:6], outs[6], outs[7]
-    gain_outs = outs[8:]
+    keys, routers, gain_outs, messages = outs[0], outs[1], outs[2:5], outs[5:]
     low = lax.broadcasted_iota(jnp.int32, (8, LANES), 1) < 64
-
-    def key_rows(g, base=0):
-        return pl.ds(pl.multiple_of(base + t * 512 + g * 64, 64), 64)
-
-    router_rows = pl.ds(pl.multiple_of(t * 32, 32), 32)
-    stores = []
-
-    def store(source, target):
-        copy = pltpu.make_async_copy(source, target, sems.at[len(stores)])
-        copy.start()
-        stores.append(copy)
-
     row = lax.broadcasted_iota(jnp.int32, (8, LANES), 0)
     scaled = jnp.zeros((8, LANES), jnp.float32)
     for z in range(8):
@@ -309,61 +295,87 @@
         for a in range(3):
             routers[a, rows, columns] = new[a]
         message[pl.ds(256 + at * 8, 8)] = new[0].astype(jnp.bfloat16)
-        for a in range(3):
-            store(keys.at[a, pl.ds(g * 64, 64)], key_outs[a].at[key_rows(g)])
-        if at == 3:
-            write_message(t, half, g // 4, message, key_weight, router_weight, store)
+        if after_group is not None:
+            after_group(g)
+
+
+class Stores:
+    def __init__(self, sems):
+        self.sems, self.copies = sems, []
+
+    def __call__(self, source, target):
+        copy = pltpu.make_async_copy(source, target, self.sems.at[len(self.copies)])
+        copy.start()
+        self.copies.append(copy)
+
+    def wait(self):
+        for copy in self.copies:
+            copy.wait()
+
+
+def store_weights(store, t, half, g, message, key_weight, router_weight):
+    rows = pl.ds(pl.multiple_of(half * 1024 + t * 512 + g * 64, 64), 64)
+    store(message.at[pl.ds(g % 4 * 64, 64)], key_weight.at[rows])
+    rows = pl.ds(pl.multiple_of(t * 32 + g // 2 * 8, 8), 8)
+    columns = pl.ds(pl.multiple_of(half * 1024 + g % 2 * 512, 512), 512)
+    store(message.at[pl.ds(256 + g % 4 * 8, 8)], router_weight.at[rows, columns])
+
+
+def store_group(store, t, half, g, keys, message, outs):
+    rows = pl.ds(pl.multiple_of(t * 512 + g * 64, 64), 64)
     for a in range(3):
-        store(routers.at[a], router_outs[a].at[router_rows])
-    for copy in stores:
-        copy.wait()
-
-
-def write_message(t, half, which, message, key_weight, router_weight, store):
-    rows = pl.ds(pl.multiple_of(half * 1024 + t * 512 + which * 256, 256), 256)
-    store(message.at[pl.ds(0, 256)], key_weight.at[rows])
-    for i in range(4):
-        rows = pl.ds(pl.multiple_of(t * 32 + (which * 2 + i // 2) * 8, 8), 8)
-        columns = pl.ds(pl.multiple_of(half * 1024 + i % 2 * 512, 512), 512)
-        store(message.at[pl.ds(256 + i * 8, 8)], router_weight.at[rows, columns])
+        store(keys.at[a, pl.ds(g * 64, 64)], outs[a].at[rows])
+    store_weights(store, t, half, g, message, outs[6], outs[7])
+
+
+def store_routers(store, t, routers, outs):
+    rows = pl.ds(pl.multiple_of(t * 32, 32), 32)
+    for a in range(3):
+        store(routers.at[a], outs[3 + a].at[rows])
 
 
 def update_first(where_ref, *refs):
-    squares, blocks_ref, ins = refs[:4], refs[4], refs[5:14]
-    outs, messages, scratch = refs[14:25], refs[25:27], refs[27:]
-    update_rows(where_ref, squares, blocks_ref, ins, outs, messages, *scratch)
+    update_rows(where_ref, refs[:4], refs[4], refs[5:14], refs[14:])
 
 
 def update_second(where_ref, *refs):
-    squares, blocks_ref, ins = refs[:4], refs[4], refs[5:14]
-    outs, scratch = refs[22:33], refs[33:]
-    update_rows(where_ref, squares, blocks_ref, ins, outs, scratch[:2], *scratch[2:])
+    squares, blocks_ref, ins, first = refs[:4], refs[4], refs[5:14], refs[14:18]
+    outs, gains, scratch = refs[18:26], refs[26:29], refs[29:]
+    keys, routers, messages, sems = scratch[0], scratch[1], scratch[2:4], scratch[4]
+    t, half = where_ref[0], where_ref[1]
+    store = Stores(sems)
+    for g in range(8):
+        store_group(store, 1 - t, half, g, first[0], first[2 + g // 4], outs)
+    store_routers(store, 1 - t, first[1], outs)
+    update_rows(
+        where_ref,
+        squares,
+        blocks_ref,
+        ins,
+        (keys, routers, *gains, *messages),
+        lambda g: store_group(store, t, half, g, keys, messages[g // 4], outs),
+    )
+    store_routers(store, t, routers, outs)
+    store.wait()
 
 
 def write_received(where_ref, far0, far1, near0, near1, *refs):
     first_gains, second_gains = refs[:3], refs[3:6]
     key_weight, router_weight, gain_outs, gain_weight, sems = *refs[8:10], refs[10:13], *refs[13:]
     t, half = where_ref[0], where_ref[1]
-    stores = []
-
-    def store(source, target):
-        copy = pltpu.make_async_copy(source, target, sems.at[len(stores)])
-        copy.start()
-        stores.append(copy)
-
-    write_message(t, 1 - half, 0, far0, key_weight, router_weight, store)
-    write_message(t, 1 - half, 1, far1, key_weight, router_weight, store)
-    write_message(1 - t, 1 - half, 0, near0, key_weight, router_weight, store)
-    write_message(1 - t, 1 - half, 1, near1, key_weight, router_weight, store)
+    store = Stores(sems)
+    for g in range(8):
+        store_weights(store, t, 1 - half, g, (far0, far1)[g // 4], key_weight, router_weight)
+        store_weights(store, 1 - t, 1 - half, g, (near0, near1)[g // 4], key_weight, router_weight)
     for a in range(3):
         gain_outs[a][...] = jnp.where(t == 0, first_gains[a][...], second_gains[a][...])
     rows = pl.ds(288, 8)
     far, near = far0[rows, :LANES].astype(jnp.float32), near0[rows, :LANES].astype(jnp.float32)
-    far, mine = jnp.where(t == 0, far, near), gain_outs[0][...]
+    far = jnp.where(t == 0, far, near)
+    mine = jnp.where(t == 0, first_gains[0][...], second_gains[0][...])
     gain_weight[:8] = jnp.where(half == 0, mine, far).astype(jnp.bfloat16)
     gain_weight[8:] = jnp.where(half == 0, far, mine).astype(jnp.bfloat16)
-    for copy in stores:
-        copy.wait()
+    store.wait()
 
 
 IN_VMEM = pl.BlockSpec(memory_space=pltpu.VMEM)
@@ -383,34 +395,30 @@
         jax.ShapeDtypeStruct((EXPERTS, D), jnp.bfloat16),
     ]
     gain_shapes = [jax.ShapeDtypeStruct((8, LANES), jnp.float32)] * 3
-    scratch = [
-        pltpu.VMEM((3, 512, KEY_WIDTH), jnp.float32),
-        pltpu.VMEM((3, 32, 1024), jnp.float32),
-        pltpu.SemaphoreType.DMA((37,)),
-    ]
-    params = pltpu.CompilerParams(vmem_limit_bytes=6 * 1024 * 1024)
+    rows = [((3, 512, KEY_WIDTH), jnp.float32), ((3, 32, 1024), jnp.float32)]
     cost = pl.CostEstimate(flops=7_000_000, bytes_accessed=8_000_000, transcendentals=600_000)
-    outs = pl.pallas_call(
+    keys, routers, *outs = pl.pallas_call(
         update_first,
         in_specs=[IN_SMEM] + [IN_VMEM] * 14,
-        out_specs=[IN_HBM] * 8 + [IN_VMEM] * 5,
-        out_shape=shapes + gain_shapes + [jax.ShapeDtypeStruct(*m) for m in MESSAGES],
-        scratch_shapes=scratch,
-        compiler_params=params,
+        out_specs=[IN_VMEM] * 7,
+        out_shape=[jax.ShapeDtypeStruct(*r) for r in rows]
+        + gain_shapes
+        + [jax.ShapeDtypeStruct(*m) for m in MESSAGES],
+        compiler_params=pltpu.CompilerParams(vmem_limit_bytes=2 * 1024 * 1024),
         cost_estimate=cost,
     )(jnp.stack([core, half]), *squares, parts, *states, *gains)
-    outs, first_gains, sent = outs[:8], outs[8:11], outs[11:]
+    first_gains, sent = outs[:3], outs[3:]
     far = [send(sent[0], PARTNER), send(sent[1], OTHER_PARTNER)]
     outs = pl.pallas_call(
         update_second,
-        in_specs=[IN_SMEM] + [IN_VMEM] * 14 + [IN_HBM] * 8,
+        in_specs=[IN_SMEM] + [IN_VMEM] * 18,
         out_specs=[IN_HBM] * 8 + [IN_VMEM] * 3,
         out_shape=shapes + gain_shapes,
-        input_output_aliases={15 + i: i for i in range(8)},
-        scratch_shapes=[pltpu.VMEM(*m) for m in MESSAGES] + scratch,
-        compiler_params=params,
+        scratch_shapes=[pltpu.VMEM(*r) for r in rows + MESSAGES]
+        + [pltpu.SemaphoreType.DMA((86,))],
+        compiler_params=pltpu.CompilerParams(vmem_limit_bytes=8 * 1024 * 1024),
         cost_estimate=cost,
-    )(jnp.stack([1 - core, half]), *squares, other, *states, *gains, *outs)
+    )(jnp.stack([1 - core, half]), *squares, other, *states, *gains, keys, routers, *sent)
     outs, second_gains = outs[:8], outs[8:]
     far0, far1, gain_new = lax.optimization_barrier((*far, second_gains[0]))
     far, second_gains = [far0, far1], [gain_new, *second_gains[1:]]
@@ -421,7 +429,7 @@
         out_specs=[IN_HBM] * 2 + [IN_VMEM] * 4,
         out_shape=shapes[6:] + gain_shapes + [jax.ShapeDtypeStruct((16, LANES), jnp.bfloat16)],
         input_output_aliases={11: 0, 12: 1},
-        scratch_shapes=[pltpu.SemaphoreType.DMA((20,))],
+        scratch_shapes=[pltpu.SemaphoreType.DMA((32,))],
         compiler_params=pltpu.CompilerParams(vmem_limit_bytes=2 * 1024 * 1024),
     )(jnp.stack([core, half]), *far, *near, *first_gains, *second_gains, *outs[6:])
     return outs[:6], gains, key_weight, router_weight, gain_weight
@@ -466,15 +474,16 @@
         0,
         tiled=True,
     )
+    wide_parts = parts.astype(jnp.float32)
+    [squares] = in_vmem(add_squares, [wide_parts], [((8, LANES), jnp.float32)])
+    squares = [squares] + [send(squares, to) for to in (SIBLING, PARTNER, PARTNER_SIBLING)]
+    parts, *squares = lax.optimization_barrier((parts, *squares))
     other = send(parts, SIBLING).astype(jnp.float32)
-    parts = parts.astype(jnp.float32)
-    [squares] = in_vmem(add_squares, [parts], [((8, LANES), jnp.float32)])
-    squares = [squares] + [send(squares, to) for to in (SIBLING, PARTNER, PARTNER_SIBLING)]
     states, gains, key_weight, router_weight, gain_weight = updated(
         core,
         half,
         squares,
-        parts,
+        wide_parts,
         other,
         states,
         [gain.reshape(8, LANES) for gain in (gain_master, gain_first, gain_second)],

time: 99.1 us -> 98.4 us (level)
  starting transfers between devices: 29.1 us -> 27.7 us
  waiting for transfers between devices: 23.3 us -> 24.7 us
    pallas_call x1, Pallas kernels: 3.61 us -> 1.61 us  [updated(): pl.pallas_call(update_first, in_specs=[IN_SMEM] + [IN_VMEM] * 14, out_spe...]
    ppermute x12, starting transfers between devices: 19.3 us -> 18 us  [send(): return lax.ppermute(x, ALL, pairs)]
    ppermute x12, waiting for transfers between devices: 13.4 us -> 14.8 us  [send(): return lax.ppermute(x, ALL, pairs)]
    pallas_call x1, Pallas kernels: 3.62 us -> 4.78 us  [updated(): pl.pallas_call(update_second, in_specs=[IN_SMEM] + [IN_VMEM] * 18, out_sp...]
  transfers between devices with their start and end apart: 13 -> 13, of which waited for: 6 -> 7; matrix products, arithmetic and copies ran while one was open for 0% -> 0% of each run, Pallas kernels for 10% -> 9%
where the time goes in v7:
time: 98.4 us; the launch traced here: 98 us
  blocking collectives  27.8 us (28%)
  starting transfers between devices  27.7 us (28%)
  waiting for transfers between devices  24.7 us (25%)
  Pallas kernels  15.3 us (16%)
  other arithmetic  1.29 us (1%)
  between operations  1.03 us (1%)
    all_to_all x1, blocking collectives, on_device(): lax.all_to_all(jnp.broadcast_to(code.astype(jnp.float16)[None], (64, 8, R...  27.8 us
    ppermute x12, starting transfers between devices, send(): return lax.ppermute(x, ALL, pairs)  18 us
    ppermute x12, waiting for transfers between devices, send(): return lax.ppermute(x, ALL, pairs)  14.8 us
    all_to_all x1, waiting for transfers between devices, on_device(): lax.all_to_all(code.astype(jnp.float16), ALL, 0, 0, axis_index_groups=SEC...  9.93 us
    all_to_all x1, starting transfers between devices, on_device(): lax.all_to_all(code.astype(jnp.float16), ALL, 0, 0, axis_index_groups=SEC...  9.76 us
    pallas_call x2, Pallas kernels, pack(): pl.pallas_call(pack_local, in_specs=[pl.BlockSpec(memory_space=pltpu.SMEM...  5.32 us
    pallas_call x1, Pallas kernels, updated(): pl.pallas_call(update_second, in_specs=[IN_SMEM] + [IN_VMEM] * 18, out_sp...  4.78 us
    pallas_call x1, Pallas kernels, updated(): pl.pallas_call(write_received, in_specs=[IN_SMEM] + [IN_VMEM] * 10 + [IN_...  2.44 us
  transfers between devices with their start and end apart: 13, of which 7 were waited for; matrix products, arithmetic and copies ran while one was open for 0% of the time, Pallas kernels for 9%

profile of v7, /device:TPU:1, one launch (start us, length us, event | category | flops | bytes accessed | tf_op | source)
XLA Modules:
  0.0 98.0 jit_solution(8156008358505306656)
XLA Ops:
  0.7 0.1 pad_add_fusion.1.where_ref
  0.7 2.7 %shard_map.212 = bf16[4,4,8,8,640]{4,3,2,1,0:T(8,128)(2,1)S(1)} custom-call(s32[2]{0:T(128)S(1)} %pad_add_fusion.1.where_ref, bf16[2,2048,512]{2,1,0:T(8,128)(2,1)} %bitcast.23, bf16[2,64,2048]{2,1,0:T(8,128)(2,1)} %bitcast.25, bf16[2,2048]{1,0:T(2,128)(2,1)} %bitcast.27), custom_call_target="tpu_custom_call" | custom-call | tf_op jit(solution)/shard_map/pallas_call | solution.py:135
  3.4 3.3 %collective-permute-start = (bf16[4,4,8,8,640]{4,3,2,1,0:T(8,128)(2,1)S(1)}, bf16[4,4,8,8,640]{4,3,2,1,0:T(8,128)(2,1)S(1)}, u32[]{:S(2)}, u32[]{:S(2)}) collective-permute-start(bf16[4,4,8,8,640]{4,3,2,1,0:T(8,128)(2,1)S(1)} %shard_map.212), channel_id=1, source_target_pairs={{0,2},{2,0},{1,3},{3,1},{4,6},{6,4},{5,7},{7,5},{8,10},{10,8},{9,1... | collective-permute-start | bytes 3932168 | tf_op jit(solution)/shard_map/ppermute | solution.py:64
  6.8 2.7 %shard_map.211.kept_ref = bf16[4,4,8,8,640]{4,3,2,1,0:T(8,128)(2,1)S(1)} custom-call(s32[2]{0:T(128)S(1)} %pad_add_fusion.where_ref, bf16[2,2048,512]{2,1,0:T(8,128)(2,1)} %bitcast.24, bf16[2,64,2048]{2,1,0:T(8,128)(2,1)} %bitcast.26, bf16[2,2048]{1,0:T(2,128)(2,1)} %bitcast.28), custom_call_target="tpu_custom_call" | custom-call | tf_op jit(solution)/shard_map/pallas_call | solution.py:135
  9.5 0.3 shard_map.213
  9.8 0.1 collective-permute-start.1
  9.9 2.2 %collective-permute-start.2 = (bf16[4,8,8,640]{3,2,1,0:T(8,128)(2,1)S(1)}, bf16[4,8,8,640]{3,2,1,0:T(8,128)(2,1)S(1)}, u32[]{:S(2)}, u32[]{:S(2)}) collective-permute-start(bf16[4,8,8,640]{3,2,1,0:T(8,128)(2,1)S(1)} %get-tuple-element.50), channel_id=1, source_target_pairs={{0,4},{2,18},{1,5},{3,19},{4,0},{6,22},{5,1},{7,23},{8,12},{10,26}... | collective-permute-start | bytes 983048 | tf_op jit(solution)/shard_map/ppermute | solution.py:64
  12.1 1.1 %collective-permute-start.3 = (bf16[4,8,8,640]{3,2,1,0:T(8,128)(2,1)S(1)}, bf16[4,8,8,640]{3,2,1,0:T(8,128)(2,1)S(1)}, u32[]{:S(2)}, u32[]{:S(2)}) collective-permute-start(bf16[4,8,8,640]{3,2,1,0:T(8,128)(2,1)S(1)} %get-tuple-element.51), channel_id=1, source_target_pairs={{0,5},{2,26},{1,0},{3,27},{4,1},{6,30},{5,4},{7,31},{8,13},{10,2},... | collective-permute-start | bytes 983048 | tf_op jit(solution)/shard_map/ppermute | solution.py:64
  13.1 7.7 %collective-permute-done.1.refs_1_ = bf16[4,8,8,640]{3,2,1,0:T(8,128)(2,1)S(1)} collective-permute-done((bf16[4,8,8,640]{3,2,1,0:T(8,128)(2,1)S(1)}, bf16[4,8,8,640]{3,2,1,0:T(8,128)(2,1)S(1)}, u32[]{:S(2)}, u32[]{:S(2)}) %collective-permute-start.1) | collective-permute-done | bytes 327712 | tf_op jit(solution)/shard_map/ppermute | solution.py:64
  20.8 0.6 collective-permute-done.3.refs_3_
  21.4 0.3 shard_map.214
  21.8 0.8 convert_element_type.15
  22.6 9.8 %all-to-all-start = ((f16[32,8,640]{2,1,0:T(8,128)(2,1)}), f16[32,8,640]{2,1,0:T(8,128)(2,1)S(1)}, u32[]{:S(2)}, u32[]{:S(2)}) async-start(f16[32,8,640]{2,1,0:T(8,128)(2,1)} %convert_element_type.15), calls=%async_computation | async-start | bytes 655360 | tf_op jit(solution)/shard_map/all_to_all | solution.py:466
  32.3 9.9 %all-to-all-done = f16[32,8,640]{2,1,0:T(8,128)(2,1)S(1)} async-done(((f16[32,8,640]{2,1,0:T(8,128)(2,1)}), f16[32,8,640]{2,1,0:T(8,128)(2,1)S(1)}, u32[]{:S(2)}, u32[]{:S(2)}) %all-to-all-start) | async-done | bytes 327712 | tf_op jit(solution)/shard_map/all_to_all | solution.py:466
  42.3 0.3 shard_map.215
  42.8 27.8 %all_to_all.10 = f16[64,8,640]{2,1,0:T(8,128)(2,1)S(1)} all-to-all(f16[64,8,640]{2,1,0:T(8,128)(2,1)S(1)} %broadcast_in_dim.2), channel_id=1, replica_groups=mesh['z'=8,'y'=4,'xh'=2,'c'=2,'xl'=2] {'xh','y','z'}, dimensions={0} | all-to-all | bytes 1310720 | tf_op jit(solution)/shard_map/all_to_all | solution.py:470
  70.6 0.1 convert_element_type.18.blocks_ref.refs_4_
  70.7 0.2 shard_map.216.refs_0_
  70.9 5.5 %collective-permute-start.4 = (f32[8,128]{1,0:T(8,128)S(1)}, f32[8,128]{1,0:T(8,128)S(1)}, u32[]{:S(2)}, u32[]{:S(2)}) collective-permute-start(f32[8,128]{1,0:T(8,128)S(1)} %shard_map.216.refs_0_), channel_id=1, source_target_pairs={{0,2},{2,0},{1,3},{3,1},{4,6},{6,4},{5,7},{7,5},{8,10},{10,8},{9,1... | collective-permute-start | bytes 12296 | tf_op jit(solution)/shard_map/ppermute | solution.py:64
  76.4 1.7 %collective-permute-start.6 = (f32[8,128]{1,0:T(8,128)S(1)}, f32[8,128]{1,0:T(8,128)S(1)}, u32[]{:S(2)}, u32[]{:S(2)}) collective-permute-start(f32[8,128]{1,0:T(8,128)S(1)} %shard_map.216.refs_0_), channel_id=1, source_target_pairs={{0,3},{2,1},{1,2},{3,0},{4,7},{6,5},{5,6},{7,4},{8,11},{10,9},{9,1... | collective-permute-start | bytes 12296 | tf_op jit(solution)/shard_map/ppermute | solution.py:64
  78.1 0.7 collective-permute-done.5.refs_2_
  78.9 0.8 collective-permute-done.6.refs_3_
  79.7 0.4 collective-permute-start.7
  80.2 1.6 %shard_map.217 = (f32[3,512,512]{2,1,0:T(8,128)S(1)}, f32[3,32,1024]{2,1,0:T(8,128)S(1)}, f32[8,128]{1,0:T(8,128)S(1)}, f32[8,128]{1,0:T(8,128)S(1)}, f32[8,128]...) custom-call(s32[2]{0:T(128)S(1)} %pad_add_fusion.2.where_ref, ...), custom_call_target="tpu_custom_call" | custom-call | flops 7000000 | bytes 8000000 | tf_op jit(solution)/shard_map/pallas_call | solution.py:400
  81.9 1.3 %collective-permute-start.8 = (bf16[296,512]{1,0:T(8,128)(2,1)S(1)}, bf16[296,512]{1,0:T(8,128)(2,1)S(1)}, u32[]{:S(2)}, u32[]{:S(2)}) collective-permute-start(bf16[296,512]{1,0:T(8,128)(2,1)S(1)} %get-tuple-element.59.refs_16_), channel_id=1, source_target_pairs={{0,1},{2,3},{1,0},{3,2},{4,5},{6,7},{5,4},{7,6},{8,9},{10,11},{9,8... | collective-permute-start | bytes 909320 | tf_op jit(solution)/shard_map/ppermute | solution.py:64
  83.1 1.1 %collective-permute-start.9 = (bf16[288,512]{1,0:T(8,128)(2,1)S(1)}, bf16[288,512]{1,0:T(8,128)(2,1)S(1)}, u32[]{:S(2)}, u32[]{:S(2)}) collective-permute-start(bf16[288,512]{1,0:T(8,128)(2,1)S(1)} %get-tuple-element.60.refs_17_), channel_id=1, source_target_pairs={{0,5},{2,7},{1,4},{3,6},{4,1},{6,3},{5,0},{7,2},{8,13},{10,15},{9,... | collective-permute-start | bytes 884744 | tf_op jit(solution)/shard_map/ppermute | solution.py:64
  84.3 0.1 convert_element_type.19.refs_4_
  84.4 4.8 %shard_map.218 = (f32[1024,512]{1,0:T(8,128)}, f32[1024,512]{1,0:T(8,128)}, f32[1024,512]{1,0:T(8,128)}, f32[64,1024]{1,0:T(8,128)}, f32[64,1024]{1,0:T(8,128)},...) custom-call(s32[2]{0:T(128)S(1)} %pad_add_fusion.3.where_ref, ...), custom_call_target="tpu_custom_call" | custom-call | flops 7000000 | bytes 8000000 | tf_op jit(solution)/shard_map/pallas_call | solution.py:412
  89.2 3.2 %collective-permute-done.9.far1 = bf16[288,512]{1,0:T(8,128)(2,1)S(1)} collective-permute-done((bf16[288,512]{1,0:T(8,128)(2,1)S(1)}, bf16[288,512]{1,0:T(8,128)(2,1)S(1)}, u32[]{:S(2)}, u32[]{:S(2)}) %collective-permute-start.9) | collective-permute-done | bytes 294944 | tf_op jit(solution)/shard_map/ppermute | solution.py:64
  92.5 1.3 %collective-permute-start.10 = (bf16[296,512]{1,0:T(8,128)(2,1)S(1)}, bf16[296,512]{1,0:T(8,128)(2,1)S(1)}, u32[]{:S(2)}, u32[]{:S(2)}) collective-permute-start(bf16[296,512]{1,0:T(8,128)(2,1)S(1)} %collective-permute-done.8.far0), channel_id=1, source_target_pairs={{0,2},{2,0},{1,3},{3,1},{4,6},{6,4},{5,7},{7,5},{8,10},{10,8},{9,1... | collective-permute-start | bytes 909320 | tf_op jit(solution)/shard_map/ppermute | solution.py:64
  93.8 1.6 %collective-permute-done.11.near1 = bf16[288,512]{1,0:T(8,128)(2,1)S(1)} collective-permute-done((bf16[288,512]{1,0:T(8,128)(2,1)S(1)}, bf16[288,512]{1,0:T(8,128)(2,1)S(1)}, u32[]{:S(2)}, u32[]{:S(2)}) %collective-permute-start.11) | collective-permute-done | bytes 294944 | tf_op jit(solution)/shard_map/ppermute | solution.py:64
  95.4 2.4 %shard_map.219 = (bf16[2048,512]{1,0:T(8,128)(2,1)}, bf16[64,2048]{1,0:T(8,128)(2,1)}, f32[8,128]{1,0:T(8,128)}, f32[8,128]{1,0:T(8,128)}, f32[8,128]{1,0:T(8,128)}, /*index=5*/bf16[16,128]{1,0:T(8,128)(2,1)}) custom-call(s32[2]{0:T(128)S(1)} %pad_add_fusion.2.where_ref, ...), custom_call_target="tpu_custom_call", output_to_operand_aliasing={{0}: (11, {}), {1}: (12, {})} | custom-call | tf_op jit(solution)/shard_map/pallas_call | solution.py:426
  (32 shorter events, 0.4 us)
Async XLA Ops:
  3.4 6.1 %collective-permute-start = (bf16[4,4,8,8,640]{4,3,2,1,0:T(8,128)(2,1)S(1)}, bf16[4,4,8,8,640]{4,3,2,1,0:T(8,128)(2,1)S(1)}, u32[]{:S(2)}, u32[]{:S(2)}) collective-permute-start(bf16[4,4,8,8,640]{4,3,2,1,0:T(8,128)(2,1)S(1)} %shard_map.212), channel_id=1, source_target_pairs={{0,2},{2,0},{1,3},{3,1},{4,6},{6,4},{5,7},{7,5},{8,10},{10,8},{9,1... | collective-permute-start | bytes 3932168 | tf_op jit(solution)/shard_map/ppermute | solution.py:64
  9.8 11.0 %collective-permute-start.1 = (bf16[4,8,8,640]{3,2,1,0:T(8,128)(2,1)S(1)}, bf16[4,8,8,640]{3,2,1,0:T(8,128)(2,1)S(1)}, u32[]{:S(2)}, u32[]{:S(2)}) collective-permute-start(bf16[4,8,8,640]{3,2,1,0:T(8,128)(2,1)S(1)} %get-tuple-element.49), channel_id=1, source_target_pairs={{0,1},{2,10},{1,4},{3,11},{4,5},{6,14},{5,0},{7,15},{8,9},{10,18},... | collective-permute-start | bytes 983048 | tf_op jit(solution)/shard_map/ppermute | solution.py:64
  9.9 10.9 %collective-permute-start.2 = (bf16[4,8,8,640]{3,2,1,0:T(8,128)(2,1)S(1)}, bf16[4,8,8,640]{3,2,1,0:T(8,128)(2,1)S(1)}, u32[]{:S(2)}, u32[]{:S(2)}) collective-permute-start(bf16[4,8,8,640]{3,2,1,0:T(8,128)(2,1)S(1)} %get-tuple-element.50), channel_id=1, source_target_pairs={{0,4},{2,18},{1,5},{3,19},{4,0},{6,22},{5,1},{7,23},{8,12},{10,26}... | collective-permute-start | bytes 983048 | tf_op jit(solution)/shard_map/ppermute | solution.py:64
  12.1 9.4 %collective-permute-start.3 = (bf16[4,8,8,640]{3,2,1,0:T(8,128)(2,1)S(1)}, bf16[4,8,8,640]{3,2,1,0:T(8,128)(2,1)S(1)}, u32[]{:S(2)}, u32[]{:S(2)}) collective-permute-start(bf16[4,8,8,640]{3,2,1,0:T(8,128)(2,1)S(1)} %get-tuple-element.51), channel_id=1, source_target_pairs={{0,5},{2,26},{1,0},{3,27},{4,1},{6,30},{5,4},{7,31},{8,13},{10,2},... | collective-permute-start | bytes 983048 | tf_op jit(solution)/shard_map/ppermute | solution.py:64
  22.6 57.6 %copy-start.5 = (f32[64,1024]{1,0:T(8,128)S(1)}, f32[64,1024]{1,0:T(8,128)}, u32[]{:S(2)}) copy-start(f32[64,1024]{1,0:T(8,128)} %refs_10_.3) | copy-start | bytes 786436
  22.6 19.7 %all-to-all-start = ((f16[32,8,640]{2,1,0:T(8,128)(2,1)}), f16[32,8,640]{2,1,0:T(8,128)(2,1)S(1)}, u32[]{:S(2)}, u32[]{:S(2)}) async-start(f16[32,8,640]{2,1,0:T(8,128)(2,1)} %convert_element_type.15), calls=%async_computation | async-start | bytes 655360 | tf_op jit(solution)/shard_map/all_to_all | solution.py:466
  42.3 37.9 %copy-start.2 = (f32[1024,512]{1,0:T(8,128)S(1)}, f32[1024,512]{1,0:T(8,128)}, u32[]{:S(2)}) copy-start(f32[1024,512]{1,0:T(8,128)} %refs_7_.3) | copy-start | bytes 6291460
  42.7 37.5 %copy-start.4 = (f32[64,1024]{1,0:T(8,128)S(1)}, f32[64,1024]{1,0:T(8,128)}, u32[]{:S(2)}) copy-start(f32[64,1024]{1,0:T(8,128)} %refs_9_.3) | copy-start | bytes 786436
  42.7 37.5 %copy-start = (f32[1024,512]{1,0:T(8,128)S(1)}, f32[1024,512]{1,0:T(8,128)}, u32[]{:S(2)}) copy-start(f32[1024,512]{1,0:T(8,128)} %refs_5_.3) | copy-start | bytes 6291460
  42.7 37.4 %copy-start.1 = (f32[1024,512]{1,0:T(8,128)S(1)}, f32[1024,512]{1,0:T(8,128)}, u32[]{:S(2)}) copy-start(f32[1024,512]{1,0:T(8,128)} %refs_6_.3) | copy-start | bytes 6291460
  42.8 37.4 %copy-start.3 = (f32[64,1024]{1,0:T(8,128)S(1)}, f32[64,1024]{1,0:T(8,128)}, u32[]{:S(2)}) copy-start(f32[64,1024]{1,0:T(8,128)} %refs_8_.3) | copy-start | bytes 786436
  42.8 37.4 %copy-start.6 = (f32[1024]{0:T(1024)S(1)}, f32[1024]{0:T(1024)}, u32[]{:S(2)}) copy-start(f32[1024]{0:T(1024)} %param.21) | copy-start | bytes 12292
  42.8 37.4 %copy-start.7 = (f32[1024]{0:T(1024)S(1)}, f32[1024]{0:T(1024)}, u32[]{:S(2)}) copy-start(f32[1024]{0:T(1024)} %param.22) | copy-start | bytes 12292
  42.8 37.4 %copy-start.8 = (f32[1024]{0:T(1024)S(1)}, f32[1024]{0:T(1024)}, u32[]{:S(2)}) copy-start(f32[1024]{0:T(1024)} %param.23) | copy-start | bytes 12292
  70.9 7.2 %collective-permute-start.4 = (f32[8,128]{1,0:T(8,128)S(1)}, f32[8,128]{1,0:T(8,128)S(1)}, u32[]{:S(2)}, u32[]{:S(2)}) collective-permute-start(f32[8,128]{1,0:T(8,128)S(1)} %shard_map.216.refs_0_), channel_id=1, source_target_pairs={{0,2},{2,0},{1,3},{3,1},{4,6},{6,4},{5,7},{7,5},{8,10},{10,8},{9,1... | collective-permute-start | bytes 12296 | tf_op jit(solution)/shard_map/ppermute | solution.py:64
  76.4 2.5 %collective-permute-start.5 = (f32[8,128]{1,0:T(8,128)S(1)}, f32[8,128]{1,0:T(8,128)S(1)}, u32[]{:S(2)}, u32[]{:S(2)}) collective-permute-start(f32[8,128]{1,0:T(8,128)S(1)} %shard_map.216.refs_0_), channel_id=1, source_target_pairs={{0,1},{2,3},{1,0},{3,2},{4,5},{6,7},{5,4},{7,6},{8,9},{10,11},{9,8... | collective-permute-start | bytes 12296 | tf_op jit(solution)/shard_map/ppermute | solution.py:64
  76.4 3.3 %collective-permute-start.6 = (f32[8,128]{1,0:T(8,128)S(1)}, f32[8,128]{1,0:T(8,128)S(1)}, u32[]{:S(2)}, u32[]{:S(2)}) collective-permute-start(f32[8,128]{1,0:T(8,128)S(1)} %shard_map.216.refs_0_), channel_id=1, source_target_pairs={{0,3},{2,1},{1,2},{3,0},{4,7},{6,5},{5,6},{7,4},{8,11},{10,9},{9,1... | collective-permute-start | bytes 12296 | tf_op jit(solution)/shard_map/ppermute | solution.py:64
  79.7 4.6 %collective-permute-start.7 = (f16[64,8,640]{2,1,0:T(8,128)(2,1)S(1)}, f16[64,8,640]{2,1,0:T(8,128)(2,1)S(1)}, u32[]{:S(2)}, u32[]{:S(2)}) collective-permute-start(f16[64,8,640]{2,1,0:T(8,128)(2,1)S(1)} %all_to_all.10), channel_id=1, source_target_pairs={{0,2},{2,0},{1,3},{3,1},{4,6},{6,4},{5,7},{7,5},{8,10},{10,8},{9,1... | collective-permute-start | bytes 1966088 | tf_op jit(solution)/shard_map/ppermute | solution.py:64
  81.9 10.6 %collective-permute-start.8 = (bf16[296,512]{1,0:T(8,128)(2,1)S(1)}, bf16[296,512]{1,0:T(8,128)(2,1)S(1)}, u32[]{:S(2)}, u32[]{:S(2)}) collective-permute-start(bf16[296,512]{1,0:T(8,128)(2,1)S(1)} %get-tuple-element.59.refs_16_), channel_id=1, source_target_pairs={{0,1},{2,3},{1,0},{3,2},{4,5},{6,7},{5,4},{7,6},{8,9},{10,11},{9,8... | collective-permute-start | bytes 909320 | tf_op jit(solution)/shard_map/ppermute | solution.py:64
  83.1 9.4 %collective-permute-start.9 = (bf16[288,512]{1,0:T(8,128)(2,1)S(1)}, bf16[288,512]{1,0:T(8,128)(2,1)S(1)}, u32[]{:S(2)}, u32[]{:S(2)}) collective-permute-start(bf16[288,512]{1,0:T(8,128)(2,1)S(1)} %get-tuple-element.60.refs_17_), channel_id=1, source_target_pairs={{0,5},{2,7},{1,4},{3,6},{4,1},{6,3},{5,0},{7,2},{8,13},{10,15},{9,... | collective-permute-start | bytes 884744 | tf_op jit(solution)/shard_map/ppermute | solution.py:64
  92.5 2.9 %collective-permute-start.10 = (bf16[296,512]{1,0:T(8,128)(2,1)S(1)}, bf16[296,512]{1,0:T(8,128)(2,1)S(1)}, u32[]{:S(2)}, u32[]{:S(2)}) collective-permute-start(bf16[296,512]{1,0:T(8,128)(2,1)S(1)} %collective-permute-done.8.far0), channel_id=1, source_target_pairs={{0,2},{2,0},{1,3},{3,1},{4,6},{6,4},{5,7},{7,5},{8,10},{10,8},{9,1... | collective-permute-start | bytes 909320 | tf_op jit(solution)/shard_map/ppermute | solution.py:64
  93.8 1.6 %collective-permute-start.11 = (bf16[288,512]{1,0:T(8,128)(2,1)S(1)}, bf16[288,512]{1,0:T(8,128)(2,1)S(1)}, u32[]{:S(2)}, u32[]{:S(2)}) collective-permute-start(bf16[288,512]{1,0:T(8,128)(2,1)S(1)} %collective-permute-done.9.far1), channel_id=1, source_target_pairs={{0,2},{2,0},{1,3},{3,1},{4,6},{6,4},{5,7},{7,5},{8,10},{10,8},{9,1... | collective-permute-start | bytes 884744 | tf_op jit(solution)/shard_map/ppermute | solution.py:64

commit v8 on v7

--- a/solution.py
+++ b/solution.py
@@ -43,8 +43,8 @@
 def along(shift):
     def target(z, y, x, c):
         if c == 0:
-            return z, y, (x + shift) % 4, c
-        return z, (y + shift) % 4, x, c
+            return z, y, x ^ shift, c
+        return z, y ^ shift, x, c
 
     return permutation(target)
 
@@ -87,7 +87,7 @@
     t, p = where_ref[0], where_ref[1]
     copies = []
     for i in range(16):
-        half, group = group_of(t, (p + i // 4) % 4, i % 4)
+        half, group = group_of(t, p ^ (i // 4), i % 4)
         rows = pl.ds(pl.multiple_of((half * 16 + group) * 64, 64), 64)
         copies.append(pltpu.make_async_copy(key_ref.at[:, rows], keys.at[i], sems.at[i]))
         rows = pl.ds(pl.multiple_of(group // 2 * 8, 8), 8)
@@ -114,7 +114,7 @@
             turned = jnp.concatenate([line[:, 64:], line[:, :64]], axis=1)
             tiles[half, z] = jnp.where(row == 0, line, jnp.where(row == 1, turned, 0.0))
     for i in range(16):
-        half, group = group_of(t, (p + i // 4) % 4, i % 4)
+        half, group = group_of(t, p ^ (i // 4), i % 4)
         copies[2 * i].wait()
         copies[2 * i + 1].wait()
         key = keys[i, 0].astype(jnp.float32) + keys[i, 1].astype(jnp.float32)
@@ -228,7 +228,7 @@
     for b in range(64):
         tile = blocks_ref[b, :, KEY_WIDTH:]
         digits = tile[6:7] + tile[5:6] * (1.0 / 256.0)
-        totals[b % 2] = totals[b % 2] + digits * jnp.exp2(2.0 * tile[7:8] + 30.0)
+        totals[b // 8 % 2] = totals[b // 8 % 2] + digits * jnp.exp2(2.0 * tile[7:8] + 30.0)
     lane = lax.broadcasted_iota(jnp.int32, (1, LANES), 1)
     total = jnp.where(lane == 64, totals[0], 0.0) + jnp.where(lane == 0, totals[1], 0.0)
     out_ref[...] = jnp.broadcast_to(jnp.sum(total, axis=1, keepdims=True), (8, LANES))
@@ -266,7 +266,7 @@
     row = lax.broadcasted_iota(jnp.int32, (8, LANES), 0)
     scaled = jnp.zeros((8, LANES), jnp.float32)
     for z in range(8):
-        tile = blocks_ref[z, :, KEY_WIDTH:]
+        tile = blocks_ref[z * 8, :, KEY_WIDTH:]
         scaled = jnp.where(row == z, gain_line(tile * (scale_of(tile, z % 2) * factor), z), scaled)
     new = adamw(*[gain[...] for gain in gain_ins], scaled, 0.0)
     for a in range(3):
@@ -276,10 +276,11 @@
         message, at = messages[g // 4], g % 4
         tiles = []
         for z in range(8):
-            tile = blocks_ref[g * 8 + z, :, KEY_WIDTH:]
+            b = z * 8 + g % 4 * 2 + g // 4
+            tile = blocks_ref[b, :, KEY_WIDTH:]
             scale = scale_of(tile, z % 2) * factor
             tiles.append(tile * scale)
-            scaled = blocks_ref[g * 8 + z, :, :KEY_WIDTH] * jnp.concatenate([scale] * 4, axis=1)
+            scaled = blocks_ref[b, :, :KEY_WIDTH] * jnp.concatenate([scale] * 4, axis=1)
             rows = pl.ds(g * 64 + z * 8, 8)
             old = pl.ds(pl.multiple_of(t * 512 + g * 64 + z * 8, 8), 8)
             new = adamw(*[key[old] for key in key_ins], scaled, 0.1)
@@ -461,7 +462,7 @@
     kept = pack(core, first_place, grads)
     parts = in_vmem(add_pair, [kept, got], [((4, 8, 8, ROW), jnp.bfloat16)] * 4)
     states = [key_master, key_first, key_second, router_master, router_first, router_second]
-    parts = [parts[0]] + [send(parts[k], along(k)) for k in (1, 2, 3)]
+    parts = [parts[0]] + [send(parts[k], along(k)) for k in (2, 1, 3)]
     [code] = in_vmem(sum_encoded, parts, [((32, 8, ROW), jnp.float32)], [z])
     code = lax.all_to_all(
         code.astype(jnp.float16), ALL, 0, 0, axis_index_groups=SECOND_GROUPS, tiled=True
@@ -469,7 +470,7 @@
     [code] = in_vmem(encode, [code.astype(jnp.float32)], [((8, ROW), jnp.float32)], [z & 1])
     parts = lax.all_to_all(
         jnp.broadcast_to(code.astype(jnp.float16)[None], (64, 8, ROW)),
-        ("xh", "y", "z"),
+        ("z", "y", "xh"),
         0,
         0,
         tiled=True,

time: 98.4 us -> 97.5 us (level)
  starting transfers between devices: 27.7 us -> 26.4 us
    ppermute x12, starting transfers between devices: 18 us -> 16.6 us  [send(): return lax.ppermute(x, ALL, pairs)]
  transfers between devices with their start and end apart: 13 -> 13, of which waited for: 7 -> 8; matrix products, arithmetic and copies ran while one was open for 0% -> 0% of each run, Pallas kernels for 9% -> 9%
where the time goes in v8:
time: 97.5 us; the launch traced here: 97.1 us
  blocking collectives  27.4 us (28%)
  starting transfers between devices  26.4 us (27%)
  waiting for transfers between devices  25.6 us (26%)
  Pallas kernels  15.3 us (16%)
  other arithmetic  1.29 us (1%)
  between operations  1.03 us (1%)
    all_to_all x1, blocking collectives, on_device(): lax.all_to_all(jnp.broadcast_to(code.astype(jnp.float16)[None], (64, 8, R...  27.4 us
    ppermute x12, starting transfers between devices, send(): return lax.ppermute(x, ALL, pairs)  16.6 us
    ppermute x12, waiting for transfers between devices, send(): return lax.ppermute(x, ALL, pairs)  15.6 us
    all_to_all x1, waiting for transfers between devices, on_device(): lax.all_to_all(code.astype(jnp.float16), ALL, 0, 0, axis_index_groups=SEC...  10 us
    all_to_all x1, starting transfers between devices, on_device(): lax.all_to_all(code.astype(jnp.float16), ALL, 0, 0, axis_index_groups=SEC...  9.82 us
    pallas_call x2, Pallas kernels, pack(): pl.pallas_call(pack_local, in_specs=[pl.BlockSpec(memory_space=pltpu.SMEM...  5.31 us
    pallas_call x1, Pallas kernels, updated(): pl.pallas_call(update_second, in_specs=[IN_SMEM] + [IN_VMEM] * 18, out_sp...  4.78 us
    pallas_call x1, Pallas kernels, updated(): pl.pallas_call(write_received, in_specs=[IN_SMEM] + [IN_VMEM] * 10 + [IN_...  2.44 us
  transfers between devices with their start and end apart: 13, of which 8 were waited for; matrix products, arithmetic and copies ran while one was open for 0% of the time, Pallas kernels for 9%

profile of v8, /device:TPU:1, one launch (start us, length us, event | category | flops | bytes accessed | tf_op | source)
XLA Modules:
  0.0 97.1 jit_solution(11873933978989379173)
XLA Ops:
  0.7 2.7 %shard_map.212 = bf16[4,4,8,8,640]{4,3,2,1,0:T(8,128)(2,1)S(1)} custom-call(s32[2]{0:T(128)S(1)} %pad_add_fusion.1.where_ref, bf16[2,2048,512]{2,1,0:T(8,128)(2,1)} %bitcast.23, bf16[2,64,2048]{2,1,0:T(8,128)(2,1)} %bitcast.25, bf16[2,2048]{1,0:T(2,128)(2,1)} %bitcast.27), custom_call_target="tpu_custom_call" | custom-call | tf_op jit(solution)/shard_map/pallas_call | solution.py:135
  3.4 3.3 %collective-permute-start = (bf16[4,4,8,8,640]{4,3,2,1,0:T(8,128)(2,1)S(1)}, bf16[4,4,8,8,640]{4,3,2,1,0:T(8,128)(2,1)S(1)}, u32[]{:S(2)}, u32[]{:S(2)}) collective-permute-start(bf16[4,4,8,8,640]{4,3,2,1,0:T(8,128)(2,1)S(1)} %shard_map.212), channel_id=1, source_target_pairs={{0,2},{2,0},{1,3},{3,1},{4,6},{6,4},{5,7},{7,5},{8,10},{10,8},{9,1... | collective-permute-start | bytes 3932168 | tf_op jit(solution)/shard_map/ppermute | solution.py:64
  6.8 2.7 %shard_map.211.kept_ref = bf16[4,4,8,8,640]{4,3,2,1,0:T(8,128)(2,1)S(1)} custom-call(s32[2]{0:T(128)S(1)} %pad_add_fusion.where_ref, bf16[2,2048,512]{2,1,0:T(8,128)(2,1)} %bitcast.24, bf16[2,64,2048]{2,1,0:T(8,128)(2,1)} %bitcast.26, bf16[2,2048]{1,0:T(2,128)(2,1)} %bitcast.28), custom_call_target="tpu_custom_call" | custom-call | tf_op jit(solution)/shard_map/pallas_call | solution.py:135
  9.5 0.3 shard_map.213
  9.8 1.3 %collective-permute-start.1 = (bf16[4,8,8,640]{3,2,1,0:T(8,128)(2,1)S(1)}, bf16[4,8,8,640]{3,2,1,0:T(8,128)(2,1)S(1)}, u32[]{:S(2)}, u32[]{:S(2)}) collective-permute-start(bf16[4,8,8,640]{3,2,1,0:T(8,128)(2,1)S(1)} %get-tuple-element.49), channel_id=1, source_target_pairs={{0,4},{2,18},{1,5},{3,19},{4,0},{6,22},{5,1},{7,23},{8,12},{10,26}... | collective-permute-start | bytes 983048 | tf_op jit(solution)/shard_map/ppermute | solution.py:64
  11.1 0.4 collective-permute-start.2
  11.5 1.7 %collective-permute-start.3 = (bf16[4,8,8,640]{3,2,1,0:T(8,128)(2,1)S(1)}, bf16[4,8,8,640]{3,2,1,0:T(8,128)(2,1)S(1)}, u32[]{:S(2)}, u32[]{:S(2)}) collective-permute-start(bf16[4,8,8,640]{3,2,1,0:T(8,128)(2,1)S(1)} %get-tuple-element.51), channel_id=1, source_target_pairs={{0,5},{2,26},{1,4},{3,27},{4,1},{6,30},{5,0},{7,31},{8,13},{10,18}... | collective-permute-start | bytes 983048 | tf_op jit(solution)/shard_map/ppermute | solution.py:64
  13.1 4.5 %collective-permute-done.1.refs_1_ = bf16[4,8,8,640]{3,2,1,0:T(8,128)(2,1)S(1)} collective-permute-done((bf16[4,8,8,640]{3,2,1,0:T(8,128)(2,1)S(1)}, bf16[4,8,8,640]{3,2,1,0:T(8,128)(2,1)S(1)}, u32[]{:S(2)}, u32[]{:S(2)}) %collective-permute-start.1) | collective-permute-done | bytes 327712 | tf_op jit(solution)/shard_map/ppermute | solution.py:64
  17.7 2.1 %collective-permute-done.2.refs_2_ = bf16[4,8,8,640]{3,2,1,0:T(8,128)(2,1)S(1)} collective-permute-done((bf16[4,8,8,640]{3,2,1,0:T(8,128)(2,1)S(1)}, bf16[4,8,8,640]{3,2,1,0:T(8,128)(2,1)S(1)}, u32[]{:S(2)}, u32[]{:S(2)}) %collective-permute-start.2) | collective-permute-done | bytes 327712 | tf_op jit(solution)/shard_map/ppermute | solution.py:64
  19.7 1.4 %collective-permute-done.3.refs_3_ = bf16[4,8,8,640]{3,2,1,0:T(8,128)(2,1)S(1)} collective-permute-done((bf16[4,8,8,640]{3,2,1,0:T(8,128)(2,1)S(1)}, bf16[4,8,8,640]{3,2,1,0:T(8,128)(2,1)S(1)}, u32[]{:S(2)}, u32[]{:S(2)}) %collective-permute-start.3) | collective-permute-done | bytes 327712 | tf_op jit(solution)/shard_map/ppermute | solution.py:64
  21.1 0.3 shard_map.214
  21.5 0.8 convert_element_type.15
  22.2 9.8 %all-to-all-start = ((f16[32,8,640]{2,1,0:T(8,128)(2,1)}), f16[32,8,640]{2,1,0:T(8,128)(2,1)S(1)}, u32[]{:S(2)}, u32[]{:S(2)}) async-start(f16[32,8,640]{2,1,0:T(8,128)(2,1)} %convert_element_type.15), calls=%async_computation | async-start | bytes 655360 | tf_op jit(solution)/shard_map/all_to_all | solution.py:467
  32.1 10.0 %all-to-all-done = f16[32,8,640]{2,1,0:T(8,128)(2,1)S(1)} async-done(((f16[32,8,640]{2,1,0:T(8,128)(2,1)}), f16[32,8,640]{2,1,0:T(8,128)(2,1)S(1)}, u32[]{:S(2)}, u32[]{:S(2)}) %all-to-all-start) | async-done | bytes 327712 | tf_op jit(solution)/shard_map/all_to_all | solution.py:467
  42.1 0.3 shard_map.215
  42.6 27.4 %all_to_all.10 = f16[64,8,640]{2,1,0:T(8,128)(2,1)S(1)} all-to-all(f16[64,8,640]{2,1,0:T(8,128)(2,1)S(1)} %broadcast_in_dim.2), channel_id=1, replica_groups=mesh['z'=8,'y'=4,'xh'=2,'c'=2,'xl'=2] {'z','y','xh'}, dimensions={0} | all-to-all | bytes 1310720 | tf_op jit(solution)/shard_map/all_to_all | solution.py:471
  70.0 0.1 convert_element_type.18.blocks_ref.refs_4_
  70.1 0.2 shard_map.216.refs_0_
  70.3 5.2 %collective-permute-start.4 = (f32[8,128]{1,0:T(8,128)S(1)}, f32[8,128]{1,0:T(8,128)S(1)}, u32[]{:S(2)}, u32[]{:S(2)}) collective-permute-start(f32[8,128]{1,0:T(8,128)S(1)} %shard_map.216.refs_0_), channel_id=1, source_target_pairs={{0,2},{2,0},{1,3},{3,1},{4,6},{6,4},{5,7},{7,5},{8,10},{10,8},{9,1... | collective-permute-start | bytes 12296 | tf_op jit(solution)/shard_map/ppermute | solution.py:64
  75.5 0.1 collective-permute-start.5
  75.6 1.6 %collective-permute-start.6 = (f32[8,128]{1,0:T(8,128)S(1)}, f32[8,128]{1,0:T(8,128)S(1)}, u32[]{:S(2)}, u32[]{:S(2)}) collective-permute-start(f32[8,128]{1,0:T(8,128)S(1)} %shard_map.216.refs_0_), channel_id=1, source_target_pairs={{0,3},{2,1},{1,2},{3,0},{4,7},{6,5},{5,6},{7,4},{8,11},{10,9},{9,1... | collective-permute-start | bytes 12296 | tf_op jit(solution)/shard_map/ppermute | solution.py:64
  77.2 0.7 collective-permute-done.5.refs_2_
  78.0 0.8 collective-permute-done.6.refs_3_
  78.8 0.4 collective-permute-start.7
  79.3 1.6 %shard_map.217 = (f32[3,512,512]{2,1,0:T(8,128)S(1)}, f32[3,32,1024]{2,1,0:T(8,128)S(1)}, f32[8,128]{1,0:T(8,128)S(1)}, f32[8,128]{1,0:T(8,128)S(1)}, f32[8,128]...) custom-call(s32[2]{0:T(128)S(1)} %pad_add_fusion.2.where_ref, ...), custom_call_target="tpu_custom_call" | custom-call | flops 7000000 | bytes 8000000 | tf_op jit(solution)/shard_map/pallas_call | solution.py:401
  80.9 1.3 %collective-permute-start.8 = (bf16[296,512]{1,0:T(8,128)(2,1)S(1)}, bf16[296,512]{1,0:T(8,128)(2,1)S(1)}, u32[]{:S(2)}, u32[]{:S(2)}) collective-permute-start(bf16[296,512]{1,0:T(8,128)(2,1)S(1)} %get-tuple-element.59.refs_16_), channel_id=1, source_target_pairs={{0,1},{2,3},{1,0},{3,2},{4,5},{6,7},{5,4},{7,6},{8,9},{10,11},{9,8... | collective-permute-start | bytes 909320 | tf_op jit(solution)/shard_map/ppermute | solution.py:64
  82.3 0.1 convert_element_type.19.refs_4_
  82.4 4.8 %shard_map.218 = (f32[1024,512]{1,0:T(8,128)}, f32[1024,512]{1,0:T(8,128)}, f32[1024,512]{1,0:T(8,128)}, f32[64,1024]{1,0:T(8,128)}, f32[64,1024]{1,0:T(8,128)},...) custom-call(s32[2]{0:T(128)S(1)} %pad_add_fusion.3.where_ref, ...), custom_call_target="tpu_custom_call" | custom-call | flops 7000000 | bytes 8000000 | tf_op jit(solution)/shard_map/pallas_call | solution.py:413
  87.2 4.4 %collective-permute-done.9.far1 = bf16[288,512]{1,0:T(8,128)(2,1)S(1)} collective-permute-done((bf16[288,512]{1,0:T(8,128)(2,1)S(1)}, bf16[288,512]{1,0:T(8,128)(2,1)S(1)}, u32[]{:S(2)}, u32[]{:S(2)}) %collective-permute-start.9) | collective-permute-done | bytes 294944 | tf_op jit(solution)/shard_map/ppermute | solution.py:64
  91.6 1.3 %collective-permute-start.10 = (bf16[296,512]{1,0:T(8,128)(2,1)S(1)}, bf16[296,512]{1,0:T(8,128)(2,1)S(1)}, u32[]{:S(2)}, u32[]{:S(2)}) collective-permute-start(bf16[296,512]{1,0:T(8,128)(2,1)S(1)} %collective-permute-done.8.far0), channel_id=1, source_target_pairs={{0,2},{2,0},{1,3},{3,1},{4,6},{6,4},{5,7},{7,5},{8,10},{10,8},{9,1... | collective-permute-start | bytes 909320 | tf_op jit(solution)/shard_map/ppermute | solution.py:64
  92.8 1.6 %collective-permute-done.11.near1 = bf16[288,512]{1,0:T(8,128)(2,1)S(1)} collective-permute-done((bf16[288,512]{1,0:T(8,128)(2,1)S(1)}, bf16[288,512]{1,0:T(8,128)(2,1)S(1)}, u32[]{:S(2)}, u32[]{:S(2)}) %collective-permute-start.11) | collective-permute-done | bytes 294944 | tf_op jit(solution)/shard_map/ppermute | solution.py:64
  94.5 2.4 %shard_map.219 = (bf16[2048,512]{1,0:T(8,128)(2,1)}, bf16[64,2048]{1,0:T(8,128)(2,1)}, f32[8,128]{1,0:T(8,128)}, f32[8,128]{1,0:T(8,128)}, f32[8,128]{1,0:T(8,128)}, /*index=5*/bf16[16,128]{1,0:T(8,128)(2,1)}) custom-call(s32[2]{0:T(128)S(1)} %pad_add_fusion.2.where_ref, ...), custom_call_target="tpu_custom_call", output_to_operand_aliasing={{0}: (11, {}), {1}: (12, {})} | custom-call | tf_op jit(solution)/shard_map/pallas_call | solution.py:427
  (32 shorter events, 0.5 us)
Async XLA Ops:
  3.4 6.1 %collective-permute-start = (bf16[4,4,8,8,640]{4,3,2,1,0:T(8,128)(2,1)S(1)}, bf16[4,4,8,8,640]{4,3,2,1,0:T(8,128)(2,1)S(1)}, u32[]{:S(2)}, u32[]{:S(2)}) collective-permute-start(bf16[4,4,8,8,640]{4,3,2,1,0:T(8,128)(2,1)S(1)} %shard_map.212), channel_id=1, source_target_pairs={{0,2},{2,0},{1,3},{3,1},{4,6},{6,4},{5,7},{7,5},{8,10},{10,8},{9,1... | collective-permute-start | bytes 3932168 | tf_op jit(solution)/shard_map/ppermute | solution.py:64
  9.8 7.9 %collective-permute-start.1 = (bf16[4,8,8,640]{3,2,1,0:T(8,128)(2,1)S(1)}, bf16[4,8,8,640]{3,2,1,0:T(8,128)(2,1)S(1)}, u32[]{:S(2)}, u32[]{:S(2)}) collective-permute-start(bf16[4,8,8,640]{3,2,1,0:T(8,128)(2,1)S(1)} %get-tuple-element.49), channel_id=1, source_target_pairs={{0,4},{2,18},{1,5},{3,19},{4,0},{6,22},{5,1},{7,23},{8,12},{10,26}... | collective-permute-start | bytes 983048 | tf_op jit(solution)/shard_map/ppermute | solution.py:64
  11.1 8.7 %collective-permute-start.2 = (bf16[4,8,8,640]{3,2,1,0:T(8,128)(2,1)S(1)}, bf16[4,8,8,640]{3,2,1,0:T(8,128)(2,1)S(1)}, u32[]{:S(2)}, u32[]{:S(2)}) collective-permute-start(bf16[4,8,8,640]{3,2,1,0:T(8,128)(2,1)S(1)} %get-tuple-element.50), channel_id=1, source_target_pairs={{0,1},{2,10},{1,0},{3,11},{4,5},{6,14},{5,4},{7,15},{8,9},{10,2},{... | collective-permute-start | bytes 983048 | tf_op jit(solution)/shard_map/ppermute | solution.py:64
  11.5 9.7 %collective-permute-start.3 = (bf16[4,8,8,640]{3,2,1,0:T(8,128)(2,1)S(1)}, bf16[4,8,8,640]{3,2,1,0:T(8,128)(2,1)S(1)}, u32[]{:S(2)}, u32[]{:S(2)}) collective-permute-start(bf16[4,8,8,640]{3,2,1,0:T(8,128)(2,1)S(1)} %get-tuple-element.51), channel_id=1, source_target_pairs={{0,5},{2,26},{1,4},{3,27},{4,1},{6,30},{5,0},{7,31},{8,13},{10,18}... | collective-permute-start | bytes 983048 | tf_op jit(solution)/shard_map/ppermute | solution.py:64
  22.2 57.0 %copy-start.5 = (f32[64,1024]{1,0:T(8,128)S(1)}, f32[64,1024]{1,0:T(8,128)}, u32[]{:S(2)}) copy-start(f32[64,1024]{1,0:T(8,128)} %refs_10_.3) | copy-start | bytes 786436
  22.2 19.8 %all-to-all-start = ((f16[32,8,640]{2,1,0:T(8,128)(2,1)}), f16[32,8,640]{2,1,0:T(8,128)(2,1)S(1)}, u32[]{:S(2)}, u32[]{:S(2)}) async-start(f16[32,8,640]{2,1,0:T(8,128)(2,1)} %convert_element_type.15), calls=%async_computation | async-start | bytes 655360 | tf_op jit(solution)/shard_map/all_to_all | solution.py:467
  42.1 37.2 %copy-start.2 = (f32[1024,512]{1,0:T(8,128)S(1)}, f32[1024,512]{1,0:T(8,128)}, u32[]{:S(2)}) copy-start(f32[1024,512]{1,0:T(8,128)} %refs_7_.3) | copy-start | bytes 6291460
  42.5 36.8 %copy-start.4 = (f32[64,1024]{1,0:T(8,128)S(1)}, f32[64,1024]{1,0:T(8,128)}, u32[]{:S(2)}) copy-start(f32[64,1024]{1,0:T(8,128)} %refs_9_.3) | copy-start | bytes 786436
  42.6 36.7 %copy-start = (f32[1024,512]{1,0:T(8,128)S(1)}, f32[1024,512]{1,0:T(8,128)}, u32[]{:S(2)}) copy-start(f32[1024,512]{1,0:T(8,128)} %refs_5_.3) | copy-start | bytes 6291460
  42.6 36.7 %copy-start.1 = (f32[1024,512]{1,0:T(8,128)S(1)}, f32[1024,512]{1,0:T(8,128)}, u32[]{:S(2)}) copy-start(f32[1024,512]{1,0:T(8,128)} %refs_6_.3) | copy-start | bytes 6291460
  42.6 36.7 %copy-start.3 = (f32[64,1024]{1,0:T(8,128)S(1)}, f32[64,1024]{1,0:T(8,128)}, u32[]{:S(2)}) copy-start(f32[64,1024]{1,0:T(8,128)} %refs_8_.3) | copy-start | bytes 786436
  42.6 36.7 %copy-start.6 = (f32[1024]{0:T(1024)S(1)}, f32[1024]{0:T(1024)}, u32[]{:S(2)}) copy-start(f32[1024]{0:T(1024)} %param.21) | copy-start | bytes 12292
  42.6 36.7 %copy-start.7 = (f32[1024]{0:T(1024)S(1)}, f32[1024]{0:T(1024)}, u32[]{:S(2)}) copy-start(f32[1024]{0:T(1024)} %param.22) | copy-start | bytes 12292
  42.6 36.7 %copy-start.8 = (f32[1024]{0:T(1024)S(1)}, f32[1024]{0:T(1024)}, u32[]{:S(2)}) copy-start(f32[1024]{0:T(1024)} %param.23) | copy-start | bytes 12292
  70.3 7.0 %collective-permute-start.4 = (f32[8,128]{1,0:T(8,128)S(1)}, f32[8,128]{1,0:T(8,128)S(1)}, u32[]{:S(2)}, u32[]{:S(2)}) collective-permute-start(f32[8,128]{1,0:T(8,128)S(1)} %shard_map.216.refs_0_), channel_id=1, source_target_pairs={{0,2},{2,0},{1,3},{3,1},{4,6},{6,4},{5,7},{7,5},{8,10},{10,8},{9,1... | collective-permute-start | bytes 12296 | tf_op jit(solution)/shard_map/ppermute | solution.py:64
  75.5 2.5 %collective-permute-start.5 = (f32[8,128]{1,0:T(8,128)S(1)}, f32[8,128]{1,0:T(8,128)S(1)}, u32[]{:S(2)}, u32[]{:S(2)}) collective-permute-start(f32[8,128]{1,0:T(8,128)S(1)} %shard_map.216.refs_0_), channel_id=1, source_target_pairs={{0,1},{2,3},{1,0},{3,2},{4,5},{6,7},{5,4},{7,6},{8,9},{10,11},{9,8... | collective-permute-start | bytes 12296 | tf_op jit(solution)/shard_map/ppermute | solution.py:64
  75.6 3.2 %collective-permute-start.6 = (f32[8,128]{1,0:T(8,128)S(1)}, f32[8,128]{1,0:T(8,128)S(1)}, u32[]{:S(2)}, u32[]{:S(2)}) collective-permute-start(f32[8,128]{1,0:T(8,128)S(1)} %shard_map.216.refs_0_), channel_id=1, source_target_pairs={{0,3},{2,1},{1,2},{3,0},{4,7},{6,5},{5,6},{7,4},{8,11},{10,9},{9,1... | collective-permute-start | bytes 12296 | tf_op jit(solution)/shard_map/ppermute | solution.py:64
  78.8 3.5 %collective-permute-start.7 = (f16[64,8,640]{2,1,0:T(8,128)(2,1)S(1)}, f16[64,8,640]{2,1,0:T(8,128)(2,1)S(1)}, u32[]{:S(2)}, u32[]{:S(2)}) collective-permute-start(f16[64,8,640]{2,1,0:T(8,128)(2,1)S(1)} %all_to_all.10), channel_id=1, source_target_pairs={{0,2},{2,0},{1,3},{3,1},{4,6},{6,4},{5,7},{7,5},{8,10},{10,8},{9,1... | collective-permute-start | bytes 1966088 | tf_op jit(solution)/shard_map/ppermute | solution.py:64
  80.9 10.6 %collective-permute-start.8 = (bf16[296,512]{1,0:T(8,128)(2,1)S(1)}, bf16[296,512]{1,0:T(8,128)(2,1)S(1)}, u32[]{:S(2)}, u32[]{:S(2)}) collective-permute-start(bf16[296,512]{1,0:T(8,128)(2,1)S(1)} %get-tuple-element.59.refs_16_), channel_id=1, source_target_pairs={{0,1},{2,3},{1,0},{3,2},{4,5},{6,7},{5,4},{7,6},{8,9},{10,11},{9,8... | collective-permute-start | bytes 909320 | tf_op jit(solution)/shard_map/ppermute | solution.py:64
  82.2 9.4 %collective-permute-start.9 = (bf16[288,512]{1,0:T(8,128)(2,1)S(1)}, bf16[288,512]{1,0:T(8,128)(2,1)S(1)}, u32[]{:S(2)}, u32[]{:S(2)}) collective-permute-start(bf16[288,512]{1,0:T(8,128)(2,1)S(1)} %get-tuple-element.60.refs_17_), channel_id=1, source_target_pairs={{0,5},{2,7},{1,4},{3,6},{4,1},{6,3},{5,0},{7,2},{8,13},{10,15},{9,... | collective-permute-start | bytes 884744 | tf_op jit(solution)/shard_map/ppermute | solution.py:64
  91.6 2.9 %collective-permute-start.10 = (bf16[296,512]{1,0:T(8,128)(2,1)S(1)}, bf16[296,512]{1,0:T(8,128)(2,1)S(1)}, u32[]{:S(2)}, u32[]{:S(2)}) collective-permute-start(bf16[296,512]{1,0:T(8,128)(2,1)S(1)} %collective-permute-done.8.far0), channel_id=1, source_target_pairs={{0,2},{2,0},{1,3},{3,1},{4,6},{6,4},{5,7},{7,5},{8,10},{10,8},{9,1... | collective-permute-start | bytes 909320 | tf_op jit(solution)/shard_map/ppermute | solution.py:64
  92.8 1.6 %collective-permute-start.11 = (bf16[288,512]{1,0:T(8,128)(2,1)S(1)}, bf16[288,512]{1,0:T(8,128)(2,1)S(1)}, u32[]{:S(2)}, u32[]{:S(2)}) collective-permute-start(bf16[288,512]{1,0:T(8,128)(2,1)S(1)} %collective-permute-done.9.far1), channel_id=1, source_target_pairs={{0,2},{2,0},{1,3},{3,1},{4,6},{6,4},{5,7},{7,5},{8,10},{10,8},{9,1... | collective-permute-start | bytes 884744 | tf_op jit(solution)/shard_map/ppermute | solution.py:64

commit v9 on v8

--- a/solution.py
+++ b/solution.py
@@ -228,7 +228,7 @@
     for b in range(64):
         tile = blocks_ref[b, :, KEY_WIDTH:]
         digits = tile[6:7] + tile[5:6] * (1.0 / 256.0)
-        totals[b // 8 % 2] = totals[b // 8 % 2] + digits * jnp.exp2(2.0 * tile[7:8] + 30.0)
+        totals[b % 2] = totals[b % 2] + digits * jnp.exp2(2.0 * tile[7:8] + 30.0)
     lane = lax.broadcasted_iota(jnp.int32, (1, LANES), 1)
     total = jnp.where(lane == 64, totals[0], 0.0) + jnp.where(lane == 0, totals[1], 0.0)
     out_ref[...] = jnp.broadcast_to(jnp.sum(total, axis=1, keepdims=True), (8, LANES))
@@ -266,7 +266,7 @@
     row = lax.broadcasted_iota(jnp.int32, (8, LANES), 0)
     scaled = jnp.zeros((8, LANES), jnp.float32)
     for z in range(8):
-        tile = blocks_ref[z * 8, :, KEY_WIDTH:]
+        tile = blocks_ref[z, :, KEY_WIDTH:]
         scaled = jnp.where(row == z, gain_line(tile * (scale_of(tile, z % 2) * factor), z), scaled)
     new = adamw(*[gain[...] for gain in gain_ins], scaled, 0.0)
     for a in range(3):
@@ -276,7 +276,7 @@
         message, at = messages[g // 4], g % 4
         tiles = []
         for z in range(8):
-            b = z * 8 + g % 4 * 2 + g // 4
+            b = (g % 4 * 2 + g // 4) * 8 + z
             tile = blocks_ref[b, :, KEY_WIDTH:]
             scale = scale_of(tile, z % 2) * factor
             tiles.append(tile * scale)
@@ -468,13 +468,11 @@
         code.astype(jnp.float16), ALL, 0, 0, axis_index_groups=SECOND_GROUPS, tiled=True
     )
     [code] = in_vmem(encode, [code.astype(jnp.float32)], [((8, ROW), jnp.float32)], [z & 1])
-    parts = lax.all_to_all(
-        jnp.broadcast_to(code.astype(jnp.float16)[None], (64, 8, ROW)),
-        ("z", "y", "xh"),
-        0,
-        0,
-        tiled=True,
-    )
+    line = lax.all_to_all(
+        jnp.broadcast_to(code.astype(jnp.float16)[None], (8, 8, ROW)), "z", 0, 0, tiled=True
+    )
+    line = jnp.broadcast_to(line[None], (8, 8, 8, ROW)).reshape(64, 8, ROW)
+    parts = lax.all_to_all(line, ("y", "xh"), 0, 0, tiled=True)
     wide_parts = parts.astype(jnp.float32)
     [squares] = in_vmem(add_squares, [wide_parts], [((8, LANES), jnp.float32)])
     squares = [squares] + [send(squares, to) for to in (SIBLING, PARTNER, PARTNER_SIBLING)]

time: 97.5 us -> 97.1 us (level)
    all_to_all x1 -> x2, blocking collectives: 27.4 us -> 27.4 us  [the longest x1 14.7 us: on_device(): parts = lax.all_to_all(line, ('y', 'xh'), 0, 0, tiled=True)]
where the time goes in v9:
time: 97.1 us; the launch traced here: 96.7 us
  blocking collectives  27.4 us (28%)
  starting transfers between devices  26.1 us (27%)
  waiting for transfers between devices  25.5 us (26%)
  Pallas kernels  15.3 us (16%)
  other arithmetic  1.29 us (1%)
  between operations  1.03 us (1%)
    ppermute x12, starting transfers between devices, send(): return lax.ppermute(x, ALL, pairs)  16.4 us
    ppermute x12, waiting for transfers between devices, send(): return lax.ppermute(x, ALL, pairs)  15.5 us
    all_to_all x1, blocking collectives, on_device(): parts = lax.all_to_all(line, ('y', 'xh'), 0, 0, tiled=True)  14.7 us
    all_to_all x1, blocking collectives, on_device(): lax.all_to_all(jnp.broadcast_to(code.astype(jnp.float16)[None], (8, 8, RO...  12.7 us
    all_to_all x1, waiting for transfers between devices, on_device(): lax.all_to_all(code.astype(jnp.float16), ALL, 0, 0, axis_index_groups=SEC...  10 us
    all_to_all x1, starting transfers between devices, on_device(): lax.all_to_all(code.astype(jnp.float16), ALL, 0, 0, axis_index_groups=SEC...  9.69 us
    pallas_call x2, Pallas kernels, pack(): pl.pallas_call(pack_local, in_specs=[pl.BlockSpec(memory_space=pltpu.SMEM...  5.31 us
    pallas_call x1, Pallas kernels, updated(): pl.pallas_call(update_second, in_specs=[IN_SMEM] + [IN_VMEM] * 18, out_sp...  4.78 us
  transfers between devices with their start and end apart: 13, of which 8 were waited for; matrix products, arithmetic and copies ran while one was open for 0% of the time, Pallas kernels for 9%

profile of v9, /device:TPU:1, one launch (start us, length us, event | category | flops | bytes accessed | tf_op | source)
XLA Modules:
  0.0 96.7 jit_solution(6152317035850612621)
XLA Ops:
  0.7 2.7 %shard_map.212 = bf16[4,4,8,8,640]{4,3,2,1,0:T(8,128)(2,1)S(1)} custom-call(s32[2]{0:T(128)S(1)} %pad_add_fusion.1.where_ref, bf16[2,2048,512]{2,1,0:T(8,128)(2,1)} %bitcast.24, bf16[2,64,2048]{2,1,0:T(8,128)(2,1)} %bitcast.27, bf16[2,2048]{1,0:T(2,128)(2,1)} %bitcast.29), custom_call_target="tpu_custom_call" | custom-call | tf_op jit(solution)/shard_map/pallas_call | solution.py:135
  3.4 3.3 %collective-permute-start = (bf16[4,4,8,8,640]{4,3,2,1,0:T(8,128)(2,1)S(1)}, bf16[4,4,8,8,640]{4,3,2,1,0:T(8,128)(2,1)S(1)}, u32[]{:S(2)}, u32[]{:S(2)}) collective-permute-start(bf16[4,4,8,8,640]{4,3,2,1,0:T(8,128)(2,1)S(1)} %shard_map.212), channel_id=1, source_target_pairs={{0,2},{2,0},{1,3},{3,1},{4,6},{6,4},{5,7},{7,5},{8,10},{10,8},{9,1... | collective-permute-start | bytes 3932168 | tf_op jit(solution)/shard_map/ppermute | solution.py:64
  6.8 2.7 %shard_map.211.kept_ref = bf16[4,4,8,8,640]{4,3,2,1,0:T(8,128)(2,1)S(1)} custom-call(s32[2]{0:T(128)S(1)} %pad_add_fusion.where_ref, bf16[2,2048,512]{2,1,0:T(8,128)(2,1)} %bitcast.25, bf16[2,64,2048]{2,1,0:T(8,128)(2,1)} %bitcast.28, bf16[2,2048]{1,0:T(2,128)(2,1)} %bitcast.30), custom_call_target="tpu_custom_call" | custom-call | tf_op jit(solution)/shard_map/pallas_call | solution.py:135
  9.5 0.3 shard_map.213
  9.8 1.3 %collective-permute-start.1 = (bf16[4,8,8,640]{3,2,1,0:T(8,128)(2,1)S(1)}, bf16[4,8,8,640]{3,2,1,0:T(8,128)(2,1)S(1)}, u32[]{:S(2)}, u32[]{:S(2)}) collective-permute-start(bf16[4,8,8,640]{3,2,1,0:T(8,128)(2,1)S(1)} %get-tuple-element.49), channel_id=1, source_target_pairs={{0,4},{2,18},{1,5},{3,19},{4,0},{6,22},{5,1},{7,23},{8,12},{10,26}... | collective-permute-start | bytes 983048 | tf_op jit(solution)/shard_map/ppermute | solution.py:64
  11.1 0.4 collective-permute-start.2
  11.5 1.7 %collective-permute-start.3 = (bf16[4,8,8,640]{3,2,1,0:T(8,128)(2,1)S(1)}, bf16[4,8,8,640]{3,2,1,0:T(8,128)(2,1)S(1)}, u32[]{:S(2)}, u32[]{:S(2)}) collective-permute-start(bf16[4,8,8,640]{3,2,1,0:T(8,128)(2,1)S(1)} %get-tuple-element.51), channel_id=1, source_target_pairs={{0,5},{2,26},{1,4},{3,27},{4,1},{6,30},{5,0},{7,31},{8,13},{10,18}... | collective-permute-start | bytes 983048 | tf_op jit(solution)/shard_map/ppermute | solution.py:64
  13.1 4.5 %collective-permute-done.1.refs_1_ = bf16[4,8,8,640]{3,2,1,0:T(8,128)(2,1)S(1)} collective-permute-done((bf16[4,8,8,640]{3,2,1,0:T(8,128)(2,1)S(1)}, bf16[4,8,8,640]{3,2,1,0:T(8,128)(2,1)S(1)}, u32[]{:S(2)}, u32[]{:S(2)}) %collective-permute-start.1) | collective-permute-done | bytes 327712 | tf_op jit(solution)/shard_map/ppermute | solution.py:64
  17.7 2.1 %collective-permute-done.2.refs_2_ = bf16[4,8,8,640]{3,2,1,0:T(8,128)(2,1)S(1)} collective-permute-done((bf16[4,8,8,640]{3,2,1,0:T(8,128)(2,1)S(1)}, bf16[4,8,8,640]{3,2,1,0:T(8,128)(2,1)S(1)}, u32[]{:S(2)}, u32[]{:S(2)}) %collective-permute-start.2) | collective-permute-done | bytes 327712 | tf_op jit(solution)/shard_map/ppermute | solution.py:64
  19.7 1.4 %collective-permute-done.3.refs_3_ = bf16[4,8,8,640]{3,2,1,0:T(8,128)(2,1)S(1)} collective-permute-done((bf16[4,8,8,640]{3,2,1,0:T(8,128)(2,1)S(1)}, bf16[4,8,8,640]{3,2,1,0:T(8,128)(2,1)S(1)}, u32[]{:S(2)}, u32[]{:S(2)}) %collective-permute-start.3) | collective-permute-done | bytes 327712 | tf_op jit(solution)/shard_map/ppermute | solution.py:64
  21.1 0.3 shard_map.214
  21.5 0.8 convert_element_type.15
  22.2 9.7 %all-to-all-start = ((f16[32,8,640]{2,1,0:T(8,128)(2,1)}), f16[32,8,640]{2,1,0:T(8,128)(2,1)S(1)}, u32[]{:S(2)}, u32[]{:S(2)}) async-start(f16[32,8,640]{2,1,0:T(8,128)(2,1)} %convert_element_type.15), calls=%async_computation | async-start | bytes 655360 | tf_op jit(solution)/shard_map/all_to_all | solution.py:467
  31.9 10.0 %all-to-all-done = f16[32,8,640]{2,1,0:T(8,128)(2,1)S(1)} async-done(((f16[32,8,640]{2,1,0:T(8,128)(2,1)}), f16[32,8,640]{2,1,0:T(8,128)(2,1)S(1)}, u32[]{:S(2)}, u32[]{:S(2)}) %all-to-all-start) | async-done | bytes 327712 | tf_op jit(solution)/shard_map/all_to_all | solution.py:467
  42.0 0.3 shard_map.215
  42.4 12.7 %all_to_all.15 = f16[8,8,640]{2,1,0:T(8,128)(2,1)S(1)} all-to-all(f16[8,8,640]{2,1,0:T(8,128)(2,1)S(1)} %broadcast_in_dim.4), channel_id=1, replica_groups=mesh['z'=8,'y'=4,'xh'=2,'c'=2,'xl'=2] {'z'}, dimensions={0} | all-to-all | bytes 163840 | tf_op jit(solution)/shard_map/all_to_all | solution.py:471
  55.2 14.7 %all_to_all.16 = f16[64,8,640]{2,1,0:T(8,128)(2,1)S(1)} all-to-all(f16[64,8,640]{2,1,0:T(8,128)(2,1)S(1)} %bitcast.26), channel_id=1, replica_groups=mesh['z'=8,'y'=4,'xh'=2,'c'=2,'xl'=2] {'y','xh'}, dimensions={0} | all-to-all | bytes 1310720 | tf_op jit(solution)/shard_map/all_to_all | solution.py:475
  70.0 0.2 shard_map.216.refs_0_
  70.2 4.9 %collective-permute-start.4 = (f32[8,128]{1,0:T(8,128)S(1)}, f32[8,128]{1,0:T(8,128)S(1)}, u32[]{:S(2)}, u32[]{:S(2)}) collective-permute-start(f32[8,128]{1,0:T(8,128)S(1)} %shard_map.216.refs_0_), channel_id=1, source_target_pairs={{0,2},{2,0},{1,3},{3,1},{4,6},{6,4},{5,7},{7,5},{8,10},{10,8},{9,1... | collective-permute-start | bytes 12296 | tf_op jit(solution)/shard_map/ppermute | solution.py:64
  75.1 0.3 collective-permute-start.5
  75.4 1.4 %collective-permute-start.6 = (f32[8,128]{1,0:T(8,128)S(1)}, f32[8,128]{1,0:T(8,128)S(1)}, u32[]{:S(2)}, u32[]{:S(2)}) collective-permute-start(f32[8,128]{1,0:T(8,128)S(1)} %shard_map.216.refs_0_), channel_id=1, source_target_pairs={{0,3},{2,1},{1,2},{3,0},{4,7},{6,5},{5,6},{7,4},{8,11},{10,9},{9,1... | collective-permute-start | bytes 12296 | tf_op jit(solution)/shard_map/ppermute | solution.py:64
  76.8 0.7 collective-permute-done.5.refs_2_
  77.6 0.9 collective-permute-done.6.refs_3_
  78.4 0.4 collective-permute-start.7
  79.0 1.6 %shard_map.217 = (f32[3,512,512]{2,1,0:T(8,128)S(1)}, f32[3,32,1024]{2,1,0:T(8,128)S(1)}, f32[8,128]{1,0:T(8,128)S(1)}, f32[8,128]{1,0:T(8,128)S(1)}, f32[8,128]...) custom-call(s32[2]{0:T(128)S(1)} %pad_add_fusion.2.where_ref, ...), custom_call_target="tpu_custom_call" | custom-call | flops 7000000 | bytes 8000000 | tf_op jit(solution)/shard_map/pallas_call | solution.py:401
  80.6 1.2 %collective-permute-start.8 = (bf16[296,512]{1,0:T(8,128)(2,1)S(1)}, bf16[296,512]{1,0:T(8,128)(2,1)S(1)}, u32[]{:S(2)}, u32[]{:S(2)}) collective-permute-start(bf16[296,512]{1,0:T(8,128)(2,1)S(1)} %get-tuple-element.59.refs_16_), channel_id=1, source_target_pairs={{0,1},{2,3},{1,0},{3,2},{4,5},{6,7},{5,4},{7,6},{8,9},{10,11},{9,8... | collective-permute-start | bytes 909320 | tf_op jit(solution)/shard_map/ppermute | solution.py:64
  81.8 0.2 collective-permute-start.9
  82.2 4.8 %shard_map.218 = (f32[1024,512]{1,0:T(8,128)}, f32[1024,512]{1,0:T(8,128)}, f32[1024,512]{1,0:T(8,128)}, f32[64,1024]{1,0:T(8,128)}, f32[64,1024]{1,0:T(8,128)},...) custom-call(s32[2]{0:T(128)S(1)} %pad_add_fusion.3.where_ref, ...), custom_call_target="tpu_custom_call" | custom-call | flops 7000000 | bytes 8000000 | tf_op jit(solution)/shard_map/pallas_call | solution.py:413
  87.0 4.2 %collective-permute-done.9.far1 = bf16[288,512]{1,0:T(8,128)(2,1)S(1)} collective-permute-done((bf16[288,512]{1,0:T(8,128)(2,1)S(1)}, bf16[288,512]{1,0:T(8,128)(2,1)S(1)}, u32[]{:S(2)}, u32[]{:S(2)}) %collective-permute-start.9) | collective-permute-done | bytes 294944 | tf_op jit(solution)/shard_map/ppermute | solution.py:64
  91.2 1.3 %collective-permute-start.10 = (bf16[296,512]{1,0:T(8,128)(2,1)S(1)}, bf16[296,512]{1,0:T(8,128)(2,1)S(1)}, u32[]{:S(2)}, u32[]{:S(2)}) collective-permute-start(bf16[296,512]{1,0:T(8,128)(2,1)S(1)} %collective-permute-done.8.far0), channel_id=1, source_target_pairs={{0,2},{2,0},{1,3},{3,1},{4,6},{6,4},{5,7},{7,5},{8,10},{10,8},{9,1... | collective-permute-start | bytes 909320 | tf_op jit(solution)/shard_map/ppermute | solution.py:64
  92.4 1.6 %collective-permute-done.11.near1 = bf16[288,512]{1,0:T(8,128)(2,1)S(1)} collective-permute-done((bf16[288,512]{1,0:T(8,128)(2,1)S(1)}, bf16[288,512]{1,0:T(8,128)(2,1)S(1)}, u32[]{:S(2)}, u32[]{:S(2)}) %collective-permute-start.11) | collective-permute-done | bytes 294944 | tf_op jit(solution)/shard_map/ppermute | solution.py:64
  94.1 2.4 %shard_map.219 = (bf16[2048,512]{1,0:T(8,128)(2,1)}, bf16[64,2048]{1,0:T(8,128)(2,1)}, f32[8,128]{1,0:T(8,128)}, f32[8,128]{1,0:T(8,128)}, f32[8,128]{1,0:T(8,128)}, /*index=5*/bf16[16,128]{1,0:T(8,128)(2,1)}) custom-call(s32[2]{0:T(128)S(1)} %pad_add_fusion.2.where_ref, ...), custom_call_target="tpu_custom_call", output_to_operand_aliasing={{0}: (11, {}), {1}: (12, {})} | custom-call | tf_op jit(solution)/shard_map/pallas_call | solution.py:427
  (34 shorter events, 0.7 us)
Async XLA Ops:
  3.4 6.1 %collective-permute-start = (bf16[4,4,8,8,640]{4,3,2,1,0:T(8,128)(2,1)S(1)}, bf16[4,4,8,8,640]{4,3,2,1,0:T(8,128)(2,1)S(1)}, u32[]{:S(2)}, u32[]{:S(2)}) collective-permute-start(bf16[4,4,8,8,640]{4,3,2,1,0:T(8,128)(2,1)S(1)} %shard_map.212), channel_id=1, source_target_pairs={{0,2},{2,0},{1,3},{3,1},{4,6},{6,4},{5,7},{7,5},{8,10},{10,8},{9,1... | collective-permute-start | bytes 3932168 | tf_op jit(solution)/shard_map/ppermute | solution.py:64
  9.8 7.9 %collective-permute-start.1 = (bf16[4,8,8,640]{3,2,1,0:T(8,128)(2,1)S(1)}, bf16[4,8,8,640]{3,2,1,0:T(8,128)(2,1)S(1)}, u32[]{:S(2)}, u32[]{:S(2)}) collective-permute-start(bf16[4,8,8,640]{3,2,1,0:T(8,128)(2,1)S(1)} %get-tuple-element.49), channel_id=1, source_target_pairs={{0,4},{2,18},{1,5},{3,19},{4,0},{6,22},{5,1},{7,23},{8,12},{10,26}... | collective-permute-start | bytes 983048 | tf_op jit(solution)/shard_map/ppermute | solution.py:64
  11.1 8.7 %collective-permute-start.2 = (bf16[4,8,8,640]{3,2,1,0:T(8,128)(2,1)S(1)}, bf16[4,8,8,640]{3,2,1,0:T(8,128)(2,1)S(1)}, u32[]{:S(2)}, u32[]{:S(2)}) collective-permute-start(bf16[4,8,8,640]{3,2,1,0:T(8,128)(2,1)S(1)} %get-tuple-element.50), channel_id=1, source_target_pairs={{0,1},{2,10},{1,0},{3,11},{4,5},{6,14},{5,4},{7,15},{8,9},{10,2},{... | collective-permute-start | bytes 983048 | tf_op jit(solution)/shard_map/ppermute | solution.py:64
  11.5 9.7 %collective-permute-start.3 = (bf16[4,8,8,640]{3,2,1,0:T(8,128)(2,1)S(1)}, bf16[4,8,8,640]{3,2,1,0:T(8,128)(2,1)S(1)}, u32[]{:S(2)}, u32[]{:S(2)}) collective-permute-start(bf16[4,8,8,640]{3,2,1,0:T(8,128)(2,1)S(1)} %get-tuple-element.51), channel_id=1, source_target_pairs={{0,5},{2,26},{1,4},{3,27},{4,1},{6,30},{5,0},{7,31},{8,13},{10,18}... | collective-permute-start | bytes 983048 | tf_op jit(solution)/shard_map/ppermute | solution.py:64
  22.2 19.7 %all-to-all-start = ((f16[32,8,640]{2,1,0:T(8,128)(2,1)}), f16[32,8,640]{2,1,0:T(8,128)(2,1)S(1)}, u32[]{:S(2)}, u32[]{:S(2)}) async-start(f16[32,8,640]{2,1,0:T(8,128)(2,1)} %convert_element_type.15), calls=%async_computation | async-start | bytes 655360 | tf_op jit(solution)/shard_map/all_to_all | solution.py:467
  41.9 37.0 %copy-start.3 = (f32[64,1024]{1,0:T(8,128)S(1)}, f32[64,1024]{1,0:T(8,128)}, u32[]{:S(2)}) copy-start(f32[64,1024]{1,0:T(8,128)} %refs_8_.3) | copy-start | bytes 786436
  41.9 37.0 %copy-start.4 = (f32[64,1024]{1,0:T(8,128)S(1)}, f32[64,1024]{1,0:T(8,128)}, u32[]{:S(2)}) copy-start(f32[64,1024]{1,0:T(8,128)} %refs_9_.3) | copy-start | bytes 786436
  41.9 37.0 %copy-start.5 = (f32[64,1024]{1,0:T(8,128)S(1)}, f32[64,1024]{1,0:T(8,128)}, u32[]{:S(2)}) copy-start(f32[64,1024]{1,0:T(8,128)} %refs_10_.3) | copy-start | bytes 786436
  41.9 37.0 %copy-start.8 = (f32[1024]{0:T(1024)S(1)}, f32[1024]{0:T(1024)}, u32[]{:S(2)}) copy-start(f32[1024]{0:T(1024)} %param.23) | copy-start | bytes 12292
  42.0 36.9 %copy-start.2 = (f32[1024,512]{1,0:T(8,128)S(1)}, f32[1024,512]{1,0:T(8,128)}, u32[]{:S(2)}) copy-start(f32[1024,512]{1,0:T(8,128)} %refs_7_.3) | copy-start | bytes 6291460
  55.2 23.8 %copy-start = (f32[1024,512]{1,0:T(8,128)S(1)}, f32[1024,512]{1,0:T(8,128)}, u32[]{:S(2)}) copy-start(f32[1024,512]{1,0:T(8,128)} %refs_5_.3) | copy-start | bytes 6291460
  55.2 23.7 %copy-start.1 = (f32[1024,512]{1,0:T(8,128)S(1)}, f32[1024,512]{1,0:T(8,128)}, u32[]{:S(2)}) copy-start(f32[1024,512]{1,0:T(8,128)} %refs_6_.3) | copy-start | bytes 6291460
  55.2 23.7 %copy-start.6 = (f32[1024]{0:T(1024)S(1)}, f32[1024]{0:T(1024)}, u32[]{:S(2)}) copy-start(f32[1024]{0:T(1024)} %param.21) | copy-start | bytes 12292
  55.2 23.7 %copy-start.7 = (f32[1024]{0:T(1024)S(1)}, f32[1024]{0:T(1024)}, u32[]{:S(2)}) copy-start(f32[1024]{0:T(1024)} %param.22) | copy-start | bytes 12292
  70.2 6.6 %collective-permute-start.4 = (f32[8,128]{1,0:T(8,128)S(1)}, f32[8,128]{1,0:T(8,128)S(1)}, u32[]{:S(2)}, u32[]{:S(2)}) collective-permute-start(f32[8,128]{1,0:T(8,128)S(1)} %shard_map.216.refs_0_), channel_id=1, source_target_pairs={{0,2},{2,0},{1,3},{3,1},{4,6},{6,4},{5,7},{7,5},{8,10},{10,8},{9,1... | collective-permute-start | bytes 12296 | tf_op jit(solution)/shard_map/ppermute | solution.py:64
  75.1 2.5 %collective-permute-start.5 = (f32[8,128]{1,0:T(8,128)S(1)}, f32[8,128]{1,0:T(8,128)S(1)}, u32[]{:S(2)}, u32[]{:S(2)}) collective-permute-start(f32[8,128]{1,0:T(8,128)S(1)} %shard_map.216.refs_0_), channel_id=1, source_target_pairs={{0,1},{2,3},{1,0},{3,2},{4,5},{6,7},{5,4},{7,6},{8,9},{10,11},{9,8... | collective-permute-start | bytes 12296 | tf_op jit(solution)/shard_map/ppermute | solution.py:64
  75.4 3.0 %collective-permute-start.6 = (f32[8,128]{1,0:T(8,128)S(1)}, f32[8,128]{1,0:T(8,128)S(1)}, u32[]{:S(2)}, u32[]{:S(2)}) collective-permute-start(f32[8,128]{1,0:T(8,128)S(1)} %shard_map.216.refs_0_), channel_id=1, source_target_pairs={{0,3},{2,1},{1,2},{3,0},{4,7},{6,5},{5,6},{7,4},{8,11},{10,9},{9,1... | collective-permute-start | bytes 12296 | tf_op jit(solution)/shard_map/ppermute | solution.py:64
  78.4 3.6 %collective-permute-start.7 = (f16[64,8,640]{2,1,0:T(8,128)(2,1)S(1)}, f16[64,8,640]{2,1,0:T(8,128)(2,1)S(1)}, u32[]{:S(2)}, u32[]{:S(2)}) collective-permute-start(f16[64,8,640]{2,1,0:T(8,128)(2,1)S(1)} %all_to_all.16), channel_id=1, source_target_pairs={{0,2},{2,0},{1,3},{3,1},{4,6},{6,4},{5,7},{7,5},{8,10},{10,8},{9,1... | collective-permute-start | bytes 1966088 | tf_op jit(solution)/shard_map/ppermute | solution.py:64
  80.6 10.6 %collective-permute-start.8 = (bf16[296,512]{1,0:T(8,128)(2,1)S(1)}, bf16[296,512]{1,0:T(8,128)(2,1)S(1)}, u32[]{:S(2)}, u32[]{:S(2)}) collective-permute-start(bf16[296,512]{1,0:T(8,128)(2,1)S(1)} %get-tuple-element.59.refs_16_), channel_id=1, source_target_pairs={{0,1},{2,3},{1,0},{3,2},{4,5},{6,7},{5,4},{7,6},{8,9},{10,11},{9,8... | collective-permute-start | bytes 909320 | tf_op jit(solution)/shard_map/ppermute | solution.py:64
  81.8 9.4 %collective-permute-start.9 = (bf16[288,512]{1,0:T(8,128)(2,1)S(1)}, bf16[288,512]{1,0:T(8,128)(2,1)S(1)}, u32[]{:S(2)}, u32[]{:S(2)}) collective-permute-start(bf16[288,512]{1,0:T(8,128)(2,1)S(1)} %get-tuple-element.60.refs_17_), channel_id=1, source_target_pairs={{0,5},{2,7},{1,4},{3,6},{4,1},{6,3},{5,0},{7,2},{8,13},{10,15},{9,... | collective-permute-start | bytes 884744 | tf_op jit(solution)/shard_map/ppermute | solution.py:64
  91.2 2.9 %collective-permute-start.10 = (bf16[296,512]{1,0:T(8,128)(2,1)S(1)}, bf16[296,512]{1,0:T(8,128)(2,1)S(1)}, u32[]{:S(2)}, u32[]{:S(2)}) collective-permute-start(bf16[296,512]{1,0:T(8,128)(2,1)S(1)} %collective-permute-done.8.far0), channel_id=1, source_target_pairs={{0,2},{2,0},{1,3},{3,1},{4,6},{6,4},{5,7},{7,5},{8,10},{10,8},{9,1... | collective-permute-start | bytes 909320 | tf_op jit(solution)/shard_map/ppermute | solution.py:64
  92.4 1.6 %collective-permute-start.11 = (bf16[288,512]{1,0:T(8,128)(2,1)S(1)}, bf16[288,512]{1,0:T(8,128)(2,1)S(1)}, u32[]{:S(2)}, u32[]{:S(2)}) collective-permute-start(bf16[288,512]{1,0:T(8,128)(2,1)S(1)} %collective-permute-done.9.far1), channel_id=1, source_target_pairs={{0,2},{2,0},{1,3},{3,1},{4,6},{6,4},{5,7},{7,5},{8,10},{10,8},{9,1... | collective-permute-start | bytes 884744 | tf_op jit(solution)/shard_map/ppermute | solution.py:64

commit v10 on v9

--- a/solution.py
+++ b/solution.py
@@ -40,20 +40,15 @@
     ]
 
 
-def along(shift):
+def along(stage, shift):
     def target(z, y, x, c):
-        if c == 0:
+        if c == stage:
             return z, y, x ^ shift, c
         return z, y ^ shift, x, c
 
     return permutation(target)
 
 
-SECOND_GROUPS = [
-    [place(z, q, p, c) if c == 0 else place(z, p, q, c) for q in range(4) for z in range(8)]
-    for c in range(2)
-    for p in range(4)
-]
 SIBLING = permutation(lambda z, y, x, c: (z, y, x, 1 - c))
 PARTNER = permutation(lambda z, y, x, c: (z, y, x ^ 1, c))
 OTHER_PARTNER = permutation(lambda z, y, x, c: (z, y, x ^ 3, c))
@@ -182,20 +177,27 @@
     return jnp.max(jnp.max(jnp.abs(x), axis=1, keepdims=True), axis=0, keepdims=True)
 
 
-def sum_encoded(where_ref, *refs):
+def add_rows(where_ref, *refs):
+    terms, outs = refs[:4], refs[4:]
+    for k in range(4):
+        at = where_ref[0] ^ k
+        total = terms[0][at].astype(jnp.float32)
+        for term in terms[1:]:
+            total = total + term[at].astype(jnp.float32)
+        outs[k][...] = total
+
+
+def sum_encoded(*refs):
     terms, out_ref = refs[:4], refs[4]
     largest = jnp.zeros((8, ROW), jnp.float32)
-    for q in range(4):
-        for z in range(8):
-            total = terms[0][q, z].astype(jnp.float32)
-            for term in terms[1:]:
-                total = total + term[q, z].astype(jnp.float32)
-            out_ref[q * 8 + z] = total
-            largest = jnp.maximum(largest, jnp.abs(total))
+    for b in range(8):
+        total = (terms[0][b] + terms[1][b]) + (terms[2][b] + terms[3][b])
+        out_ref[b] = total
+        largest = jnp.maximum(largest, jnp.abs(total))
     exponent = exponent_of(largest_of(largest))
     scale = jnp.concatenate([jnp.exp2(-exponent)] * 5, axis=1)
     row = lax.broadcasted_iota(jnp.int32, (8, LANES), 0)
-    for b in range(32):
+    for b in range(8):
         own = out_ref[b] * scale
         spare = spare_lanes(b % 2) & (row == 7)
         out_ref[b, :, :KEY_WIDTH] = own[:, :KEY_WIDTH]
@@ -206,7 +208,7 @@
     parity = where_ref[0]
     row = lax.broadcasted_iota(jnp.int32, (8, LANES), 0)
     own = jnp.zeros((8, ROW), jnp.float32)
-    for b in range(32):
+    for b in range(8):
         block = blocks_ref[b]
         scale = scale_of(block[:, KEY_WIDTH:], parity)
         own = own + block * jnp.concatenate([scale] * 5, axis=1)
@@ -462,11 +464,11 @@
     kept = pack(core, first_place, grads)
     parts = in_vmem(add_pair, [kept, got], [((4, 8, 8, ROW), jnp.bfloat16)] * 4)
     states = [key_master, key_first, key_second, router_master, router_first, router_second]
-    parts = [parts[0]] + [send(parts[k], along(k)) for k in (2, 1, 3)]
-    [code] = in_vmem(sum_encoded, parts, [((32, 8, ROW), jnp.float32)], [z])
-    code = lax.all_to_all(
-        code.astype(jnp.float16), ALL, 0, 0, axis_index_groups=SECOND_GROUPS, tiled=True
-    )
+    parts = [parts[0]] + [send(parts[k], along(0, k)) for k in (2, 1, 3)]
+    parts = in_vmem(add_rows, parts, [((8, 8, ROW), jnp.float32)] * 4, [second_place])
+    parts = [parts[0]] + [send(parts[k], along(1, k)) for k in (2, 1, 3)]
+    [code] = in_vmem(sum_encoded, parts, [((8, 8, ROW), jnp.float32)])
+    code = lax.all_to_all(code.astype(jnp.float16), "z", 0, 0, tiled=True)
     [code] = in_vmem(encode, [code.astype(jnp.float32)], [((8, ROW), jnp.float32)], [z & 1])
     line = lax.all_to_all(
         jnp.broadcast_to(code.astype(jnp.float16)[None], (8, 8, ROW)), "z", 0, 0, tiled=True

time: 97.1 us -> 99 us (1.020)
  starting transfers between devices: 26.1 us -> 28.6 us
  blocking collectives: 27.4 us -> 25.3 us
  waiting for transfers between devices: 25.5 us -> 27.2 us
    ppermute x12 -> x15, starting transfers between devices: 16.4 us -> 20.8 us  [send(): return lax.ppermute(x, ALL, pairs)]
    ppermute x12 -> x15, waiting for transfers between devices: 15.5 us -> 19.8 us  [send(): return lax.ppermute(x, ALL, pairs)]
    all_to_all x1, blocking collectives: 12.7 us -> 9.78 us  [on_device(): lax.all_to_all(jnp.broadcast_to(code.astype(jnp.float16)[None], (8, 8, RO...]
    all_to_all x1, waiting for transfers between devices: 10 us -> 7.4 us  [on_device(): code = lax.all_to_all(code.astype(jnp.float16), 'z', 0, 0, tiled=True)]
    all_to_all x1, starting transfers between devices: 9.69 us -> 7.85 us  [on_device(): code = lax.all_to_all(code.astype(jnp.float16), 'z', 0, 0, tiled=True)]
  transfers between devices with their start and end apart: 13 -> 16, of which waited for: 8 -> 11; matrix products, arithmetic and copies ran while one was open for 0% -> 0% of each run, Pallas kernels for 9% -> 9%
where the time goes in v10:
time: 99 us; the launch traced here: 98.6 us
  starting transfers between devices  28.6 us (29%)
  waiting for transfers between devices  27.2 us (27%)
  blocking collectives  25.3 us (26%)
  Pallas kernels  15.2 us (15%)
  other arithmetic  1.14 us (1%)
  between operations  1.03 us (1%)
    ppermute x15, starting transfers between devices, send(): return lax.ppermute(x, ALL, pairs)  20.8 us
    ppermute x15, waiting for transfers between devices, send(): return lax.ppermute(x, ALL, pairs)  19.8 us
    all_to_all x1, blocking collectives, on_device(): parts = lax.all_to_all(line, ('y', 'xh'), 0, 0, tiled=True)  15.5 us
    all_to_all x1, blocking collectives, on_device(): lax.all_to_all(jnp.broadcast_to(code.astype(jnp.float16)[None], (8, 8, RO...  9.78 us
    all_to_all x1, starting transfers between devices, on_device(): code = lax.all_to_all(code.astype(jnp.float16), 'z', 0, 0, tiled=True)  7.85 us
    all_to_all x1, waiting for transfers between devices, on_device(): code = lax.all_to_all(code.astype(jnp.float16), 'z', 0, 0, tiled=True)  7.4 us
    pallas_call x2, Pallas kernels, pack(): pl.pallas_call(pack_local, in_specs=[pl.BlockSpec(memory_space=pltpu.SMEM...  5.31 us
    pallas_call x1, Pallas kernels, updated(): pl.pallas_call(update_second, in_specs=[IN_SMEM] + [IN_VMEM] * 18, out_sp...  4.78 us
  transfers between devices with their start and end apart: 16, of which 11 were waited for; matrix products, arithmetic and copies ran while one was open for 0% of the time, Pallas kernels for 9%

profile of v10, /device:TPU:1, one launch (start us, length us, event | category | flops | bytes accessed | tf_op | source)
XLA Modules:
  0.0 98.6 jit_solution(8134243776164257439)
XLA Ops:
  0.7 2.7 %shard_map.212 = bf16[4,4,8,8,640]{4,3,2,1,0:T(8,128)(2,1)S(1)} custom-call(s32[2]{0:T(128)S(1)} %pad_add_fusion.1.where_ref, bf16[2,2048,512]{2,1,0:T(8,128)(2,1)} %bitcast.23, bf16[2,64,2048]{2,1,0:T(8,128)(2,1)} %bitcast.26, bf16[2,2048]{1,0:T(2,128)(2,1)} %bitcast.28), custom_call_target="tpu_custom_call" | custom-call | tf_op jit(solution)/shard_map/pallas_call | solution.py:130
  3.4 3.3 %collective-permute-start = (bf16[4,4,8,8,640]{4,3,2,1,0:T(8,128)(2,1)S(1)}, bf16[4,4,8,8,640]{4,3,2,1,0:T(8,128)(2,1)S(1)}, u32[]{:S(2)}, u32[]{:S(2)}) collective-permute-start(bf16[4,4,8,8,640]{4,3,2,1,0:T(8,128)(2,1)S(1)} %shard_map.212), channel_id=1, source_target_pairs={{0,2},{2,0},{1,3},{3,1},{4,6},{6,4},{5,7},{7,5},{8,10},{10,8},{9,1... | collective-permute-start | bytes 3932168 | tf_op jit(solution)/shard_map/ppermute | solution.py:59
  6.8 2.7 %shard_map.211.kept_ref = bf16[4,4,8,8,640]{4,3,2,1,0:T(8,128)(2,1)S(1)} custom-call(s32[2]{0:T(128)S(1)} %pad_add_fusion.where_ref, bf16[2,2048,512]{2,1,0:T(8,128)(2,1)} %bitcast.24, bf16[2,64,2048]{2,1,0:T(8,128)(2,1)} %bitcast.27, bf16[2,2048]{1,0:T(2,128)(2,1)} %bitcast.29), custom_call_target="tpu_custom_call" | custom-call | tf_op jit(solution)/shard_map/pallas_call | solution.py:130
  9.8 1.3 %collective-permute-start.1 = (bf16[4,8,8,640]{3,2,1,0:T(8,128)(2,1)S(1)}, bf16[4,8,8,640]{3,2,1,0:T(8,128)(2,1)S(1)}, u32[]{:S(2)}, u32[]{:S(2)}) collective-permute-start(bf16[4,8,8,640]{3,2,1,0:T(8,128)(2,1)S(1)} %get-tuple-element.53), channel_id=1, source_target_pairs={{0,4},{2,18},{1,5},{3,19},{4,0},{6,22},{5,1},{7,23},{8,12},{10,26}... | collective-permute-start | bytes 983048 | tf_op jit(solution)/shard_map/ppermute | solution.py:59
  11.1 0.4 collective-permute-start.2
  11.5 1.7 %collective-permute-start.3 = (bf16[4,8,8,640]{3,2,1,0:T(8,128)(2,1)S(1)}, bf16[4,8,8,640]{3,2,1,0:T(8,128)(2,1)S(1)}, u32[]{:S(2)}, u32[]{:S(2)}) collective-permute-start(bf16[4,8,8,640]{3,2,1,0:T(8,128)(2,1)S(1)} %get-tuple-element.55), channel_id=1, source_target_pairs={{0,5},{2,26},{1,4},{3,27},{4,1},{6,30},{5,0},{7,31},{8,13},{10,18}... | collective-permute-start | bytes 983048 | tf_op jit(solution)/shard_map/ppermute | solution.py:59
  13.1 4.5 %collective-permute-done.1.refs_1_ = bf16[4,8,8,640]{3,2,1,0:T(8,128)(2,1)S(1)} collective-permute-done((bf16[4,8,8,640]{3,2,1,0:T(8,128)(2,1)S(1)}, bf16[4,8,8,640]{3,2,1,0:T(8,128)(2,1)S(1)}, u32[]{:S(2)}, u32[]{:S(2)}) %collective-permute-start.1) | collective-permute-done | bytes 327712 | tf_op jit(solution)/shard_map/ppermute | solution.py:59
  17.7 2.1 %collective-permute-done.2.refs_2_ = bf16[4,8,8,640]{3,2,1,0:T(8,128)(2,1)S(1)} collective-permute-done((bf16[4,8,8,640]{3,2,1,0:T(8,128)(2,1)S(1)}, bf16[4,8,8,640]{3,2,1,0:T(8,128)(2,1)S(1)}, u32[]{:S(2)}, u32[]{:S(2)}) %collective-permute-start.2) | collective-permute-done | bytes 327712 | tf_op jit(solution)/shard_map/ppermute | solution.py:59
  19.7 1.4 %collective-permute-done.3.refs_3_ = bf16[4,8,8,640]{3,2,1,0:T(8,128)(2,1)S(1)} collective-permute-done((bf16[4,8,8,640]{3,2,1,0:T(8,128)(2,1)S(1)}, bf16[4,8,8,640]{3,2,1,0:T(8,128)(2,1)S(1)}, u32[]{:S(2)}, u32[]{:S(2)}) %collective-permute-start.3) | collective-permute-done | bytes 327712 | tf_op jit(solution)/shard_map/ppermute | solution.py:59
  21.3 1.5 %collective-permute-start.4 = (f32[8,8,640]{2,1,0:T(8,128)S(1)}, f32[8,8,640]{2,1,0:T(8,128)S(1)}, u32[]{:S(2)}, u32[]{:S(2)}) collective-permute-start(f32[8,8,640]{2,1,0:T(8,128)S(1)} %get-tuple-element.57), channel_id=1, source_target_pairs={{0,16},{2,6},{1,17},{3,7},{4,20},{6,2},{5,21},{7,3},{8,24},{10,14}... | collective-permute-start | bytes 491528 | tf_op jit(solution)/shard_map/ppermute | solution.py:59
  23.1 1.5 %collective-permute-start.6 = (f32[8,8,640]{2,1,0:T(8,128)S(1)}, f32[8,8,640]{2,1,0:T(8,128)S(1)}, u32[]{:S(2)}, u32[]{:S(2)}) collective-permute-start(f32[8,8,640]{2,1,0:T(8,128)S(1)} %get-tuple-element.59), channel_id=1, source_target_pairs={{0,24},{2,7},{1,25},{3,6},{4,28},{6,3},{5,29},{7,2},{8,16},{10,15}... | collective-permute-start | bytes 491528 | tf_op jit(solution)/shard_map/ppermute | solution.py:59
  24.6 2.7 %collective-permute-done.4.refs_1_ = f32[8,8,640]{2,1,0:T(8,128)S(1)} collective-permute-done((f32[8,8,640]{2,1,0:T(8,128)S(1)}, f32[8,8,640]{2,1,0:T(8,128)S(1)}, u32[]{:S(2)}, u32[]{:S(2)}) %collective-permute-start.4) | collective-permute-done | bytes 163872 | tf_op jit(solution)/shard_map/ppermute | solution.py:59
  27.3 0.5 collective-permute-done.5.refs_2_
  27.8 1.1 %collective-permute-done.6.refs_3_ = f32[8,8,640]{2,1,0:T(8,128)S(1)} collective-permute-done((f32[8,8,640]{2,1,0:T(8,128)S(1)}, f32[8,8,640]{2,1,0:T(8,128)S(1)}, u32[]{:S(2)}, u32[]{:S(2)}) %collective-permute-start.6) | collective-permute-done | bytes 163872 | tf_op jit(solution)/shard_map/ppermute | solution.py:59
  29.1 0.6 convert_element_type.15
  29.8 7.8 %all-to-all-start = ((f16[8,8,640]{2,1,0:T(8,128)(2,1)}), f16[8,8,640]{2,1,0:T(8,128)(2,1)S(1)}, u32[]{:S(2)}, u32[]{:S(2)}) async-start(f16[8,8,640]{2,1,0:T(8,128)(2,1)} %convert_element_type.15), calls=%async_computation | async-start | bytes 163840 | tf_op jit(solution)/shard_map/all_to_all | solution.py:471
  37.6 7.4 %all-to-all-done = f16[8,8,640]{2,1,0:T(8,128)(2,1)S(1)} async-done(((f16[8,8,640]{2,1,0:T(8,128)(2,1)}), f16[8,8,640]{2,1,0:T(8,128)(2,1)S(1)}, u32[]{:S(2)}, u32[]{:S(2)}) %all-to-all-start) | async-done | bytes 81952 | tf_op jit(solution)/shard_map/all_to_all | solution.py:471
  45.4 9.8 %all_to_all.15 = f16[8,8,640]{2,1,0:T(8,128)(2,1)S(1)} all-to-all(f16[8,8,640]{2,1,0:T(8,128)(2,1)S(1)} %broadcast_in_dim.4), channel_id=1, replica_groups=mesh['z'=8,'y'=4,'xh'=2,'c'=2,'xl'=2] {'z'}, dimensions={0} | all-to-all | bytes 163840 | tf_op jit(solution)/shard_map/all_to_all | solution.py:473
  55.3 15.5 %all_to_all.16 = f16[64,8,640]{2,1,0:T(8,128)(2,1)S(1)} all-to-all(f16[64,8,640]{2,1,0:T(8,128)(2,1)S(1)} %bitcast.25), channel_id=1, replica_groups=mesh['z'=8,'y'=4,'xh'=2,'c'=2,'xl'=2] {'y','xh'}, dimensions={0} | all-to-all | bytes 1310720 | tf_op jit(solution)/shard_map/all_to_all | solution.py:477
  71.0 6.0 %collective-permute-start.7 = (f32[8,128]{1,0:T(8,128)S(1)}, f32[8,128]{1,0:T(8,128)S(1)}, u32[]{:S(2)}, u32[]{:S(2)}) collective-permute-start(f32[8,128]{1,0:T(8,128)S(1)} %shard_map.217.refs_0_), channel_id=1, source_target_pairs={{0,2},{2,0},{1,3},{3,1},{4,6},{6,4},{5,7},{7,5},{8,10},{10,8},{9,1... | collective-permute-start | bytes 12296 | tf_op jit(solution)/shard_map/ppermute | solution.py:59
  77.0 0.3 collective-permute-start.8
  77.3 1.4 %collective-permute-start.9 = (f32[8,128]{1,0:T(8,128)S(1)}, f32[8,128]{1,0:T(8,128)S(1)}, u32[]{:S(2)}, u32[]{:S(2)}) collective-permute-start(f32[8,128]{1,0:T(8,128)S(1)} %shard_map.217.refs_0_), channel_id=1, source_target_pairs={{0,3},{2,1},{1,2},{3,0},{4,7},{6,5},{5,6},{7,4},{8,11},{10,9},{9,1... | collective-permute-start | bytes 12296 | tf_op jit(solution)/shard_map/ppermute | solution.py:59
  78.7 0.7 collective-permute-done.8.refs_2_
  79.5 0.9 collective-permute-done.9.refs_3_
  80.4 0.4 collective-permute-start.10
  80.9 1.6 %shard_map.218 = (f32[3,512,512]{2,1,0:T(8,128)S(1)}, f32[3,32,1024]{2,1,0:T(8,128)S(1)}, f32[8,128]{1,0:T(8,128)S(1)}, f32[8,128]{1,0:T(8,128)S(1)}, f32[8,128]...) custom-call(s32[2]{0:T(128)S(1)} %pad_add_fusion.2.where_ref, ...), custom_call_target="tpu_custom_call" | custom-call | flops 7000000 | bytes 8000000 | tf_op jit(solution)/shard_map/pallas_call | solution.py:403
  82.5 1.2 %collective-permute-start.11 = (bf16[296,512]{1,0:T(8,128)(2,1)S(1)}, bf16[296,512]{1,0:T(8,128)(2,1)S(1)}, u32[]{:S(2)}, u32[]{:S(2)}) collective-permute-start(bf16[296,512]{1,0:T(8,128)(2,1)S(1)} %get-tuple-element.67.refs_16_), channel_id=1, source_target_pairs={{0,1},{2,3},{1,0},{3,2},{4,5},{6,7},{5,4},{7,6},{8,9},{10,11},{9,8... | collective-permute-start | bytes 909320 | tf_op jit(solution)/shard_map/ppermute | solution.py:59
  84.1 4.8 %shard_map.219 = (f32[1024,512]{1,0:T(8,128)}, f32[1024,512]{1,0:T(8,128)}, f32[1024,512]{1,0:T(8,128)}, f32[64,1024]{1,0:T(8,128)}, f32[64,1024]{1,0:T(8,128)},...) custom-call(s32[2]{0:T(128)S(1)} %pad_add_fusion.3.where_ref, ...), custom_call_target="tpu_custom_call" | custom-call | flops 7000000 | bytes 8000000 | tf_op jit(solution)/shard_map/pallas_call | solution.py:415
  88.9 4.2 %collective-permute-done.12.far1 = bf16[288,512]{1,0:T(8,128)(2,1)S(1)} collective-permute-done((bf16[288,512]{1,0:T(8,128)(2,1)S(1)}, bf16[288,512]{1,0:T(8,128)(2,1)S(1)}, u32[]{:S(2)}, u32[]{:S(2)}) %collective-permute-start.12) | collective-permute-done | bytes 294944 | tf_op jit(solution)/shard_map/ppermute | solution.py:59
  93.1 1.3 %collective-permute-start.13 = (bf16[296,512]{1,0:T(8,128)(2,1)S(1)}, bf16[296,512]{1,0:T(8,128)(2,1)S(1)}, u32[]{:S(2)}, u32[]{:S(2)}) collective-permute-start(bf16[296,512]{1,0:T(8,128)(2,1)S(1)} %collective-permute-done.11.far0), channel_id=1, source_target_pairs={{0,2},{2,0},{1,3},{3,1},{4,6},{6,4},{5,7},{7,5},{8,10},{10,8},{9,1... | collective-permute-start | bytes 909320 | tf_op jit(solution)/shard_map/ppermute | solution.py:59
  94.4 1.6 %collective-permute-done.14.near1 = bf16[288,512]{1,0:T(8,128)(2,1)S(1)} collective-permute-done((bf16[288,512]{1,0:T(8,128)(2,1)S(1)}, bf16[288,512]{1,0:T(8,128)(2,1)S(1)}, u32[]{:S(2)}, u32[]{:S(2)}) %collective-permute-start.14) | collective-permute-done | bytes 294944 | tf_op jit(solution)/shard_map/ppermute | solution.py:59
  96.0 2.4 %shard_map.220 = (bf16[2048,512]{1,0:T(8,128)(2,1)}, bf16[64,2048]{1,0:T(8,128)(2,1)}, f32[8,128]{1,0:T(8,128)}, f32[8,128]{1,0:T(8,128)}, f32[8,128]{1,0:T(8,128)}, /*index=5*/bf16[16,128]{1,0:T(8,128)(2,1)}) custom-call(s32[2]{0:T(128)S(1)} %pad_add_fusion.2.where_ref, ...), custom_call_target="tpu_custom_call", output_to_operand_aliasing={{0}: (11, {}), {1}: (12, {})} | custom-call | tf_op jit(solution)/shard_map/pallas_call | solution.py:429
  (41 shorter events, 2.2 us)
Async XLA Ops:
  3.4 6.1 %collective-permute-start = (bf16[4,4,8,8,640]{4,3,2,1,0:T(8,128)(2,1)S(1)}, bf16[4,4,8,8,640]{4,3,2,1,0:T(8,128)(2,1)S(1)}, u32[]{:S(2)}, u32[]{:S(2)}) collective-permute-start(bf16[4,4,8,8,640]{4,3,2,1,0:T(8,128)(2,1)S(1)} %shard_map.212), channel_id=1, source_target_pairs={{0,2},{2,0},{1,3},{3,1},{4,6},{6,4},{5,7},{7,5},{8,10},{10,8},{9,1... | collective-permute-start | bytes 3932168 | tf_op jit(solution)/shard_map/ppermute | solution.py:59
  9.8 7.9 %collective-permute-start.1 = (bf16[4,8,8,640]{3,2,1,0:T(8,128)(2,1)S(1)}, bf16[4,8,8,640]{3,2,1,0:T(8,128)(2,1)S(1)}, u32[]{:S(2)}, u32[]{:S(2)}) collective-permute-start(bf16[4,8,8,640]{3,2,1,0:T(8,128)(2,1)S(1)} %get-tuple-element.53), channel_id=1, source_target_pairs={{0,4},{2,18},{1,5},{3,19},{4,0},{6,22},{5,1},{7,23},{8,12},{10,26}... | collective-permute-start | bytes 983048 | tf_op jit(solution)/shard_map/ppermute | solution.py:59
  11.1 8.7 %collective-permute-start.2 = (bf16[4,8,8,640]{3,2,1,0:T(8,128)(2,1)S(1)}, bf16[4,8,8,640]{3,2,1,0:T(8,128)(2,1)S(1)}, u32[]{:S(2)}, u32[]{:S(2)}) collective-permute-start(bf16[4,8,8,640]{3,2,1,0:T(8,128)(2,1)S(1)} %get-tuple-element.54), channel_id=1, source_target_pairs={{0,1},{2,10},{1,0},{3,11},{4,5},{6,14},{5,4},{7,15},{8,9},{10,2},{... | collective-permute-start | bytes 983048 | tf_op jit(solution)/shard_map/ppermute | solution.py:59
  11.5 9.7 %collective-permute-start.3 = (bf16[4,8,8,640]{3,2,1,0:T(8,128)(2,1)S(1)}, bf16[4,8,8,640]{3,2,1,0:T(8,128)(2,1)S(1)}, u32[]{:S(2)}, u32[]{:S(2)}) collective-permute-start(bf16[4,8,8,640]{3,2,1,0:T(8,128)(2,1)S(1)} %get-tuple-element.55), channel_id=1, source_target_pairs={{0,5},{2,26},{1,4},{3,27},{4,1},{6,30},{5,0},{7,31},{8,13},{10,18}... | collective-permute-start | bytes 983048 | tf_op jit(solution)/shard_map/ppermute | solution.py:59
  21.3 6.1 %collective-permute-start.4 = (f32[8,8,640]{2,1,0:T(8,128)S(1)}, f32[8,8,640]{2,1,0:T(8,128)S(1)}, u32[]{:S(2)}, u32[]{:S(2)}) collective-permute-start(f32[8,8,640]{2,1,0:T(8,128)S(1)} %get-tuple-element.57), channel_id=1, source_target_pairs={{0,16},{2,6},{1,17},{3,7},{4,20},{6,2},{5,21},{7,3},{8,24},{10,14}... | collective-permute-start | bytes 491528 | tf_op jit(solution)/shard_map/ppermute | solution.py:59
  22.8 5.1 %collective-permute-start.5 = (f32[8,8,640]{2,1,0:T(8,128)S(1)}, f32[8,8,640]{2,1,0:T(8,128)S(1)}, u32[]{:S(2)}, u32[]{:S(2)}) collective-permute-start(f32[8,8,640]{2,1,0:T(8,128)S(1)} %get-tuple-element.58), channel_id=1, source_target_pairs={{0,8},{2,3},{1,9},{3,2},{4,12},{6,7},{5,13},{7,6},{8,0},{10,11},{9... | collective-permute-start | bytes 491528 | tf_op jit(solution)/shard_map/ppermute | solution.py:59
  23.1 5.9 %collective-permute-start.6 = (f32[8,8,640]{2,1,0:T(8,128)S(1)}, f32[8,8,640]{2,1,0:T(8,128)S(1)}, u32[]{:S(2)}, u32[]{:S(2)}) collective-permute-start(f32[8,8,640]{2,1,0:T(8,128)S(1)} %get-tuple-element.59), channel_id=1, source_target_pairs={{0,24},{2,7},{1,25},{3,6},{4,28},{6,3},{5,29},{7,2},{8,16},{10,15}... | collective-permute-start | bytes 491528 | tf_op jit(solution)/shard_map/ppermute | solution.py:59
  28.9 51.9 %copy-start.3 = (f32[64,1024]{1,0:T(8,128)S(1)}, f32[64,1024]{1,0:T(8,128)}, u32[]{:S(2)}) copy-start(f32[64,1024]{1,0:T(8,128)} %refs_8_.3) | copy-start | bytes 786436
  28.9 51.9 %copy-start.4 = (f32[64,1024]{1,0:T(8,128)S(1)}, f32[64,1024]{1,0:T(8,128)}, u32[]{:S(2)}) copy-start(f32[64,1024]{1,0:T(8,128)} %refs_9_.3) | copy-start | bytes 786436
  28.9 51.9 %copy-start.5 = (f32[64,1024]{1,0:T(8,128)S(1)}, f32[64,1024]{1,0:T(8,128)}, u32[]{:S(2)}) copy-start(f32[64,1024]{1,0:T(8,128)} %refs_10_.3) | copy-start | bytes 786436
  29.1 51.7 %copy-start.2 = (f32[1024,512]{1,0:T(8,128)S(1)}, f32[1024,512]{1,0:T(8,128)}, u32[]{:S(2)}) copy-start(f32[1024,512]{1,0:T(8,128)} %refs_7_.3) | copy-start | bytes 6291460
  29.8 15.2 %all-to-all-start = ((f16[8,8,640]{2,1,0:T(8,128)(2,1)}), f16[8,8,640]{2,1,0:T(8,128)(2,1)S(1)}, u32[]{:S(2)}, u32[]{:S(2)}) async-start(f16[8,8,640]{2,1,0:T(8,128)(2,1)} %convert_element_type.15), calls=%async_computation | async-start | bytes 163840 | tf_op jit(solution)/shard_map/all_to_all | solution.py:471
  55.2 25.6 %copy-start = (f32[1024,512]{1,0:T(8,128)S(1)}, f32[1024,512]{1,0:T(8,128)}, u32[]{:S(2)}) copy-start(f32[1024,512]{1,0:T(8,128)} %refs_5_.3) | copy-start | bytes 6291460
  55.2 25.6 %copy-start.1 = (f32[1024,512]{1,0:T(8,128)S(1)}, f32[1024,512]{1,0:T(8,128)}, u32[]{:S(2)}) copy-start(f32[1024,512]{1,0:T(8,128)} %refs_6_.3) | copy-start | bytes 6291460
  55.2 25.6 %copy-start.6 = (f32[1024]{0:T(1024)S(1)}, f32[1024]{0:T(1024)}, u32[]{:S(2)}) copy-start(f32[1024]{0:T(1024)} %param.21) | copy-start | bytes 12292
  55.2 25.6 %copy-start.7 = (f32[1024]{0:T(1024)S(1)}, f32[1024]{0:T(1024)}, u32[]{:S(2)}) copy-start(f32[1024]{0:T(1024)} %param.22) | copy-start | bytes 12292
  55.2 25.6 %copy-start.8 = (f32[1024]{0:T(1024)S(1)}, f32[1024]{0:T(1024)}, u32[]{:S(2)}) copy-start(f32[1024]{0:T(1024)} %param.23) | copy-start | bytes 12292
  71.0 7.7 %collective-permute-start.7 = (f32[8,128]{1,0:T(8,128)S(1)}, f32[8,128]{1,0:T(8,128)S(1)}, u32[]{:S(2)}, u32[]{:S(2)}) collective-permute-start(f32[8,128]{1,0:T(8,128)S(1)} %shard_map.217.refs_0_), channel_id=1, source_target_pairs={{0,2},{2,0},{1,3},{3,1},{4,6},{6,4},{5,7},{7,5},{8,10},{10,8},{9,1... | collective-permute-start | bytes 12296 | tf_op jit(solution)/shard_map/ppermute | solution.py:59
  77.0 2.5 %collective-permute-start.8 = (f32[8,128]{1,0:T(8,128)S(1)}, f32[8,128]{1,0:T(8,128)S(1)}, u32[]{:S(2)}, u32[]{:S(2)}) collective-permute-start(f32[8,128]{1,0:T(8,128)S(1)} %shard_map.217.refs_0_), channel_id=1, source_target_pairs={{0,1},{2,3},{1,0},{3,2},{4,5},{6,7},{5,4},{7,6},{8,9},{10,11},{9,8... | collective-permute-start | bytes 12296 | tf_op jit(solution)/shard_map/ppermute | solution.py:59
  77.3 3.0 %collective-permute-start.9 = (f32[8,128]{1,0:T(8,128)S(1)}, f32[8,128]{1,0:T(8,128)S(1)}, u32[]{:S(2)}, u32[]{:S(2)}) collective-permute-start(f32[8,128]{1,0:T(8,128)S(1)} %shard_map.217.refs_0_), channel_id=1, source_target_pairs={{0,3},{2,1},{1,2},{3,0},{4,7},{6,5},{5,6},{7,4},{8,11},{10,9},{9,1... | collective-permute-start | bytes 12296 | tf_op jit(solution)/shard_map/ppermute | solution.py:59
  80.4 3.7 %collective-permute-start.10 = (f16[64,8,640]{2,1,0:T(8,128)(2,1)S(1)}, f16[64,8,640]{2,1,0:T(8,128)(2,1)S(1)}, u32[]{:S(2)}, u32[]{:S(2)}) collective-permute-start(f16[64,8,640]{2,1,0:T(8,128)(2,1)S(1)} %all_to_all.16), channel_id=1, source_target_pairs={{0,2},{2,0},{1,3},{3,1},{4,6},{6,4},{5,7},{7,5},{8,10},{10,8},{9,1... | collective-permute-start | bytes 1966088 | tf_op jit(solution)/shard_map/ppermute | solution.py:59
  82.5 10.6 %collective-permute-start.11 = (bf16[296,512]{1,0:T(8,128)(2,1)S(1)}, bf16[296,512]{1,0:T(8,128)(2,1)S(1)}, u32[]{:S(2)}, u32[]{:S(2)}) collective-permute-start(bf16[296,512]{1,0:T(8,128)(2,1)S(1)} %get-tuple-element.67.refs_16_), channel_id=1, source_target_pairs={{0,1},{2,3},{1,0},{3,2},{4,5},{6,7},{5,4},{7,6},{8,9},{10,11},{9,8... | collective-permute-start | bytes 909320 | tf_op jit(solution)/shard_map/ppermute | solution.py:59
  83.7 9.4 %collective-permute-start.12 = (bf16[288,512]{1,0:T(8,128)(2,1)S(1)}, bf16[288,512]{1,0:T(8,128)(2,1)S(1)}, u32[]{:S(2)}, u32[]{:S(2)}) collective-permute-start(bf16[288,512]{1,0:T(8,128)(2,1)S(1)} %get-tuple-element.68.refs_17_), channel_id=1, source_target_pairs={{0,5},{2,7},{1,4},{3,6},{4,1},{6,3},{5,0},{7,2},{8,13},{10,15},{9,... | collective-permute-start | bytes 884744 | tf_op jit(solution)/shard_map/ppermute | solution.py:59
  93.1 2.9 %collective-permute-start.13 = (bf16[296,512]{1,0:T(8,128)(2,1)S(1)}, bf16[296,512]{1,0:T(8,128)(2,1)S(1)}, u32[]{:S(2)}, u32[]{:S(2)}) collective-permute-start(bf16[296,512]{1,0:T(8,128)(2,1)S(1)} %collective-permute-done.11.far0), channel_id=1, source_target_pairs={{0,2},{2,0},{1,3},{3,1},{4,6},{6,4},{5,7},{7,5},{8,10},{10,8},{9,1... | collective-permute-start | bytes 909320 | tf_op jit(solution)/shard_map/ppermute | solution.py:59
  94.4 1.6 %collective-permute-start.14 = (bf16[288,512]{1,0:T(8,128)(2,1)S(1)}, bf16[288,512]{1,0:T(8,128)(2,1)S(1)}, u32[]{:S(2)}, u32[]{:S(2)}) collective-permute-start(bf16[288,512]{1,0:T(8,128)(2,1)S(1)} %collective-permute-done.12.far1), channel_id=1, source_target_pairs={{0,2},{2,0},{1,3},{3,1},{4,6},{6,4},{5,7},{7,5},{8,10},{10,8},{9,1... | collective-permute-start | bytes 884744 | tf_op jit(solution)/shard_map/ppermute | solution.py:59
